TPU v7x, 32 devices: a whole 2x2x4 slice. The times are simulated.
32 devices in a mesh: by: 4 (over y, x), bz: 8 (over z, core).
Axes of the slice: x: 2, y: 2, z: 4, core: 2. Of those that a mesh axis runs over, the one named last changes fastest.
Arguments:
- camera_tiles: bfloat16 [128, 2, 256, 4, 128], P('bz', None, 'by'), may hold values from 0.05 to 5
- tile_block: int32 [128, 1], replicated, may hold values from 0 to 7; in each aligned block of 16 rows (0 to 15, 16 to 31, ...) at most 4 rows name the same one
- tile_offset: int32 [128], replicated, may hold values from 0 to 63
- band_index: int32 [256], P('by'), may hold values from 0 to 8
- interp: bfloat16 [256, 2], P('by'), may hold values from 0.19921875 to 1
- psf_taps: float32 [2, 3, 31], replicated, may hold values from 0.02 to 1
- background: float32 [2], replicated, may hold values from 0.05 to 0.5
Outputs:
- deskewed: float32 [2, 256, 512, 128], P(None, 'by', 'bz')
- estimate: float32 [2, 256, 512, 128], P(None, 'by', 'bz')
Inputs may be any that keep to these rules, and one draw needn't show every extreme that they name: `tile_block`: within the tiles of one device along bz (aligned blocks of 16 rows) no block index is named by more than 4 tiles, and in some such block one index is named by exactly 4.
All inputs are finite; a program needn't handle non-finite values.
Results may differ from a plain program's by a relative error of at most 0.0006.
Values may be sent and summed in bfloat16 or wider, within the bound.
No kernel may reach another device: no remote copies, remote signals or barrier semaphores. Data moves between devices by JAX's collectives and lax.ppermute only.
A program may use at most 128 MiB of HBM per device.

v0:
```python
import functools

import jax
import jax.numpy as jnp
from jax import lax
from jax.experimental import pallas as pl
from jax.experimental.pallas import tpu as pltpu
from jax.sharding import PartitionSpec as P


SHIFT = 8
ITERS = 2
Z_DEV = 64
HALO = 16
F32 = jnp.float32
BF16 = jnp.bfloat16


def in_vmem(count):
    return [pl.BlockSpec(memory_space=pltpu.VMEM) for _ in range(count)]


def place_kernel(channel_ref, own_ref, other_ref, out_ref, sems):
    rows = other_ref.shape[0]
    channel = channel_ref[0]
    copies = [
        pltpu.make_async_copy(own_ref.at[pl.ds(channel * rows, rows)], out_ref.at[channel], sems.at[0]),
        pltpu.make_async_copy(other_ref, out_ref.at[1 - channel], sems.at[1]),
    ]
    for copy in copies:
        copy.start()
    for copy in copies:
        copy.wait()


def place_halves(channel, both_rows, other):
    return pl.pallas_call(
        place_kernel,
        out_shape=jax.ShapeDtypeStruct((2,) + other.shape, other.dtype),
        in_specs=[pl.BlockSpec(memory_space=pltpu.SMEM)] + in_vmem(2),
        out_specs=pl.BlockSpec(memory_space=pl.ANY),
        scratch_shapes=[pltpu.SemaphoreType.DMA((2,))],
        compiler_params=pltpu.CompilerParams(vmem_limit_bytes=40 << 20),
        name="place_halves",
    )(channel[None], both_rows, other)


def gather_planes_kernel(starts_ref, arrived_ref, planes_ref, over_ref):
    halves, slots, planes, rows = arrived_ref.shape[:4]
    reach = over_ref.shape[0]
    height = planes_ref.shape[0]

    def clear(z, carry):
        planes_ref[z] = jnp.zeros(planes_ref.shape[1:], F32)
        return carry

    lax.fori_loop(0, height, clear, 0)

    def add(j, carry):
        start = starts_ref[j]

        @pl.when(start >= 0)
        def _():
            for s in range(planes):
                for h in range(halves):
                    here = pl.ds(h * rows, rows)
                    planes_ref[start + s, here, :] += arrived_ref[h, j, s].astype(F32)

        return carry

    lax.fori_loop(0, slots, add, 0)
    over_ref[...] = planes_ref[height - reach:]


def gather_planes(arrived, starts):
    halves, _, planes, rows, nx = arrived.shape
    height = Z_DEV + planes - 1
    return pl.pallas_call(
        gather_planes_kernel,
        out_shape=[
            jax.ShapeDtypeStruct((height, halves * rows, nx), F32),
            jax.ShapeDtypeStruct((SHIFT + planes, halves * rows, nx), F32),
        ],
        in_specs=[pl.BlockSpec(memory_space=pltpu.SMEM)] + in_vmem(1),
        out_specs=in_vmem(2),
        compiler_params=pltpu.CompilerParams(vmem_limit_bytes=40 << 20),
        name="gather_planes",
    )(starts, arrived)


def deskew_kernel(backdrop_ref, band_ref, near_ref, far_ref, planes_ref, before_ref,
                  out_ref, cast_ref, out_low_ref, out_high_ref, all_ref, *, pitch):
    ny, nz = out_ref.shape[:2]
    reach = before_ref.shape[0]
    ahead = SHIFT + 1
    backdrop = backdrop_ref[0]
    for z in range(ahead + nz):
        if z < ahead:
            plane = before_ref[z]
        elif z < reach:
            plane = before_ref[z] + planes_ref[z - ahead]
        else:
            plane = planes_ref[z - ahead]
        all_ref[pl.ds(z * pitch, ny), :] = plane

    def row(y, carry):
        first = (ahead - band_ref[y]) * pitch + y
        value = near_ref[y] * all_ref[pl.ds(first, nz, stride=pitch), :]
        value = value + far_ref[y] * all_ref[pl.ds(first - pitch, nz, stride=pitch), :]
        out_ref[y] = value
        cast = (value + backdrop).astype(BF16)
        cast_ref[y] = cast
        out_low_ref[y] = cast[:HALO]
        out_high_ref[y] = cast[nz - HALO:]
        return carry

    lax.fori_loop(0, ny, row, 0, unroll=4)


def deskew(backdrop, band, near, far, planes, before):
    ny, nx = planes.shape[1:]
    pitch = ny + 8
    smem = [pl.BlockSpec(memory_space=pltpu.SMEM)] * 4
    return pl.pallas_call(
        functools.partial(deskew_kernel, pitch=pitch),
        out_shape=[
            jax.ShapeDtypeStruct((ny, Z_DEV, nx), F32),
            jax.ShapeDtypeStruct((ny, Z_DEV, nx), BF16),
            jax.ShapeDtypeStruct((ny, HALO, nx), BF16),
            jax.ShapeDtypeStruct((ny, HALO, nx), BF16),
        ],
        in_specs=smem + in_vmem(2),
        out_specs=in_vmem(4),
        scratch_shapes=[pltpu.VMEM(((Z_DEV + SHIFT + 1) * pitch, nx), F32)],
        compiler_params=pltpu.CompilerParams(vmem_limit_bytes=40 << 20),
        name="deskew",
    )(backdrop, band, near, far, planes, before)


def blur_kernel(backdrop_ref, own_ref, low_ref, high_ref, side_ref, side_low_ref, side_high_ref,
                mx_ref, mz_ref, my_ref, point_ref, *rest, quotient, first, ny, nz, nside):
    if quotient:
        cast_ref, out_low_ref, out_high_ref, mid_ref, blur_ref = rest
    else:
        full_ref, cast_ref, out_low_ref, out_high_ref, mid_ref, blur_ref = rest
    total = ny + nside
    mx, mz, my = mx_ref[...], mz_ref[...], my_ref[...]
    lanes = mx.shape[1]
    pitch = nz + 8
    width = nz + 2 * HALO
    group = 16
    ahead = 8

    def planes(load, base, count):
        def body(g, carry):
            pieces = []
            for k in range(group):
                pieces += list(load(g * group + k))
            stack = jnp.concatenate(pieces, axis=0)
            alongx = jnp.dot(jnp.concatenate([stack, stack], axis=1), mx, preferred_element_type=F32)
            alongx = alongx.astype(BF16)
            for k in range(0, group, 2):
                pair = jnp.concatenate(
                    [alongx[k * width:(k + 1) * width], alongx[(k + 1) * width:(k + 2) * width]], axis=1
                )
                both = jnp.dot(mz, jnp.concatenate([pair, pair], axis=0), preferred_element_type=F32)
                row = pl.multiple_of((base + g * group + k) * pitch, 8)
                mid_ref[pl.ds(row, nz), :] = both[:, :lanes]
                mid_ref[pl.ds(row + pitch, nz), :] = both[:, lanes:]
            return carry

        lax.fori_loop(0, count // group, body, 0)

    planes(lambda y: (low_ref[y], own_ref[y], high_ref[y]), 0, ny)
    planes(lambda y: (side_low_ref[y], side_ref[y], side_high_ref[y]), ny, nside)

    def split(z):
        column = mid_ref[pl.ds(z, total, stride=pitch), :]
        head = column.astype(BF16)
        tail = (column - head.astype(F32)).astype(BF16)
        return jnp.concatenate([head, tail, head], axis=0)

    def columns(g, carry):
        for k in range(ahead):
            z = (g * ahead + k) * 2
            both = jnp.dot(my, jnp.concatenate([split(z), split(z + 1)], axis=1), preferred_element_type=F32)
            blur_ref[pl.ds(z, ny, stride=pitch), :] = both[:, :lanes]
            blur_ref[pl.ds(z + 1, ny, stride=pitch), :] = both[:, lanes:]
        return carry

    lax.fori_loop(0, nz // (2 * ahead), columns, 0)
    backdrop = backdrop_ref[0]

    def finish(y, carry):
        row = pl.multiple_of(y * pitch, 8)
        blurred = blur_ref[pl.ds(row, nz), :]
        if quotient:
            value = point_ref[y] / (blurred + backdrop)
        else:
            value = (point_ref[y] + backdrop if first else point_ref[y]) * blurred
            full_ref[y] = value
        cast = value.astype(BF16)
        cast_ref[y] = cast
        out_low_ref[y] = cast[:HALO]
        out_high_ref[y] = cast[nz - HALO:]
        return carry

    lax.fori_loop(0, ny, finish, 0, unroll=8)


def blur_block(quotient, first, backdrop, field, halos, matrices, point):
    ny, nz, nx = field[0].shape
    nside = halos[2].shape[0]
    outs = [
        jax.ShapeDtypeStruct((ny, nz, nx), BF16),
        jax.ShapeDtypeStruct((ny, HALO, nx), BF16),
        jax.ShapeDtypeStruct((ny, HALO, nx), BF16),
    ]
    if not quotient:
        outs = [jax.ShapeDtypeStruct((ny, nz, nx), F32)] + outs
    return pl.pallas_call(
        functools.partial(blur_kernel, quotient=quotient, first=first, ny=ny, nz=nz, nside=nside),
        out_shape=outs,
        in_specs=[pl.BlockSpec(memory_space=pltpu.SMEM)] + in_vmem(10),
        out_specs=in_vmem(len(outs)),
        scratch_shapes=[
            pltpu.VMEM(((ny + nside) * (nz + 8), nx), F32),
            pltpu.VMEM((ny * (nz + 8), nx), F32),
        ],
        compiler_params=pltpu.CompilerParams(vmem_limit_bytes=56 << 20),
        cost_estimate=pl.CostEstimate(flops=20_000_000_000, transcendentals=0, bytes_accessed=16_000_000),
        name="blur_quotient" if quotient else "blur_estimate",
    )(backdrop, field[0], halos[0], halos[1], halos[2], halos[3], halos[4], *matrices, point)


def halo_exchange(field):
    block, face_low, face_high = field
    rows = block.shape[0]
    blocks = lax.axis_size("bz")
    wide = lax.axis_size("by")
    halves = wide // 2
    up = [(i, i + 1) for i in range(blocks - 1)]
    down = [(i + 1, i) for i in range(blocks - 1)]
    place = lax.axis_index("by") // 2

    if halves == 2:
        sides = [(jnp.where(place == 0, rows - HALO, 0), [(i, i ^ 2) for i in range(wide)])]
    else:
        sides = [
            (rows - HALO, [(i, i + 2) for i in range(wide - 2)]),
            (0, [(i + 2, i) for i in range(wide - 2)]),
        ]

    def both(pairs, step):
        return [
            (a * blocks + z, b * blocks + z + step)
            for a, b in pairs
            for z in range(blocks)
            if 0 <= z + step < blocks
        ]

    side, side_low, side_high = [], [], []
    for start, pairs in sides:
        cut = lambda x: lax.dynamic_slice_in_dim(x, start, HALO, 0)
        side.append(lax.ppermute(cut(block), "by", pairs))
        side_low.append(lax.ppermute(cut(face_high), ("by", "bz"), both(pairs, 1)))
        side_high.append(lax.ppermute(cut(face_low), ("by", "bz"), both(pairs, -1)))
    low = lax.ppermute(face_high, "bz", up)
    high = lax.ppermute(face_low, "bz", down)
    join = lambda parts: parts[0] if len(parts) == 1 else jnp.concatenate(parts, axis=0)
    return low, high, join(side), join(side_low), join(side_high)


def head_tail(matrix):
    head = lax.reduce_precision(matrix, 8, 7)
    return head.astype(BF16), (matrix - head).astype(BF16)


def band(taps, out_place, in_place):
    count = taps.shape[0]
    offset = in_place[None, :] - out_place[:, None] + count // 2
    matches = (offset[:, :, None] == jnp.arange(count)[None, None, :]).astype(F32)
    return jnp.einsum("ijw,cw->cij", matches, jnp.stack([taps, taps[::-1]]), precision=lax.Precision.HIGHEST)


def band_matrices(taps, ny, nz, nx):
    halves = lax.axis_size("by") // 2
    place = lax.axis_index("by") // 2
    before, after = jnp.arange(HALO) - HALO, jnp.arange(HALO) + ny
    if halves == 2:
        sides = [jnp.where(place == 0, after, before)]
    else:
        sides = [before, after]
    along = jnp.arange(nx)
    xh, xl = head_tail(band(taps[2], along, along)[::-1])
    zh, zl = head_tail(band(taps[1], jnp.arange(nz), jnp.arange(nz + 2 * HALO) - HALO))
    yh, yl = head_tail(band(taps[0], jnp.arange(ny), jnp.concatenate([jnp.arange(ny)] + sides)))
    mx = jnp.concatenate([xh, xl], axis=1)
    mz = jnp.concatenate([zh, zl], axis=2)
    my = jnp.concatenate([yh, yh, yl], axis=2)
    return (mx[0], mz[0], my[0]), (mx[1], mz[1], my[1])


def swap_pair(x):
    return lax.ppermute(x, "by", [(i, i ^ 1) for i in range(lax.axis_size("by"))])


def route_tiles(camera_tiles, tile_block, tile_offset):
    tile_count, channels = camera_tiles.shape[:2]
    blocks = lax.axis_size("bz")
    wide = lax.axis_size("by")
    capacity = max(2, 2 * tile_count // blocks)
    own_index = lax.axis_index("bz")
    targets = tile_block[:, 0].reshape(blocks, tile_count)
    offsets = tile_offset.reshape(blocks, tile_count)
    matches = (targets[:, :, None] == jnp.arange(blocks)[None, None, :]).astype(jnp.int32)
    places = jnp.sum((jnp.cumsum(matches, axis=1) - matches) * matches, axis=2)
    own_slot = lax.dynamic_index_in_dim(targets * capacity + places, own_index, 0, keepdims=False)
    slots = jnp.arange(blocks * capacity)
    tile_of = jnp.sum(
        jnp.where(own_slot[None, :] == slots[:, None], jnp.arange(tile_count)[None, :], 0), axis=1
    )
    rows = jnp.concatenate([tile_of * channels + c for c in range(channels)])
    planar = jnp.swapaxes(camera_tiles, 2, 3)
    outgoing = jnp.take(planar.reshape((tile_count * channels,) + planar.shape[2:]), rows, axis=0, mode="clip")
    outgoing = outgoing.reshape((channels * blocks, capacity) + planar.shape[2:])
    groups = [
        [(2 * j + c) * blocks + z for c in range(2) for z in range(blocks)] for j in range(wide // 2)
    ]
    arrived = lax.all_to_all(
        outgoing, ("by", "bz"), split_axis=0, concat_axis=0, axis_index_groups=groups, tiled=True
    )
    chosen = (targets[:, :, None] == own_index) & (
        places[:, :, None] == jnp.arange(capacity)[None, None, :]
    )
    starts = jnp.sum(jnp.where(chosen, offsets[:, :, None] + 1, 0), axis=1) - 1
    return (
        arrived.reshape((channels, blocks * capacity) + planar.shape[2:]),
        starts.reshape(blocks * capacity),
    )


def pair_stack(first_is_own, own, other):
    return jnp.stack([jnp.where(first_is_own, own, other), jnp.where(first_is_own, other, own)])


def shards(camera_tiles, tile_block, tile_offset, band_index, interp, psf_taps, background):
    channel = lax.axis_index("by") % 2
    first = channel == 0
    rows = camera_tiles.shape[2]
    table = jnp.concatenate([band_index[:, None].astype(F32), interp.astype(F32)], axis=1)
    table = pair_stack(first, table, swap_pair(table))

    taps = lax.dynamic_index_in_dim(psf_taps, channel, 0, keepdims=False)
    kernels = taps / jnp.sum(taps, axis=1, keepdims=True)
    nx = camera_tiles.shape[4]
    forward, backward = band_matrices(kernels, 2 * rows, Z_DEV, nx)
    backdrop = lax.dynamic_slice_in_dim(background, channel, 1, 0)

    arrived, starts = route_tiles(camera_tiles, tile_block, tile_offset)
    planes, over = gather_planes(arrived, starts)
    blocks = lax.axis_size("bz")
    before = lax.ppermute(over, "bz", [(i, i + 1) for i in range(blocks - 1)])
    table = table.reshape(2 * rows, 3)
    deskewed, *field = deskew(backdrop, table[:, 0].astype(jnp.int32), table[:, 1], table[:, 2], planes, before)

    half = lambda x, start: lax.dynamic_slice_in_dim(x, start, rows, 0)
    other_start = (1 - channel) * rows
    deskewed_other = swap_pair(half(deskewed, other_start))

    estimate = deskewed
    for iteration in range(ITERS):
        halos = halo_exchange(field)
        field = blur_block(True, False, backdrop, field, halos, forward, deskewed)
        halos = halo_exchange(field)
        estimate, *field = blur_block(
            False, iteration == 0, backdrop, field, halos, backward, estimate
        )
    deskewed_out = place_halves(channel, deskewed, deskewed_other)

    theirs = half(estimate, other_start)
    scale = jnp.exp2(jnp.floor(jnp.log2(jnp.max(theirs))) - 13.0)
    got = swap_pair((theirs / scale).astype(jnp.float16)).astype(F32) * swap_pair(scale)
    return deskewed_out, place_halves(channel, estimate, got)


def solution(mesh):
    placed = (P("bz", None, "by", None, None), P(), P(), P("by"), P("by", None), P(), P())
    return jax.shard_map(
        shards,
        mesh=mesh,
        in_specs=placed,
        out_specs=(P(None, "by", "bz", None), P(None, "by", "bz", None)),
        check_vma=False,
    )
```

profile of v0, /device:TPU:1, one launch (start us, length us, event | category | flops | bytes accessed | tf_op | source)
XLA Modules:
  0.0 335.6 jit_solution(16099168991354373303)
XLA Ops:
  1.2 1.4 reduce.6
  3.6 6.4 %gather_fusion = bf16[64,4,64,128]{3,1,2,0:T(4,128)(2,1)} fusion(bf16[32,4,64,128]{3,1,2,0:T(4,128)(2,1)S(1)} %bitcast.53, s32[1024]{0:T(1024)S(1)} %pad_clamp_fusion), kind=kCustom, calls=%fused_computation | custom fusion | bytes 8388864 | tf_op jit(solution)/shard_map/jit(_take)/gather | solution.py:325
  9.9 5.4 %copy.60 = bf16[64,4,64,128]{3,2,1,0:T(8,128)(2,1)} copy(bf16[64,4,64,128]{3,1,2,0:T(4,128)(2,1)} %gather_fusion) | data formatting | bytes 8388608 | tf_op jit(solution)/shard_map/jit(_take)/gather | solution.py:325
  15.3 7.5 %all-to-all-start = ((bf16[16,4,4,64,128]{4,3,2,1,0:T(8,128)(2,1)}), bf16[16,4,4,64,128]{4,3,2,1,0:T(8,128)(2,1)}, u32[]{:S(2)}, u32[]{:S(2)}) async-start(bf16[16,4,4,64,128]{4,3,2,1,0:T(8,128)(2,1)} %bitcast.54), calls=%async_computation | async-start | bytes 8388608 | tf_op jit(solution)/shard_map/all_to_all | solution.py:330
  22.9 1.4 collective-permute-start
  28.7 82.5 %all-to-all-done = bf16[16,4,4,64,128]{4,3,2,1,0:T(8,128)(2,1)} async-done(((bf16[16,4,4,64,128]{4,3,2,1,0:T(8,128)(2,1)}), bf16[16,4,4,64,128]{4,3,2,1,0:T(8,128)(2,1)}, u32[]{:S(2)}, u32[]{:S(2)}) %all-to-all-start) | async-done | bytes 4194336 | tf_op jit(solution)/shard_map/all_to_all | solution.py:330
  111.2 3.4 %gather_planes.1 = (f32[67,128,128]{2,1,0:T(8,128)S(1)}, f32[12,128,128]{2,1,0:T(8,128)S(1)}) custom-call(s32[32]{0:T(128)S(1)} %sub.92.starts_ref, bf16[2,32,4,64,128]{4,3,2,1,0:T(8,128)(2,1)} %bitcast.10.arrived_ref), custom_call_target="tpu_custom_call" | custom-call | tf_op jit(solution)/shard_map/gather_planes/pallas_call | solution.py:78
  114.6 2.0 copy-done.5
  116.7 7.2 %collective-permute-start.1 = (f32[12,128,128]{2,1,0:T(8,128)S(1)}, f32[12,128,128]{2,1,0:T(8,128)S(1)}, u32[]{:S(2)}, u32[]{:S(2)}) collective-permute-start(f32[12,128,128]{2,1,0:T(8,128)S(1)} %get-tuple-element.20), channel_id=1, source_target_pairs={{0,1},{1,2},{2,3},{3,4},{4,5},{5,6},{6,7},{8,9},{9,10},{10,11},{11... | collective-permute-start | bytes 2359304 | tf_op jit(solution)/shard_map/ppermute | solution.py:363
  124.7 8.1 %collective-permute-done.1.before_ref = f32[12,128,128]{2,1,0:T(8,128)S(1)} collective-permute-done((f32[12,128,128]{2,1,0:T(8,128)S(1)}, f32[12,128,128]{2,1,0:T(8,128)S(1)}, u32[]{:S(2)}, u32[]{:S(2)}) %collective-permute-start.1) | collective-permute-done | bytes 786464 | tf_op jit(solution)/shard_map/ppermute | solution.py:363
  132.8 2.2 copy-done.6
  135.0 3.9 %deskew.1 = (f32[128,64,128]{2,1,0:T(8,128)S(1)}, bf16[128,64,128]{2,1,0:T(8,128)(2,1)S(1)}, bf16[128,16,128]{2,1,0:T(8,128)(2,1)S(1)}, bf16[128,16,128]{2,1,0:T(8,128)(2,1)S(1)}) custom-call(f32[1]{0:T(128)} %dynamic_slice.53.backdrop_ref, s32[128]{0:T(128)S(1)} %get-tuple-element.60.band_ref, f32[128]{0:T(128)S(1)} %get-tuple-element.59.near_ref, ...), custom_call_target="tpu_custom_call" | custom-call | tf_op jit(solution)/shard_map/deskew/pallas_call | solution.py:124
  138.9 2.0 copy-done.3
  141.0 4.4 %collective-permute-start.3 = (bf16[128,16,128]{2,1,0:T(8,128)(2,1)S(1)}, bf16[128,16,128]{2,1,0:T(8,128)(2,1)S(1)}, u32[]{:S(2)}, u32[]{:S(2)}) collective-permute-start(bf16[128,16,128]{2,1,0:T(8,128)(2,1)S(1)} %get-tuple-element.23), channel_id=1, source_target_pairs={{0,1},{1,2},{2,3},{3,4},{4,5},{5,6},{6,7},{8,9},{9,10},{10,11},{11... | collective-permute-start | bytes 1572872 | tf_op jit(solution)/shard_map/ppermute | solution.py:268
  145.3 1.9 collective-permute-start.4
  148.0 1.3 collective-permute-start.5
  149.3 3.9 %collective-permute-start.6 = (bf16[16,16,128]{2,1,0:T(8,128)(2,1)S(1)}, bf16[16,16,128]{2,1,0:T(8,128)(2,1)S(1)}, u32[]{:S(2)}, u32[]{:S(2)}) collective-permute-start(bf16[16,16,128]{2,1,0:T(8,128)(2,1)S(1)} %constant_dynamic-slice_fusion.11), channel_id=1, source_target_pairs={{0,17},{1,18},{2,19},{3,20},{4,21},{5,22},{6,23},{8,25},{9,26},{10... | collective-permute-start | bytes 196616 | tf_op jit(solution)/shard_map/ppermute | solution.py:266
  153.2 1.9 collective-permute-start.7
  155.8 3.8 %collective-permute-done.7.side_high_ref = bf16[16,16,128]{2,1,0:T(8,128)(2,1)S(1)} collective-permute-done((bf16[16,16,128]{2,1,0:T(8,128)(2,1)S(1)}, bf16[16,16,128]{2,1,0:T(8,128)(2,1)S(1)}, u32[]{:S(2)}, u32[]{:S(2)}) %collective-permute-start.7) | collective-permute-done | bytes 65568 | tf_op jit(solution)/shard_map/ppermute | solution.py:267
  160.7 14.8 %blur_quotient.2 = (bf16[128,64,128]{2,1,0:T(8,128)(2,1)}, bf16[128,16,128]{2,1,0:T(8,128)(2,1)}, bf16[128,16,128]{2,1,0:T(8,128)(2,1)}) custom-call(f32[1]{0:T(128)} %dynamic_slice.53.backdrop_ref, bf16[128,64,128]{2,1,0:T(8,128)(2,1)} %copy-done.7, bf16[128,16,128]{2,1,0:T(8,128)(2,1)} %copy-done.11, bf16[128,16,128]{2,1,0:T(8,128)(2,1)} %copy-done.12, ...), custom_call_target="tpu_custom_call" | custom-call | flops 20000000000 | bytes 16000000 | tf_op jit(solution)/shard_map/blur_quotient/pallas_call | solution.py:221
  175.5 1.9 collective-permute-start.8
  177.5 2.4 collective-permute-start.9
  180.9 1.3 collective-permute-start.10
  183.9 3.3 collective-permute-start.11
  187.2 2.2 collective-permute-start.12
  189.5 4.2 %collective-permute-done.12.side_high_ref = bf16[16,16,128]{2,1,0:T(8,128)(2,1)S(1)} collective-permute-done((bf16[16,16,128]{2,1,0:T(8,128)(2,1)S(1)}, bf16[16,16,128]{2,1,0:T(8,128)(2,1)S(1)}, u32[]{:S(2)}, u32[]{:S(2)}) %collective-permute-start.12) | collective-permute-done | bytes 65568 | tf_op jit(solution)/shard_map/ppermute | solution.py:267
  194.8 16.0 %blur_estimate.2 = (f32[128,64,128]{2,1,0:T(8,128)}, bf16[128,64,128]{2,1,0:T(8,128)(2,1)}, bf16[128,16,128]{2,1,0:T(8,128)(2,1)}, bf16[128,16,128]{2,1,0:T(8,128)(2,1)}) custom-call(f32[1]{0:T(128)} %dynamic_slice.53.backdrop_ref, bf16[128,64,128]{2,1,0:T(8,128)(2,1)} %get-tuple-element.25.own_ref, bf16[128,16,128]{2,1,0:T(8,128)(2,1)} %copy-done.13, ...), custom_call_target="tpu_custom_call" | custom-call | flops 20000000000 | bytes 16000000 | tf_op jit(solution)/shard_map/blur_estimate/pallas_call | solution.py:221
  210.8 1.9 collective-permute-start.13
  212.7 2.6 collective-permute-start.14
  216.3 1.3 collective-permute-start.15
  219.3 3.3 collective-permute-start.16
  222.7 2.2 collective-permute-start.17
  225.0 4.2 %collective-permute-done.17.side_high_ref = bf16[16,16,128]{2,1,0:T(8,128)(2,1)S(1)} collective-permute-done((bf16[16,16,128]{2,1,0:T(8,128)(2,1)S(1)}, bf16[16,16,128]{2,1,0:T(8,128)(2,1)S(1)}, u32[]{:S(2)}, u32[]{:S(2)}) %collective-permute-start.17) | collective-permute-done | bytes 65568 | tf_op jit(solution)/shard_map/ppermute | solution.py:267
  230.9 14.8 %blur_quotient.3 = (bf16[128,64,128]{2,1,0:T(8,128)(2,1)}, bf16[128,16,128]{2,1,0:T(8,128)(2,1)}, bf16[128,16,128]{2,1,0:T(8,128)(2,1)}) custom-call(f32[1]{0:T(128)} %dynamic_slice.53.backdrop_ref, bf16[128,64,128]{2,1,0:T(8,128)(2,1)} %get-tuple-element.28.own_ref, bf16[128,16,128]{2,1,0:T(8,128)(2,1)} %copy-done.14, bf16[128,16,128]{2,1,0:T(8,128)(2,1)} %copy-done.16, ...), custom_call_target="tpu_custom_call" | custom-call | flops 20000000000 | bytes 16000000 | tf_op jit(solution)/shard_map/blur_quotient/pallas_call | solution.py:221
  245.7 1.9 collective-permute-start.18
  247.6 2.4 collective-permute-start.19
  251.0 1.3 collective-permute-start.20
  253.2 3.3 collective-permute-start.21
  257.4 2.2 collective-permute-start.22
  259.6 3.2 constant_dynamic-slice_fusion.13
  265.0 15.9 %blur_estimate.3 = (f32[128,64,128]{2,1,0:T(8,128)}, bf16[128,64,128]{2,1,0:T(8,128)(2,1)}, bf16[128,16,128]{2,1,0:T(8,128)(2,1)}, bf16[128,16,128]{2,1,0:T(8,128)(2,1)}) custom-call(f32[1]{0:T(128)} %dynamic_slice.53.backdrop_ref, bf16[128,64,128]{2,1,0:T(8,128)(2,1)} %get-tuple-element.31.own_ref, bf16[128,16,128]{2,1,0:T(8,128)(2,1)} %copy-done.9, ...), custom_call_target="tpu_custom_call" | custom-call | flops 20000000000 | bytes 16000000 | tf_op jit(solution)/shard_map/blur_estimate/pallas_call | solution.py:221
  280.9 2.7 dynamic-slice_reduce_fusion
  284.4 1.9 divide_convert_fusion
  287.4 23.2 %collective-permute-done.2.other_ref = f32[64,64,128]{2,1,0:T(8,128)S(1)} collective-permute-done((f32[64,64,128]{2,1,0:T(8,128)}, f32[64,64,128]{2,1,0:T(8,128)S(1)}, u32[]{:S(2)}, u32[]{:S(2)}) %collective-permute-start.2) | collective-permute-done | bytes 2097184 | tf_op jit(solution)/shard_map/ppermute | solution.py:305
  310.6 2.2 copy-done.4
  312.8 2.1 place_halves.2
  315.0 15.9 %collective-permute-start.24 = (f32[]{:T(128)}, f32[]{:T(128)}, u32[]{:S(2)}, u32[]{:S(2)}) collective-permute-start(f32[]{:T(128)} %exp2.7), channel_id=1, source_target_pairs={{0,8},{8,0},{16,24},{24,16},{1,9},{9,1},{17,25},{25,17},{2,10},{10... | collective-permute-start | bytes 20 | tf_op jit(solution)/shard_map/ppermute | solution.py:305
  332.6 2.2 place_halves.3
  (150 shorter events, 25.9 us)
Async XLA Ops:
  0.6 2.9 copy-start
  15.3 7.5 %copy-start.29 = (bf16[64,2]{0,1:T(2,128)(2,1)S(1)}, bf16[64,2]{0,1:T(2,128)(2,1)}, u32[]{:S(2)}) copy-start(bf16[64,2]{0,1:T(2,128)(2,1)} %param.11) | copy-start | bytes 772
  15.3 7.5 %copy-start.30 = (s32[64]{0:T(128)S(1)}, s32[64]{0:T(128)}, u32[]{:S(2)}) copy-start(s32[64]{0:T(128)} %param.10) | copy-start | bytes 772
  15.3 9.0 %copy-start.31 = (s32[128]{0:T(128)S(1)}, s32[128]{0:T(128)}, u32[]{:S(2)}) copy-start(s32[128]{0:T(128)} %param.9) | copy-start | bytes 1540
  15.3 9.4 %copy-start.8 = (f32[2,3,31]{2,0,1:T(2,128)S(1)}, f32[2,3,31]{2,0,1:T(2,128)}, u32[]{:S(2)}) copy-start(f32[2,3,31]{2,0,1:T(2,128)} %param.12) | copy-start | bytes 2236
  15.3 95.8 %all-to-all-start = ((bf16[16,4,4,64,128]{4,3,2,1,0:T(8,128)(2,1)}), bf16[16,4,4,64,128]{4,3,2,1,0:T(8,128)(2,1)}, u32[]{:S(2)}, u32[]{:S(2)}) async-start(bf16[16,4,4,64,128]{4,3,2,1,0:T(8,128)(2,1)} %bitcast.54), calls=%async_computation | async-start | bytes 8388608 | tf_op jit(solution)/shard_map/all_to_all | solution.py:330
  22.9 101.7 %collective-permute-start = (f32[64,3]{0,1:T(4,128)S(1)}, f32[64,3]{0,1:T(4,128)S(1)}, u32[]{:S(2)}, u32[]{:S(2)}) collective-permute-start(f32[64,3]{0,1:T(4,128)S(1)} %pad_maximum_fusion.4), channel_id=1, source_target_pairs={{0,8},{8,0},{16,24},{24,16},{1,9},{9,1},{17,25},{25,17},{2,10},{10... | collective-permute-start | bytes 2312 | tf_op jit(solution)/shard_map/ppermute | solution.py:305
  111.2 12.8 %copy-start.32 = (f32[2]{0:T(128)S(1)}, f32[2]{0:T(128)}, u32[]{:S(2)}) copy-start(f32[2]{0:T(128)} %param.13) | copy-start | bytes 28
  114.6 2.0 copy-start.5
  116.7 16.1 %collective-permute-start.1 = (f32[12,128,128]{2,1,0:T(8,128)S(1)}, f32[12,128,128]{2,1,0:T(8,128)S(1)}, u32[]{:S(2)}, u32[]{:S(2)}) collective-permute-start(f32[12,128,128]{2,1,0:T(8,128)S(1)} %get-tuple-element.20), channel_id=1, source_target_pairs={{0,1},{1,2},{2,3},{3,4},{4,5},{5,6},{6,7},{8,9},{9,10},{10,11},{11... | collective-permute-start | bytes 2359304 | tf_op jit(solution)/shard_map/ppermute | solution.py:363
  132.8 2.2 copy-start.6
  138.9 2.0 copy-start.3
  141.0 18.7 %copy-start.7 = (bf16[128,64,128]{2,1,0:T(8,128)(2,1)}, bf16[128,64,128]{2,1,0:T(8,128)(2,1)S(1)}, u32[]{:S(2)}) copy-start(bf16[128,64,128]{2,1,0:T(8,128)(2,1)S(1)} %get-tuple-element.22.own_ref) | copy-start | bytes 6291460
  141.0 18.7 %collective-permute-start.3 = (bf16[128,16,128]{2,1,0:T(8,128)(2,1)S(1)}, bf16[128,16,128]{2,1,0:T(8,128)(2,1)S(1)}, u32[]{:S(2)}, u32[]{:S(2)}) collective-permute-start(bf16[128,16,128]{2,1,0:T(8,128)(2,1)S(1)} %get-tuple-element.23), channel_id=1, source_target_pairs={{0,1},{1,2},{2,3},{3,4},{4,5},{5,6},{6,7},{8,9},{9,10},{10,11},{11... | collective-permute-start | bytes 1572872 | tf_op jit(solution)/shard_map/ppermute | solution.py:268
  145.3 14.3 %collective-permute-start.4 = (bf16[128,16,128]{2,1,0:T(8,128)(2,1)S(1)}, bf16[128,16,128]{2,1,0:T(8,128)(2,1)S(1)}, u32[]{:S(2)}, u32[]{:S(2)}) collective-permute-start(bf16[128,16,128]{2,1,0:T(8,128)(2,1)S(1)} %get-tuple-element.24), channel_id=1, source_target_pairs={{1,0},{2,1},{3,2},{4,3},{5,4},{6,5},{7,6},{9,8},{10,9},{11,10},{12... | collective-permute-start | bytes 1572872 | tf_op jit(solution)/shard_map/ppermute | solution.py:269
  148.0 11.7 %collective-permute-start.5 = (bf16[16,64,128]{2,1,0:T(8,128)(2,1)S(1)}, bf16[16,64,128]{2,1,0:T(8,128)(2,1)S(1)}, u32[]{:S(2)}, u32[]{:S(2)}) collective-permute-start(bf16[16,64,128]{2,1,0:T(8,128)(2,1)S(1)} %constant_dynamic-slice_fusion.12), channel_id=1, source_target_pairs={{0,16},{8,24},{16,0},{24,8},{1,17},{9,25},{17,1},{25,9},{2,18},{10... | collective-permute-start | bytes 786440 | tf_op jit(solution)/shard_map/ppermute | solution.py:265
  149.3 6.5 %collective-permute-start.6 = (bf16[16,16,128]{2,1,0:T(8,128)(2,1)S(1)}, bf16[16,16,128]{2,1,0:T(8,128)(2,1)S(1)}, u32[]{:S(2)}, u32[]{:S(2)}) collective-permute-start(bf16[16,16,128]{2,1,0:T(8,128)(2,1)S(1)} %constant_dynamic-slice_fusion.11), channel_id=1, source_target_pairs={{0,17},{1,18},{2,19},{3,20},{4,21},{5,22},{6,23},{8,25},{9,26},{10... | collective-permute-start | bytes 196616 | tf_op jit(solution)/shard_map/ppermute | solution.py:266
  153.2 6.5 %collective-permute-start.7 = (bf16[16,16,128]{2,1,0:T(8,128)(2,1)S(1)}, bf16[16,16,128]{2,1,0:T(8,128)(2,1)S(1)}, u32[]{:S(2)}, u32[]{:S(2)}) collective-permute-start(bf16[16,16,128]{2,1,0:T(8,128)(2,1)S(1)} %constant_dynamic-slice_fusion.10), channel_id=1, source_target_pairs={{1,16},{2,17},{3,18},{4,19},{5,20},{6,21},{7,22},{9,24},{10,25},{1... | collective-permute-start | bytes 196616 | tf_op jit(solution)/shard_map/ppermute | solution.py:267
  155.8 3.9 %copy-start.23 = (bf16[16,16,128]{2,1,0:T(8,128)(2,1)}, bf16[16,16,128]{2,1,0:T(8,128)(2,1)S(1)}, u32[]{:S(2)}) copy-start(bf16[16,16,128]{2,1,0:T(8,128)(2,1)S(1)} %collective-permute-done.6.side_low_ref) | copy-start | bytes 196612
  159.7 0.9 copy-start.11
  159.7 1.1 copy-start.12
  175.5 18.2 %collective-permute-start.8 = (bf16[128,16,128]{2,1,0:T(8,128)(2,1)}, bf16[128,16,128]{2,1,0:T(8,128)(2,1)S(1)}, u32[]{:S(2)}, u32[]{:S(2)}) collective-permute-start(bf16[128,16,128]{2,1,0:T(8,128)(2,1)} %get-tuple-element.26), channel_id=1, source_target_pairs={{0,1},{1,2},{2,3},{3,4},{4,5},{5,6},{6,7},{8,9},{9,10},{10,11},{11... | collective-permute-start | bytes 1572872 | tf_op jit(solution)/shard_map/ppermute | solution.py:268
  177.5 16.3 %collective-permute-start.9 = (bf16[128,16,128]{2,1,0:T(8,128)(2,1)}, bf16[128,16,128]{2,1,0:T(8,128)(2,1)S(1)}, u32[]{:S(2)}, u32[]{:S(2)}) collective-permute-start(bf16[128,16,128]{2,1,0:T(8,128)(2,1)} %get-tuple-element.27), channel_id=1, source_target_pairs={{1,0},{2,1},{3,2},{4,3},{5,4},{6,5},{7,6},{9,8},{10,9},{11,10},{12... | collective-permute-start | bytes 1572872 | tf_op jit(solution)/shard_map/ppermute | solution.py:269
  180.9 12.8 %collective-permute-start.10 = (bf16[16,64,128]{2,1,0:T(8,128)(2,1)S(1)}, bf16[16,64,128]{2,1,0:T(8,128)(2,1)S(1)}, u32[]{:S(2)}, u32[]{:S(2)}) collective-permute-start(bf16[16,64,128]{2,1,0:T(8,128)(2,1)S(1)} %constant_dynamic-slice_fusion.8), channel_id=1, source_target_pairs={{0,16},{8,24},{16,0},{24,8},{1,17},{9,25},{17,1},{25,9},{2,18},{10... | collective-permute-start | bytes 786440 | tf_op jit(solution)/shard_map/ppermute | solution.py:265
  183.9 5.7 %collective-permute-start.11 = (bf16[16,16,128]{2,1,0:T(8,128)(2,1)S(1)}, bf16[16,16,128]{2,1,0:T(8,128)(2,1)S(1)}, u32[]{:S(2)}, u32[]{:S(2)}) collective-permute-start(bf16[16,16,128]{2,1,0:T(8,128)(2,1)S(1)} %constant_dynamic-slice_fusion.7), channel_id=1, source_target_pairs={{0,17},{1,18},{2,19},{3,20},{4,21},{5,22},{6,23},{8,25},{9,26},{10... | collective-permute-start | bytes 196616 | tf_op jit(solution)/shard_map/ppermute | solution.py:266
  187.2 6.5 %collective-permute-start.12 = (bf16[16,16,128]{2,1,0:T(8,128)(2,1)S(1)}, bf16[16,16,128]{2,1,0:T(8,128)(2,1)S(1)}, u32[]{:S(2)}, u32[]{:S(2)}) collective-permute-start(bf16[16,16,128]{2,1,0:T(8,128)(2,1)S(1)} %constant_dynamic-slice_fusion.6), channel_id=1, source_target_pairs={{1,16},{2,17},{3,18},{4,19},{5,20},{6,21},{7,22},{9,24},{10,25},{1... | collective-permute-start | bytes 196616 | tf_op jit(solution)/shard_map/ppermute | solution.py:267
  189.5 4.2 %copy-start.25 = (bf16[16,16,128]{2,1,0:T(8,128)(2,1)}, bf16[16,16,128]{2,1,0:T(8,128)(2,1)S(1)}, u32[]{:S(2)}) copy-start(bf16[16,16,128]{2,1,0:T(8,128)(2,1)S(1)} %collective-permute-done.11.side_low_ref) | copy-start | bytes 196612
  193.7 0.9 copy-start.13
  193.7 1.1 copy-start.15
  210.8 18.4 %collective-permute-start.13 = (bf16[128,16,128]{2,1,0:T(8,128)(2,1)}, bf16[128,16,128]{2,1,0:T(8,128)(2,1)S(1)}, u32[]{:S(2)}, u32[]{:S(2)}) collective-permute-start(bf16[128,16,128]{2,1,0:T(8,128)(2,1)} %get-tuple-element.29), channel_id=1, source_target_pairs={{0,1},{1,2},{2,3},{3,4},{4,5},{5,6},{6,7},{8,9},{9,10},{10,11},{11... | collective-permute-start | bytes 1572872 | tf_op jit(solution)/shard_map/ppermute | solution.py:268
  212.7 16.5 %collective-permute-start.14 = (bf16[128,16,128]{2,1,0:T(8,128)(2,1)}, bf16[128,16,128]{2,1,0:T(8,128)(2,1)S(1)}, u32[]{:S(2)}, u32[]{:S(2)}) collective-permute-start(bf16[128,16,128]{2,1,0:T(8,128)(2,1)} %get-tuple-element.30), channel_id=1, source_target_pairs={{1,0},{2,1},{3,2},{4,3},{5,4},{6,5},{7,6},{9,8},{10,9},{11,10},{12... | collective-permute-start | bytes 1572872 | tf_op jit(solution)/shard_map/ppermute | solution.py:269
  216.3 12.8 %collective-permute-start.15 = (bf16[16,64,128]{2,1,0:T(8,128)(2,1)S(1)}, bf16[16,64,128]{2,1,0:T(8,128)(2,1)S(1)}, u32[]{:S(2)}, u32[]{:S(2)}) collective-permute-start(bf16[16,64,128]{2,1,0:T(8,128)(2,1)S(1)} %constant_dynamic-slice_fusion.5), channel_id=1, source_target_pairs={{0,16},{8,24},{16,0},{24,8},{1,17},{9,25},{17,1},{25,9},{2,18},{10... | collective-permute-start | bytes 786440 | tf_op jit(solution)/shard_map/ppermute | solution.py:265
  219.3 5.7 %collective-permute-start.16 = (bf16[16,16,128]{2,1,0:T(8,128)(2,1)S(1)}, bf16[16,16,128]{2,1,0:T(8,128)(2,1)S(1)}, u32[]{:S(2)}, u32[]{:S(2)}) collective-permute-start(bf16[16,16,128]{2,1,0:T(8,128)(2,1)S(1)} %constant_dynamic-slice_fusion.4), channel_id=1, source_target_pairs={{0,17},{1,18},{2,19},{3,20},{4,21},{5,22},{6,23},{8,25},{9,26},{10... | collective-permute-start | bytes 196616 | tf_op jit(solution)/shard_map/ppermute | solution.py:266
  222.7 6.5 %collective-permute-start.17 = (bf16[16,16,128]{2,1,0:T(8,128)(2,1)S(1)}, bf16[16,16,128]{2,1,0:T(8,128)(2,1)S(1)}, u32[]{:S(2)}, u32[]{:S(2)}) collective-permute-start(bf16[16,16,128]{2,1,0:T(8,128)(2,1)S(1)} %constant_dynamic-slice_fusion.3), channel_id=1, source_target_pairs={{1,16},{2,17},{3,18},{4,19},{5,20},{6,21},{7,22},{9,24},{10,25},{1... | collective-permute-start | bytes 196616 | tf_op jit(solution)/shard_map/ppermute | solution.py:267
  225.0 4.2 %copy-start.26 = (bf16[16,16,128]{2,1,0:T(8,128)(2,1)}, bf16[16,16,128]{2,1,0:T(8,128)(2,1)S(1)}, u32[]{:S(2)}) copy-start(bf16[16,16,128]{2,1,0:T(8,128)(2,1)S(1)} %collective-permute-done.16.side_low_ref) | copy-start | bytes 196612
  245.7 18.3 %collective-permute-start.18 = (bf16[128,16,128]{2,1,0:T(8,128)(2,1)}, bf16[128,16,128]{2,1,0:T(8,128)(2,1)S(1)}, u32[]{:S(2)}, u32[]{:S(2)}) collective-permute-start(bf16[128,16,128]{2,1,0:T(8,128)(2,1)} %get-tuple-element.32), channel_id=1, source_target_pairs={{0,1},{1,2},{2,3},{3,4},{4,5},{5,6},{6,7},{8,9},{9,10},{10,11},{11... | collective-permute-start | bytes 1572872 | tf_op jit(solution)/shard_map/ppermute | solution.py:268
  247.6 16.4 %collective-permute-start.19 = (bf16[128,16,128]{2,1,0:T(8,128)(2,1)}, bf16[128,16,128]{2,1,0:T(8,128)(2,1)S(1)}, u32[]{:S(2)}, u32[]{:S(2)}) collective-permute-start(bf16[128,16,128]{2,1,0:T(8,128)(2,1)} %get-tuple-element.33), channel_id=1, source_target_pairs={{1,0},{2,1},{3,2},{4,3},{5,4},{6,5},{7,6},{9,8},{10,9},{11,10},{12... | collective-permute-start | bytes 1572872 | tf_op jit(solution)/shard_map/ppermute | solution.py:269
  251.0 13.0 %collective-permute-start.20 = (bf16[16,64,128]{2,1,0:T(8,128)(2,1)S(1)}, bf16[16,64,128]{2,1,0:T(8,128)(2,1)S(1)}, u32[]{:S(2)}, u32[]{:S(2)}) collective-permute-start(bf16[16,64,128]{2,1,0:T(8,128)(2,1)S(1)} %constant_dynamic-slice_fusion.2), channel_id=1, source_target_pairs={{0,16},{8,24},{16,0},{24,8},{1,17},{9,25},{17,1},{25,9},{2,18},{10... | collective-permute-start | bytes 786440 | tf_op jit(solution)/shard_map/ppermute | solution.py:265
  253.2 9.6 %collective-permute-start.21 = (bf16[16,16,128]{2,1,0:T(8,128)(2,1)S(1)}, bf16[16,16,128]{2,1,0:T(8,128)(2,1)S(1)}, u32[]{:S(2)}, u32[]{:S(2)}) collective-permute-start(bf16[16,16,128]{2,1,0:T(8,128)(2,1)S(1)} %constant_dynamic-slice_fusion.1), channel_id=1, source_target_pairs={{0,17},{1,18},{2,19},{3,20},{4,21},{5,22},{6,23},{8,25},{9,26},{10... | collective-permute-start | bytes 196616 | tf_op jit(solution)/shard_map/ppermute | solution.py:266
  257.4 6.6 %collective-permute-start.22 = (bf16[16,16,128]{2,1,0:T(8,128)(2,1)S(1)}, bf16[16,16,128]{2,1,0:T(8,128)(2,1)S(1)}, u32[]{:S(2)}, u32[]{:S(2)}) collective-permute-start(bf16[16,16,128]{2,1,0:T(8,128)(2,1)S(1)} %constant_dynamic-slice_fusion), channel_id=1, source_target_pairs={{1,16},{2,17},{3,18},{4,19},{5,20},{6,21},{7,22},{9,24},{10,25},{1... | collective-permute-start | bytes 196616 | tf_op jit(solution)/shard_map/ppermute | solution.py:267
  262.8 1.3 copy-start.21
  262.8 47.9 %collective-permute-start.2 = (f32[64,64,128]{2,1,0:T(8,128)}, f32[64,64,128]{2,1,0:T(8,128)S(1)}, u32[]{:S(2)}, u32[]{:S(2)}) collective-permute-start(f32[64,64,128]{2,1,0:T(8,128)} %constant_dynamic-slice_fusion.13), channel_id=1, source_target_pairs={{0,8},{8,0},{16,24},{24,16},{1,9},{9,1},{17,25},{25,17},{2,10},{10... | collective-permute-start | bytes 6291464 | tf_op jit(solution)/shard_map/ppermute | solution.py:305
  264.0 1.0 copy-start.10
  286.3 45.4 %collective-permute-start.23 = (f16[64,64,128]{2,1,0:T(8,128)(2,1)S(1)}, f16[64,64,128]{2,1,0:T(8,128)(2,1)S(1)}, u32[]{:S(2)}, u32[]{:S(2)}) collective-permute-start(f16[64,64,128]{2,1,0:T(8,128)(2,1)S(1)} %divide_convert_fusion), channel_id=1, source_target_pairs={{0,8},{8,0},{16,24},{24,16},{1,9},{9,1},{17,25},{25,17},{2,10},{10... | collective-permute-start | bytes 3145736 | tf_op jit(solution)/shard_map/ppermute | solution.py:305
  310.6 2.2 copy-start.4
  312.8 19.7 %copy-start.2 = (f32[128,64,128]{2,1,0:T(8,128)S(1)}, f32[128,64,128]{2,1,0:T(8,128)}, u32[]{:S(2)}) copy-start(f32[128,64,128]{2,1,0:T(8,128)} %get-tuple-element.35.own_ref) | copy-start | bytes 12582916
  315.0 16.7 %collective-permute-start.24 = (f32[]{:T(128)}, f32[]{:T(128)}, u32[]{:S(2)}, u32[]{:S(2)}) collective-permute-start(f32[]{:T(128)} %exp2.7), channel_id=1, source_target_pairs={{0,8},{8,0},{16,24},{24,16},{1,9},{9,1},{17,25},{25,17},{2,10},{10... | collective-permute-start | bytes 20 | tf_op jit(solution)/shard_map/ppermute | solution.py:305
  332.6 3.1 copy-start.1
  (11 other events, 7.9 us)
where the time goes:
time: 337 us; the launch traced here: 336 us
  waiting for transfers between devices  127 us (38%)
  starting transfers between devices  81.4 us (24%)
  Pallas kernels  73.1 us (22%)
  local copies, waits for them, and re-layouts  40.2 us (12%)
  other arithmetic  9.88 us (3%)
    all_to_all x1, waiting for transfers between devices, route_tiles(): lax.all_to_all(outgoing, ('by', 'bz'), split_axis=0, concat_axis=0, axis_...  82.5 us
    pallas_call x4, Pallas kernels, blur_block(): pl.pallas_call(functools.partial(blur_kernel, quotient=quotient, first=fi...  61.5 us
    ppermute x4, waiting for transfers between devices, swap_pair(): lax.ppermute(x, 'by', [(i, i ^ 1) for i in range(lax.axis_size('by'))])  24 us
    ppermute x4, starting transfers between devices, swap_pair(): lax.ppermute(x, 'by', [(i, i ^ 1) for i in range(lax.axis_size('by'))])  19.6 us
    unnamed x67, local copies, waits for them, and re-layouts  14.7 us
    ppermute x4, starting transfers between devices, halo_exchange(): side_low.append(lax.ppermute(cut(face_high), ('by', 'bz'), both(pairs, 1)))  13.9 us
    ppermute x4, waiting for transfers between devices, halo_exchange(): side_high.append(lax.ppermute(cut(face_low), ('by', 'bz'), both(pairs, -1)))  12.2 us
    gather x2, local copies, waits for them, and re-layouts, route_tiles(): jnp.take(planar.reshape((tile_count * channels,) + planar.shape[2:]), row...  11.8 us
  transfers between devices with their start and end apart: 26, of which 9 were waited for; matrix products, arithmetic and copies ran while one was open for 7% of the time, Pallas kernels for 6%

commit v1 on v0

v1 whole, which is shorter than its diff:
```python
import functools

import jax
import jax.numpy as jnp
from jax import lax
from jax.experimental import pallas as pl
from jax.experimental.pallas import tpu as pltpu
from jax.sharding import PartitionSpec as P


SHIFT = 8
ITERS = 2
Z_DEV = 64
HALO = 16
SPILL = 2
F32 = jnp.float32
BF16 = jnp.bfloat16


def in_vmem(count):
    return [pl.BlockSpec(memory_space=pltpu.VMEM) for _ in range(count)]


def place_kernel(channel_ref, own_ref, other_ref, out_ref, sems):
    rows = other_ref.shape[0]
    channel = channel_ref[0]
    copies = [
        pltpu.make_async_copy(own_ref.at[pl.ds(channel * rows, rows)], out_ref.at[channel], sems.at[0]),
        pltpu.make_async_copy(other_ref, out_ref.at[1 - channel], sems.at[1]),
    ]
    for copy in copies:
        copy.start()
    for copy in copies:
        copy.wait()


def place_halves(channel, both_rows, other):
    return pl.pallas_call(
        place_kernel,
        out_shape=jax.ShapeDtypeStruct((2,) + other.shape, other.dtype),
        in_specs=[pl.BlockSpec(memory_space=pltpu.SMEM)] + in_vmem(2),
        out_specs=pl.BlockSpec(memory_space=pl.ANY),
        scratch_shapes=[pltpu.SemaphoreType.DMA((2,))],
        compiler_params=pltpu.CompilerParams(vmem_limit_bytes=12 << 20),
        name="place_halves",
    )(channel[None], both_rows, other)


def pack_kernel(own_ref, turn_ref, block_ref, tiles_ref, *rest, base, count):
    *based, spill_ref, seen_ref = rest
    channels, spill = spill_ref.shape[:2]
    blocks = seen_ref.shape[0]
    for block in range(blocks):
        seen_ref[block] = 0

    def place(t, spilled):
        block = block_ref[own_ref[0] * count + t]
        slot = seen_ref[block]
        seen_ref[block] = slot + 1

        if based:

            @pl.when(slot < base)
            def _():
                for c in range(channels):
                    row = (c * blocks + block) * base + slot
                    based[0][row] = jnp.swapaxes(tiles_ref[t, c], 0, 1)

        late = slot >= base

        @pl.when(late & (spilled // spill == turn_ref[0]))
        def _():
            for c in range(channels):
                spill_ref[c, spilled % spill] = jnp.swapaxes(tiles_ref[t, c], 0, 1)

        return spilled + late.astype(jnp.int32)

    lax.fori_loop(0, count, place, 0)


def pack_tiles(camera_tiles, tile_block, turn, base, with_base):
    count, channels, rows, planes, nx = camera_tiles.shape
    blocks = lax.axis_size("bz")
    shape = lambda *lead: jax.ShapeDtypeStruct(lead + (planes, rows, nx), camera_tiles.dtype)
    outs = [shape(channels, SPILL)]
    if with_base:
        outs = [shape(channels * blocks * base)] + outs
    return pl.pallas_call(
        functools.partial(pack_kernel, base=base, count=count),
        out_shape=outs,
        in_specs=[pl.BlockSpec(memory_space=pltpu.SMEM)] * 3 + in_vmem(1),
        out_specs=in_vmem(len(outs)),
        scratch_shapes=[pltpu.SMEM((blocks,), jnp.int32)],
        compiler_params=pltpu.CompilerParams(vmem_limit_bytes=12 << 20),
        name="pack_tiles" if with_base else "pack_spill",
    )(lax.axis_index("bz")[None], turn[None], tile_block, camera_tiles)


def add_tile(planes_ref, here, start, tile):
    for s in range(tile.shape[0]):
        planes_ref[start + s, here, :] += tile[s].astype(F32)


def add_spill(planes_ref, channel_ref, starts_ref, spill_refs):
    for side, spill_ref in enumerate(spill_refs):
        sources, flips, spill, _, rows = spill_ref.shape[:5]
        for m in range(sources):
            for k in range(spill):
                start = starts_ref[(side * sources + m) * spill + k]

                @pl.when(start >= 0)
                def _():
                    for flip in range(flips):
                        half = channel_ref[0] if flip == 0 else 1 - channel_ref[0]
                        here = pl.ds(pl.multiple_of(half * rows, 8), rows)
                        add_tile(planes_ref, here, start, spill_ref[m, flip, k])


def gather_planes_kernel(channel_ref, starts_ref, spill_starts_ref, arrived_ref, one_ref, two_ref, planes_ref, tail_ref):
    halves, slots, _, rows = arrived_ref.shape[:4]
    height = planes_ref.shape[0]

    def clear(z, carry):
        planes_ref[z] = jnp.zeros(planes_ref.shape[1:], F32)
        return carry

    lax.fori_loop(0, height, clear, 0)

    def add(j, carry):
        start = starts_ref[j]

        @pl.when(start >= 0)
        def _():
            for h in range(halves):
                add_tile(planes_ref, pl.ds(h * rows, rows), start, arrived_ref[h, j])

        return carry

    lax.fori_loop(0, slots, add, 0)
    add_spill(planes_ref, channel_ref, spill_starts_ref, (one_ref, two_ref))
    tail_ref[...] = planes_ref[height - tail_ref.shape[0]:]


def gather_planes(channel, starts, spill_starts, arrived, spills):
    halves, _, planes, rows, nx = arrived.shape
    return pl.pallas_call(
        gather_planes_kernel,
        out_shape=[
            jax.ShapeDtypeStruct((Z_DEV + planes - 1, halves * rows, nx), F32),
            jax.ShapeDtypeStruct((SHIFT + planes, halves * rows, nx), F32),
        ],
        in_specs=[pl.BlockSpec(memory_space=pltpu.SMEM)] * 3 + in_vmem(3),
        out_specs=in_vmem(2),
        compiler_params=pltpu.CompilerParams(vmem_limit_bytes=16 << 20),
        name="gather_planes",
    )(channel[None], starts, spill_starts, arrived, *spills)


def more_planes_kernel(channel_ref, spill_starts_ref, one_ref, two_ref, planes_in_ref, planes_ref, tail_ref):
    planes_ref[...] = planes_in_ref[...]
    add_spill(planes_ref, channel_ref, spill_starts_ref, (one_ref, two_ref))
    tail_ref[...] = planes_ref[planes_ref.shape[0] - tail_ref.shape[0]:]


def more_planes(channel, spill_starts, spills, planes, tail):
    return pl.pallas_call(
        more_planes_kernel,
        out_shape=[jax.ShapeDtypeStruct(x.shape, x.dtype) for x in (planes, tail)],
        in_specs=[pl.BlockSpec(memory_space=pltpu.SMEM)] * 2 + in_vmem(3),
        out_specs=in_vmem(2),
        compiler_params=pltpu.CompilerParams(vmem_limit_bytes=24 << 20),
        name="more_planes",
    )(channel[None], spill_starts, *spills, planes)


def deskew_kernel(odd_ref, backdrop_ref, band_ref, near_ref, far_ref, planes_ref, before_ref,
                  out_ref, cast_ref, out_a_ref, out_b_ref, all_ref, *, pitch):
    ny, nz = out_ref.shape[:2]
    reach = before_ref.shape[0]
    ahead = SHIFT + 1
    backdrop = backdrop_ref[0]
    odd = odd_ref[0] == 1
    for z in range(ahead + nz):
        if z < ahead:
            plane = before_ref[z]
        elif z < reach:
            plane = before_ref[z] + planes_ref[z - ahead]
        else:
            plane = planes_ref[z - ahead]
        all_ref[pl.ds(z * pitch, ny), :] = plane

    def row(y, carry):
        first = (ahead - band_ref[y]) * pitch + y
        value = near_ref[y] * all_ref[pl.ds(first, nz, stride=pitch), :]
        value = value + far_ref[y] * all_ref[pl.ds(first - pitch, nz, stride=pitch), :]
        out_ref[y] = value
        cast = (value + backdrop).astype(BF16)
        cast_ref[y] = cast
        bottom, top = cast[:HALO], cast[nz - HALO:]
        out_a_ref[y] = jnp.where(odd, bottom, top)
        out_b_ref[y] = jnp.where(odd, top, bottom)
        return carry

    lax.fori_loop(0, ny, row, 0, unroll=4)


def deskew(backdrop, band, near, far, planes, before):
    ny, nx = planes.shape[1:]
    pitch = ny + 8
    smem = [pl.BlockSpec(memory_space=pltpu.SMEM)] * 5
    return pl.pallas_call(
        functools.partial(deskew_kernel, pitch=pitch),
        out_shape=[
            jax.ShapeDtypeStruct((ny, Z_DEV, nx), F32),
            jax.ShapeDtypeStruct((ny, Z_DEV, nx), BF16),
            jax.ShapeDtypeStruct((ny, HALO, nx), BF16),
            jax.ShapeDtypeStruct((ny, HALO, nx), BF16),
        ],
        in_specs=smem + in_vmem(2),
        out_specs=in_vmem(4),
        scratch_shapes=[pltpu.VMEM(((Z_DEV + SHIFT + 1) * pitch, nx), F32)],
        compiler_params=pltpu.CompilerParams(vmem_limit_bytes=24 << 20),
        name="deskew",
    )(odd_block(), backdrop, band, near, far, planes, before)


def pair_lanes(x, index, height):
    return jnp.concatenate(
        [x[index * height:(index + 1) * height], x[(index + 1) * height:(index + 2) * height]], axis=1
    )


def blur_x(pieces, mx):
    stack = jnp.concatenate(pieces, axis=0)
    return jnp.dot(jnp.concatenate([stack, stack], axis=1), mx, preferred_element_type=F32).astype(BF16)


def three_terms(column):
    head = column.astype(BF16)
    tail = (column - head.astype(F32)).astype(BF16)
    return jnp.concatenate([head, tail, head], axis=0)


def inner_kernel(own_ref, mx_ref, mz_ref, my_ref, out_ref, mid_ref):
    ny, nz, lanes = own_ref.shape
    mx, mz, my = mx_ref[...], mz_ref[...], my_ref[...]
    pitch = nz + 8
    group = 16
    ahead = 8

    def planes(g, carry):
        alongx = blur_x([own_ref[g * group + k] for k in range(group)], mx)
        for k in range(0, group, 4):
            first, second = pair_lanes(alongx, k, nz), pair_lanes(alongx, k + 2, nz)
            both = jnp.dot(
                mz, jnp.concatenate([first, first, second, second], axis=0), preferred_element_type=F32
            )
            row = pl.multiple_of((g * group + k) * pitch, 8)
            mid_ref[pl.ds(row, nz), :] = both[:nz, :lanes]
            mid_ref[pl.ds(row + pitch, nz), :] = both[:nz, lanes:]
            mid_ref[pl.ds(row + 2 * pitch, nz), :] = both[nz:, :lanes]
            mid_ref[pl.ds(row + 3 * pitch, nz), :] = both[nz:, lanes:]
        return carry

    lax.fori_loop(0, ny // group, planes, 0)

    def columns(g, carry):
        for k in range(ahead):
            z = (g * ahead + k) * 2
            terms = [three_terms(mid_ref[pl.ds(z + i, ny, stride=pitch), :]) for i in range(2)]
            both = jnp.dot(my, jnp.concatenate(terms, axis=1), preferred_element_type=F32)
            out_ref[pl.ds(z, ny, stride=pitch), :] = both[:, :lanes]
            out_ref[pl.ds(z + 1, ny, stride=pitch), :] = both[:, lanes:]
        return carry

    lax.fori_loop(0, nz // (2 * ahead), columns, 0)


def outer_kernel(odd_ref, backdrop_ref, inner_ref, a_ref, b_ref, side_ref, side_a_ref, side_b_ref,
                 mx_ref, mze_ref, mzs_ref, mye_ref, mys_ref, point_ref, *rest, quotient, first, ny, nz):
    if quotient:
        cast_ref, out_a_ref, out_b_ref, edge_ref, rim_ref, more_ref = rest
    else:
        full_ref, peak_ref, cast_ref, out_a_ref, out_b_ref, edge_ref, rim_ref, more_ref = rest
    nside = side_ref.shape[0]
    mx, mze, mzs, mye, mys = mx_ref[...], mze_ref[...], mzs_ref[...], mye_ref[...], mys_ref[...]
    lanes = mx.shape[1]
    pitch = nz + 8
    faces = 2 * HALO
    edge_pitch = faces + 8
    width = nz + faces
    group = 16

    def face_planes(g, carry):
        pieces = []
        for k in range(group):
            pieces += [a_ref[g * group + k], b_ref[g * group + k]]
        alongx = blur_x(pieces, mx)
        for k in range(0, group, 8):
            pairs = []
            for p in range(4):
                pairs += [pair_lanes(alongx, k + 2 * p, faces)] * 2
            both = jnp.dot(mze, jnp.concatenate(pairs, axis=0), preferred_element_type=F32)
            for p in range(4):
                row = pl.multiple_of((g * group + k + 2 * p) * edge_pitch, 8)
                edge_ref[pl.ds(row, faces), :] = both[p * faces:(p + 1) * faces, :lanes]
                edge_ref[pl.ds(row + edge_pitch, faces), :] = both[p * faces:(p + 1) * faces, lanes:]
        return carry

    lax.fori_loop(0, ny // group, face_planes, 0)

    for g in range(nside // group):
        pieces = []
        for k in range(group):
            y = g * group + k
            pieces += [side_a_ref[y], side_ref[y], side_b_ref[y]]
        alongx = blur_x(pieces, mx)
        for k in range(0, group, 2):
            pair = pair_lanes(alongx, k, width)
            both = jnp.dot(mzs, jnp.concatenate([pair, pair], axis=0), preferred_element_type=F32)
            row = (g * group + k) * pitch
            rim_ref[pl.ds(row, nz), :] = both[:, :lanes]
            rim_ref[pl.ds(row + pitch, nz), :] = both[:, lanes:]

    def rim(z):
        return rim_ref[pl.ds(z, nside, stride=pitch), :]

    for z in range(0, nz, 2):
        if z < HALO or z >= nz - HALO:
            e = z if z < HALO else z - nz + faces
            terms = [
                three_terms(jnp.concatenate([edge_ref[pl.ds(e + i, ny, stride=edge_pitch), :], rim(z + i)], axis=0))
                for i in range(2)
            ]
            both = jnp.dot(mye, jnp.concatenate(terms, axis=1), preferred_element_type=F32)
        else:
            terms = [three_terms(rim(z + i)) for i in range(2)]
            both = jnp.dot(mys, jnp.concatenate(terms, axis=1), preferred_element_type=F32)
        more_ref[pl.ds(z, ny, stride=pitch), :] = both[:, :lanes]
        more_ref[pl.ds(z + 1, ny, stride=pitch), :] = both[:, lanes:]

    backdrop = backdrop_ref[0]
    odd = odd_ref[0] == 1

    def finish(y, carry):
        row = pl.multiple_of(y * pitch, 8)
        blurred = inner_ref[pl.ds(row, nz), :] + more_ref[pl.ds(row, nz), :]
        if quotient:
            value = point_ref[y] / (blurred + backdrop)
        else:
            value = (point_ref[y] + backdrop if first else point_ref[y]) * blurred
            full_ref[y] = value
            carry = jnp.maximum(carry, value)
        cast = value.astype(BF16)
        cast_ref[y] = cast
        bottom, top = cast[:HALO], cast[nz - HALO:]
        out_a_ref[y] = jnp.where(odd, bottom, top)
        out_b_ref[y] = jnp.where(odd, top, bottom)
        return carry

    peak = lax.fori_loop(0, ny, finish, 0 if quotient else jnp.zeros((nz, lanes), F32), unroll=8)
    if not quotient:
        peak_ref[...] = peak


def blur_inner(block, matrices):
    ny, nz, nx = block.shape
    return pl.pallas_call(
        inner_kernel,
        out_shape=jax.ShapeDtypeStruct((ny * (nz + 8), nx), F32),
        in_specs=in_vmem(4),
        out_specs=in_vmem(1)[0],
        scratch_shapes=[pltpu.VMEM((ny * (nz + 8), nx), F32)],
        compiler_params=pltpu.CompilerParams(vmem_limit_bytes=20 << 20),
        cost_estimate=pl.CostEstimate(flops=20_000_000_000, transcendentals=0, bytes_accessed=8_000_000),
        name="blur_inner",
    )(block, *matrices)


def blur_outer(quotient, first, backdrop, inner, halos, matrices, point):
    ny, nz, nx = point.shape
    nside = halos[2].shape[0]
    outs = [
        jax.ShapeDtypeStruct((ny, nz, nx), BF16),
        jax.ShapeDtypeStruct((ny, HALO, nx), BF16),
        jax.ShapeDtypeStruct((ny, HALO, nx), BF16),
    ]
    if not quotient:
        outs = [jax.ShapeDtypeStruct((ny, nz, nx), F32), jax.ShapeDtypeStruct((nz, nx), F32)] + outs
    return pl.pallas_call(
        functools.partial(outer_kernel, quotient=quotient, first=first, ny=ny, nz=nz),
        out_shape=outs,
        in_specs=[pl.BlockSpec(memory_space=pltpu.SMEM)] * 2 + in_vmem(12),
        out_specs=in_vmem(len(outs)),
        scratch_shapes=[
            pltpu.VMEM((ny * (2 * HALO + 8), nx), F32),
            pltpu.VMEM((nside * (nz + 8), nx), F32),
            pltpu.VMEM((ny * (nz + 8), nx), F32),
        ],
        compiler_params=pltpu.CompilerParams(vmem_limit_bytes=32 << 20),
        cost_estimate=pl.CostEstimate(flops=10_000_000_000, transcendentals=0, bytes_accessed=16_000_000),
        name="blur_quotient" if quotient else "blur_estimate",
    )(odd_block(), backdrop, inner, *halos, *matrices, point)


def odd_block():
    return (lax.axis_index("bz") % 2)[None]


def partners(count):
    phases = [[(i, i ^ 1) for i in range(count)]]
    if count > 2:
        phases.append([(i, ((i + 1) ^ 1) - 1) for i in range(1, count - 1)])
    return phases


def halo_exchange(field):
    block, *faces = field
    rows = block.shape[0]
    blocks = lax.axis_size("bz")
    odd = (lax.axis_index("by") // 2) % 2
    z_phases = partners(blocks)
    ends = [jnp.where(odd == 1, 0, rows - HALO), jnp.where(odd == 1, rows - HALO, 0)]
    sides = []
    corners = [[] for _ in z_phases]
    for start, pairs in zip(ends, partners(lax.axis_size("by") // 2)):
        pairs = [(2 * a + c, 2 * b + c) for a, b in pairs for c in range(2)]
        sides.append(lax.ppermute(lax.dynamic_slice_in_dim(block, start, HALO, 0), "by", pairs))
        for face, z_pairs, found in zip(faces, z_phases, corners):
            both = [(a * blocks + p, b * blocks + q) for a, b in pairs for p, q in z_pairs]
            found.append(lax.ppermute(lax.dynamic_slice_in_dim(face, start, HALO, 0), ("by", "bz"), both))
    across = [lax.ppermute(face, "bz", pairs) for face, pairs in zip(faces, z_phases)]
    join = lambda parts: parts[0] if len(parts) == 1 else jnp.concatenate(parts, axis=0)
    return *across, join(sides), *[join(found) for found in corners]


def head_tail(matrix):
    head = lax.reduce_precision(matrix, 8, 7)
    return head.astype(BF16), (matrix - head).astype(BF16)


def band(taps, out_place, in_place):
    count = taps.shape[0]
    offset = in_place[None, :] - out_place[:, None] + count // 2
    matches = (offset[:, :, None] == jnp.arange(count)[None, None, :]).astype(F32)
    return jnp.einsum("ijw,cw->cij", matches, jnp.stack([taps, taps[::-1]]), precision=lax.Precision.HIGHEST)


def band_matrices(taps, ny, nz, nx):
    near = jnp.arange(HALO)
    odd_y = (lax.axis_index("by") // 2) % 2 == 1
    odd_z = lax.axis_index("bz") % 2 == 1
    sides = [jnp.where(odd_y, near - HALO, near + ny), jnp.where(odd_y, near + ny, near - HALO)]
    sides = sides[: len(partners(lax.axis_size("by") // 2))]
    face_a = jnp.where(odd_z, near - HALO, near + nz)
    face_b = jnp.where(odd_z, near + nz, near - HALO)
    along, depth, height = jnp.arange(nx), jnp.arange(nz), jnp.arange(ny)
    side = jnp.concatenate(sides)
    edge = jnp.concatenate([near, near + nz - HALO])
    face = jnp.concatenate([face_a, face_b])

    def spread(matrix, count):
        eye = jnp.eye(count, dtype=matrix.dtype)[None, :, None, :, None]
        blocks = eye * matrix[:, None, :, None, :]
        return blocks.reshape(2, count * matrix.shape[1], count * matrix.shape[2])

    mx = jnp.concatenate(head_tail(band(taps[2], along, along)[::-1]), axis=1)
    mz = spread(jnp.concatenate(head_tail(band(taps[1], depth, depth)), axis=2), 2)
    mze = spread(jnp.concatenate(head_tail(band(taps[1], edge, face)), axis=2), 4)
    mzs = jnp.concatenate(
        head_tail(band(taps[1], depth, jnp.concatenate([face_a, depth, face_b]))), axis=2
    )

    def three(columns):
        head, tail = head_tail(band(taps[0], height, columns))
        return jnp.concatenate([head, head, tail], axis=2)

    my, mye, mys = three(height), three(jnp.concatenate([height, side])), three(side)
    return [((mx[i], mz[i], my[i]), (mx[i], mze[i], mzs[i], mye[i], mys[i])) for i in range(2)]


def swap_pair(x):
    return lax.ppermute(x, "by", [(i, i ^ 1) for i in range(lax.axis_size("by"))])


def share_spill(spill):
    blocks = lax.axis_size("bz")
    wide = lax.axis_size("by")
    channel = lax.axis_index("by") % 2
    found = []
    for m in range(0, blocks, 2):
        for flip in range(2):
            piece = lax.dynamic_index_in_dim(spill, channel ^ flip, 0, keepdims=False)
            if m or flip:
                pairs = [(b * blocks + z, (b ^ flip) * blocks + (z ^ m)) for b in range(wide) for z in range(blocks)]
                piece = lax.ppermute(piece, ("by", "bz"), pairs)
            found.append(piece)
    line = jnp.stack(found).reshape((blocks // 2, 2) + spill.shape[1:])
    return line, lax.ppermute(line, "bz", [(z, z ^ 1) for z in range(blocks)])


def route_tiles(camera_tiles, tile_block, tile_offset):
    count = camera_tiles.shape[0]
    blocks = lax.axis_size("bz")
    wide = lax.axis_size("by")
    base = max(1, count // blocks)
    own = lax.axis_index("bz")
    channel = lax.axis_index("by") % 2
    named = tile_block[:, 0]
    outgoing, spill = pack_tiles(camera_tiles, named, jnp.int32(0), base, True)
    groups = [
        [(2 * j + c) * blocks + z for c in range(2) for z in range(blocks)] for j in range(wide // 2)
    ]
    arrived = lax.all_to_all(
        outgoing.reshape((2 * blocks, base) + outgoing.shape[1:]),
        ("by", "bz"), split_axis=0, concat_axis=0, axis_index_groups=groups, tiled=True,
    )
    targets = named.reshape(blocks, count)
    offsets = tile_offset.reshape(blocks, count)
    same = (targets[:, :, None] == targets[:, None, :]) & jnp.tri(count, k=-1, dtype=bool)[None]
    places = jnp.sum(same.astype(jnp.int32), axis=2)
    late = places >= base
    order = jnp.sum(jnp.where(late[:, None, :] & jnp.tri(count, k=-1, dtype=bool)[None], 1, 0), axis=2)
    mine = targets == own
    pick = lambda chosen: jnp.sum(jnp.where(chosen, offsets[:, :, None] + 1, 0), axis=1) - 1
    starts = pick(mine[:, :, None] & (places[:, :, None] == jnp.arange(base))).reshape(-1)
    sources = jnp.concatenate([(own ^ core) ^ jnp.arange(0, blocks, 2) for core in range(2)])

    def spill_starts(turn):
        chosen = (mine & late)[:, :, None] & (order[:, :, None] == turn * SPILL + jnp.arange(SPILL))
        return jnp.take(pick(chosen), sources, axis=0, mode="clip").reshape(-1)

    turns = (jnp.max(jnp.sum(late.astype(jnp.int32), axis=1)) + SPILL - 1) // SPILL
    spills = share_spill(spill)
    arrived = arrived.reshape((2, blocks * base) + arrived.shape[2:])
    planes, tail = gather_planes(channel, starts, spill_starts(0), arrived, spills)

    def turn_step(carry):
        turn, planes, tail = carry
        again = pack_tiles(camera_tiles, named, turn, base, False)[0]
        planes, tail = more_planes(channel, spill_starts(turn), share_spill(again), planes, tail)
        return turn + 1, planes, tail

    planes, tail = lax.cond(
        turns > 1,
        lambda planes, tail: lax.while_loop(lambda c: c[0] < turns, turn_step, (jnp.int32(1), planes, tail))[1:],
        lambda planes, tail: (planes, tail),
        planes,
        tail,
    )
    return planes, tail


def pair_stack(first_is_own, own, other):
    return jnp.stack([jnp.where(first_is_own, own, other), jnp.where(first_is_own, other, own)])


def shards(camera_tiles, tile_block, tile_offset, band_index, interp, psf_taps, background):
    channel = lax.axis_index("by") % 2
    first = channel == 0
    rows = camera_tiles.shape[2]
    table = jnp.concatenate([band_index[:, None].astype(F32), interp.astype(F32)], axis=1)
    table = pair_stack(first, table, swap_pair(table))

    taps = lax.dynamic_index_in_dim(psf_taps, channel, 0, keepdims=False)
    kernels = taps / jnp.sum(taps, axis=1, keepdims=True)
    nx = camera_tiles.shape[4]
    forward, backward = band_matrices(kernels, 2 * rows, Z_DEV, nx)
    backdrop = lax.dynamic_slice_in_dim(background, channel, 1, 0)

    planes, over = route_tiles(camera_tiles, tile_block, tile_offset)
    blocks = lax.axis_size("bz")
    before = lax.ppermute(over, "bz", [(i, i + 1) for i in range(blocks - 1)])
    table = table.reshape(2 * rows, 3)
    deskewed, *field = deskew(backdrop, table[:, 0].astype(jnp.int32), table[:, 1], table[:, 2], planes, before)

    half = lambda x, start: lax.dynamic_slice_in_dim(x, start, rows, 0)
    other_start = (1 - channel) * rows
    deskewed_other = swap_pair(half(deskewed, other_start))

    estimate = deskewed
    for iteration in range(ITERS):
        halos = halo_exchange(field)
        inner = blur_inner(field[0], forward[0])
        field = blur_outer(True, False, backdrop, inner, halos, forward[1], deskewed)
        halos = halo_exchange(field)
        inner = blur_inner(field[0], backward[0])
        estimate, peak, *field = blur_outer(
            False, iteration == 0, backdrop, inner, halos, backward[1], estimate
        )
    deskewed_out = place_halves(channel, deskewed, deskewed_other)

    theirs = half(estimate, other_start)
    scale = jnp.exp2(jnp.floor(jnp.log2(jnp.max(peak))) - 13.0)
    got = swap_pair((theirs / scale).astype(jnp.float16)).astype(F32) * swap_pair(scale)
    return deskewed_out, place_halves(channel, estimate, got)


def solution(mesh):
    placed = (P("bz", None, "by", None, None), P(), P(), P("by"), P("by", None), P(), P())
    return jax.shard_map(
        shards,
        mesh=mesh,
        in_specs=placed,
        out_specs=(P(None, "by", "bz", None), P(None, "by", "bz", None)),
        check_vma=False,
    )
```

time: 337 us -> 280 us (0.83)
  waiting for transfers between devices: 127 us -> 40.4 us
  starting transfers between devices: 81.4 us -> 126 us
  local copies, waits for them, and re-layouts: 40.2 us -> 16.8 us
  other arithmetic: 9.88 us -> 13.6 us
    all_to_all x1, waiting for transfers between devices: 82.5 us -> 2.04 us  [route_tiles(): lax.all_to_all(outgoing.reshape((2 * blocks, base) + outgoing.shape[1:]),...]
    ppermute x4, starting transfers between devices: 19.6 us -> 55.5 us  [swap_pair(): lax.ppermute(x, 'by', [(i, i ^ 1) for i in range(lax.axis_size('by'))])]
    ppermute x4, waiting for transfers between devices: 24 us -> 0.01 us  [swap_pair(): lax.ppermute(x, 'by', [(i, i ^ 1) for i in range(lax.axis_size('by'))])]
    ppermute x20 -> x28, waiting for transfers between devices: 12.4 us -> 29.9 us  [the longest x7 29.9 us: share_spill(): piece = lax.ppermute(piece, ('by', 'bz'), pairs)]
    gather x2 -> x1, local copies, waits for them, and re-layouts: 11.8 us -> 0.55 us  [spill_starts(): return jnp.take(pick(chosen), sources, axis=0, mode='clip').reshape(-1)]
    ppermute x1, starting transfers between devices: 7.23 us -> 16.3 us  [shards(): before = lax.ppermute(over, 'bz', [(i, i + 1) for i in range(blocks - 1)])]
    dynamic_slice x12, local copies, waits for them, and re-layouts: 8.03 us -> 0.21 us  [the longest x4 0.11 us: halo_exchange(): lax.dynamic_slice_in_dim(block, start, HALO, 0)]
    unnamed x67 -> x35, local copies, waits for them, and re-layouts: 14.7 us -> 9.86 us
  transfers between devices with their start and end apart: 26 -> 34, of which waited for: 9 -> 4; matrix products, arithmetic and copies ran while one was open for 7% -> 10% of each run, Pallas kernels for 6% -> 13%
where the time goes in v1:
time: 280 us; the launch traced here: 279 us
  starting transfers between devices  126 us (45%)
  Pallas kernels  74.7 us (27%)
  waiting for transfers between devices  40.4 us (14%)
  local copies, waits for them, and re-layouts  16.8 us (6%)
  other arithmetic  13.6 us (5%)
  matrix products  4.62 us (2%)
  between operations  3.19 us (1%)
    ppermute x4, starting transfers between devices, swap_pair(): lax.ppermute(x, 'by', [(i, i ^ 1) for i in range(lax.axis_size('by'))])  55.5 us
    pallas_call x4, Pallas kernels, blur_outer(): pl.pallas_call(functools.partial(outer_kernel, quotient=quotient, first=f...  30.6 us
    ppermute x7, waiting for transfers between devices, share_spill(): piece = lax.ppermute(piece, ('by', 'bz'), pairs)  29.9 us
    pallas_call x4, Pallas kernels, blur_inner(): pl.pallas_call(inner_kernel, out_shape=jax.ShapeDtypeStruct((ny * (nz + 8...  26.5 us
    ppermute x8, starting transfers between devices, halo_exchange(): lax.ppermute(lax.dynamic_slice_in_dim(face, start, HALO, 0), ('by', 'bz')...  19.5 us
    ppermute x1, starting transfers between devices, shards(): before = lax.ppermute(over, 'bz', [(i, i + 1) for i in range(blocks - 1)])  16.3 us
    ppermute x8, starting transfers between devices, halo_exchange(): lax.ppermute(face, 'bz', pairs)  11.6 us
    ppermute x7, starting transfers between devices, share_spill(): piece = lax.ppermute(piece, ('by', 'bz'), pairs)  11.2 us
  transfers between devices with their start and end apart: 34, of which 4 were waited for; matrix products, arithmetic and copies ran while one was open for 10% of the time, Pallas kernels for 13%

profile of v1, /device:TPU:1, one launch (start us, length us, event | category | flops | bytes accessed | tf_op | source)
XLA Modules:
  0.0 279.4 jit_solution(16886569423901665139)
XLA Ops:
  0.7 3.3 %pack_tiles.1 = (bf16[32,4,64,128]{3,2,1,0:T(8,128)(2,1)S(1)}, bf16[2,2,4,64,128]{4,3,2,1,0:T(8,128)(2,1)S(1)}) custom-call(s32[1]{0:T(128)} %bitcast.23.own_ref, s32[1]{0:T(128)} %constant.202.clone.1.turn_ref, s32[128]{0:T(128)} %bitcast.162, bf16[16,2,64,4,128]{4,3,2,1,0:T(4,128)(2,1)} %tiles_ref.1), custom_call_target="tpu_custom_call" | custom-call | tf_op jit(solution)/shard_map/pack_tiles/pallas_call | solution.py:88
  4.0 1.3 copy-done.4
  5.3 2.1 collective-permute-start.9
  7.4 1.3 collective-permute-start.11
  8.7 2.4 collective-permute-start.12
  12.2 7.1 %all-to-all-start = ((bf16[16,2,4,64,128]{4,3,2,1,0:T(8,128)(2,1)}), bf16[16,2,4,64,128]{4,3,2,1,0:T(8,128)(2,1)S(1)}, u32[]{:S(2)}, u32[]{:S(2)}) async-start(bf16[16,2,4,64,128]{4,3,2,1,0:T(8,128)(2,1)} %bitcast.152), calls=%async_computation | async-start | bytes 4194304 | tf_op jit(solution)/shard_map/all_to_all | solution.py:514
  21.7 1.2 broadcast_add_fusion.4
  24.2 1.4 select_reduce_fusion.2
  25.7 3.2 %collective-permute-start.14 = (bf16[2,4,64,128]{3,2,1,0:T(8,128)(2,1)S(1)}, bf16[2,4,64,128]{3,2,1,0:T(8,128)(2,1)S(1)}, u32[]{:S(2)}, u32[]{:S(2)}) collective-permute-start(bf16[2,4,64,128]{3,2,1,0:T(8,128)(2,1)S(1)} %get-tuple-element.278), channel_id=1, source_target_pairs={{0,6},{1,7},{2,4},{3,5},{4,2},{5,3},{6,0},{7,1},{8,14},{9,15},{10,... | collective-permute-start | bytes 393224 | tf_op jit(solution)/shard_map/ppermute | solution.py:496
  29.7 1.2 collective-permute-start.15
  33.8 26.2 %collective-permute-done.14 = bf16[2,4,64,128]{3,2,1,0:T(8,128)(2,1)S(1)} collective-permute-done((bf16[2,4,64,128]{3,2,1,0:T(8,128)(2,1)S(1)}, bf16[2,4,64,128]{3,2,1,0:T(8,128)(2,1)S(1)}, u32[]{:S(2)}, u32[]{:S(2)}) %collective-permute-start.14) | collective-permute-done | bytes 131104 | tf_op jit(solution)/shard_map/ppermute | solution.py:496
  60.0 3.7 %collective-permute-done.15 = bf16[2,4,64,128]{3,2,1,0:T(8,128)(2,1)S(1)} collective-permute-done((bf16[2,4,64,128]{3,2,1,0:T(8,128)(2,1)S(1)}, bf16[2,4,64,128]{3,2,1,0:T(8,128)(2,1)S(1)}, u32[]{:S(2)}, u32[]{:S(2)}) %collective-permute-start.15) | collective-permute-done | bytes 131104 | tf_op jit(solution)/shard_map/ppermute | solution.py:496
  63.7 1.1 collective-permute-start.16
  64.8 1.3 reduce_max.18
  70.4 2.0 all-to-all-done
  72.4 4.6 %gather_planes.1 = (f32[67,128,128]{2,1,0:T(8,128)}, f32[12,128,128]{2,1,0:T(8,128)}) custom-call(s32[1]{0:T(128)} %bitcast.15.channel_ref, s32[16]{0:T(128)S(1)} %sub.184.starts_ref, s32[16]{0:T(128)S(1)} %reshape.245.spill_starts_ref, bf16[2,16,4,64,128]{4,3,2,1,0:T(8,128)(2,1)S(1)} %bitcast.151, bf16[4,2,2,4,64,128]{5,4,3,2,1,0:T(8,128)(2,1)S(1)} %bitcast.154, ...), custom_call_target="tpu_custom_call" | custom-call | tf_op jit(solution)/shard_map/gather_planes/pallas_call | solution.py:146
  77.1 1.5 collective-permute-start.8
  84.7 1.2 reduce-precision_convert_fusion.4
  87.1 16.3 %collective-permute-start.17 = (f32[12,128,128]{2,1,0:T(8,128)S(1)}, f32[12,128,128]{2,1,0:T(8,128)S(1)}, u32[]{:S(2)}, u32[]{:S(2)}) collective-permute-start(f32[12,128,128]{2,1,0:T(8,128)S(1)} %copy-done.10), channel_id=1, source_target_pairs={{0,1},{1,2},{2,3},{3,4},{4,5},{5,6},{6,7},{8,9},{9,10},{10,11},{11... | collective-permute-start | bytes 2359304 | tf_op jit(solution)/shard_map/ppermute | solution.py:573
  103.9 8.4 %collective-permute-done.17.before_ref = f32[12,128,128]{2,1,0:T(8,128)S(1)} collective-permute-done((f32[12,128,128]{2,1,0:T(8,128)S(1)}, f32[12,128,128]{2,1,0:T(8,128)S(1)}, u32[]{:S(2)}, u32[]{:S(2)}) %collective-permute-start.17) | collective-permute-done | bytes 786464 | tf_op jit(solution)/shard_map/ppermute | solution.py:573
  112.3 5.6 %deskew.1 = (f32[128,64,128]{2,1,0:T(8,128)S(1)}, bf16[128,64,128]{2,1,0:T(8,128)(2,1)S(1)}, bf16[128,16,128]{2,1,0:T(8,128)(2,1)S(1)}, bf16[128,16,128]{2,1,0:T(8,128)(2,1)S(1)}) custom-call(s32[1]{0:T(128)} %bitcast.16.odd_ref, f32[1]{0:T(128)} %dynamic_slice.81.backdrop_ref, s32[128]{0:T(128)S(1)} %get-tuple-element.313.band_ref, ...), custom_call_target="tpu_custom_call" | custom-call | tf_op jit(solution)/shard_map/deskew/pallas_call | solution.py:211
  118.0 4.6 %collective-permute-start.20 = (bf16[128,16,128]{2,1,0:T(8,128)(2,1)S(1)}, bf16[128,16,128]{2,1,0:T(8,128)(2,1)S(1)}, u32[]{:S(2)}, u32[]{:S(2)}) collective-permute-start(bf16[128,16,128]{2,1,0:T(8,128)(2,1)S(1)} %get-tuple-element.227), channel_id=1, source_target_pairs={{1,2},{2,1},{3,4},{4,3},{5,6},{6,5},{9,10},{10,9},{11,12},{12,11},... | collective-permute-start | bytes 1572872 | tf_op jit(solution)/shard_map/ppermute | solution.py:432
  122.6 1.3 collective-permute-start.21
  124.0 5.3 %collective-permute-start.23 = (bf16[16,16,128]{2,1,0:T(8,128)(2,1)S(1)}, bf16[16,16,128]{2,1,0:T(8,128)(2,1)S(1)}, u32[]{:S(2)}, u32[]{:S(2)}) collective-permute-start(bf16[16,16,128]{2,1,0:T(8,128)(2,1)S(1)} %constant_dynamic-slice_fusion.9), channel_id=1, source_target_pairs={{1,18},{2,17},{3,20},{4,19},{5,22},{6,21},{9,26},{10,25},{11,28},{... | collective-permute-start | bytes 196616 | tf_op jit(solution)/shard_map/ppermute | solution.py:431
  129.3 6.6 %blur_inner.4.inner_ref = f32[9216,128]{1,0:T(8,128)S(1)} custom-call(bf16[128,64,128]{2,1,0:T(8,128)(2,1)S(1)} %get-tuple-element.225.own_ref, bf16[256,128]{1,0:T(8,128)(2,1)S(1)} %get-tuple-element.286.mx_ref, bf16[128,256]{1,0:T(8,128)(2,1)S(1)} %bitcast.155, bf16[128,384]{1,0:T(8,128)(2,1)S(1)} %get-tuple-element.282.my_ref), custom_call_target="tpu_custom_call" | custom-call | flops 20000000000 | bytes 8000000 | tf_op jit(solution)/shard_map/blur_inner/pallas_call | solution.py:368
  135.9 1.6 constant_dynamic-slice_fusion.13
  137.5 7.1 %blur_quotient.2 = (bf16[128,64,128]{2,1,0:T(8,128)(2,1)S(1)}, bf16[128,16,128]{2,1,0:T(8,128)(2,1)S(1)}, bf16[128,16,128]{2,1,0:T(8,128)(2,1)S(1)}) custom-call(s32[1]{0:T(128)} %bitcast.16.odd_ref, f32[1]{0:T(128)} %dynamic_slice.81.backdrop_ref, f32[9216,128]{1,0:T(8,128)S(1)} %blur_inner.4.inner_ref, ...), custom_call_target="tpu_custom_call" | custom-call | flops 10000000000 | bytes 16000000 | tf_op jit(solution)/shard_map/blur_quotient/pallas_call | solution.py:390
  144.7 2.3 collective-permute-start.25
  147.7 4.6 %collective-permute-start.28 = (bf16[16,16,128]{2,1,0:T(8,128)(2,1)S(1)}, bf16[16,16,128]{2,1,0:T(8,128)(2,1)S(1)}, u32[]{:S(2)}, u32[]{:S(2)}) collective-permute-start(bf16[16,16,128]{2,1,0:T(8,128)(2,1)S(1)} %constant_dynamic-slice_fusion.6), channel_id=1, source_target_pairs={{1,18},{2,17},{3,20},{4,19},{5,22},{6,21},{9,26},{10,25},{11,28},{... | collective-permute-start | bytes 196616 | tf_op jit(solution)/shard_map/ppermute | solution.py:431
  152.3 6.6 %blur_inner.5.inner_ref = f32[9216,128]{1,0:T(8,128)S(1)} custom-call(bf16[128,64,128]{2,1,0:T(8,128)(2,1)S(1)} %get-tuple-element.228.own_ref, bf16[256,128]{1,0:T(8,128)(2,1)S(1)} %get-tuple-element.285.mx_ref, bf16[128,256]{1,0:T(8,128)(2,1)S(1)} %bitcast.157, bf16[128,384]{1,0:T(8,128)(2,1)S(1)} %get-tuple-element.281.my_ref), custom_call_target="tpu_custom_call" | custom-call | flops 20000000000 | bytes 8000000 | tf_op jit(solution)/shard_map/blur_inner/pallas_call | solution.py:368
  159.0 7.7 %blur_estimate.2 = (f32[128,64,128]{2,1,0:T(8,128)S(1)}, f32[64,128]{1,0:T(8,128)}, bf16[128,64,128]{2,1,0:T(8,128)(2,1)S(1)}, bf16[128,16,128]{2,1,0:T(8,128)(2,1)S(1)}, bf16[128,16,128]{2,1,0:T(8,128)(2,1)S(1)}) custom-call(s32[1]{0:T(128)} %bitcast.16.odd_ref, f32[1]{0:T(128)} %dynamic_slice.81.backdrop_ref, f32[9216,128]{1,0:T(8,128)S(1)} %blur_inner.5.inner_ref, ...), custom_call_target="tpu_custom_call" | custom-call | flops 10000000000 | bytes 16000000 | tf_op jit(solution)/shard_map/blur_estimate/pallas_call | solution.py:390
  166.8 2.1 collective-permute-start.30
  168.9 1.2 collective-permute-start.31
  170.2 4.7 %collective-permute-start.33 = (bf16[16,16,128]{2,1,0:T(8,128)(2,1)S(1)}, bf16[16,16,128]{2,1,0:T(8,128)(2,1)S(1)}, u32[]{:S(2)}, u32[]{:S(2)}) collective-permute-start(bf16[16,16,128]{2,1,0:T(8,128)(2,1)S(1)} %constant_dynamic-slice_fusion.3), channel_id=1, source_target_pairs={{1,18},{2,17},{3,20},{4,19},{5,22},{6,21},{9,26},{10,25},{11,28},{... | collective-permute-start | bytes 196616 | tf_op jit(solution)/shard_map/ppermute | solution.py:431
  174.9 6.6 %blur_inner.6.inner_ref = f32[9216,128]{1,0:T(8,128)S(1)} custom-call(bf16[128,64,128]{2,1,0:T(8,128)(2,1)S(1)} %get-tuple-element.231.own_ref, bf16[256,128]{1,0:T(8,128)(2,1)S(1)} %get-tuple-element.286.mx_ref, bf16[128,256]{1,0:T(8,128)(2,1)S(1)} %bitcast.156, bf16[128,384]{1,0:T(8,128)(2,1)S(1)} %get-tuple-element.282.my_ref), custom_call_target="tpu_custom_call" | custom-call | flops 20000000000 | bytes 8000000 | tf_op jit(solution)/shard_map/blur_inner/pallas_call | solution.py:368
  181.6 7.1 %blur_quotient.3 = (bf16[128,64,128]{2,1,0:T(8,128)(2,1)S(1)}, bf16[128,16,128]{2,1,0:T(8,128)(2,1)S(1)}, bf16[128,16,128]{2,1,0:T(8,128)(2,1)S(1)}) custom-call(s32[1]{0:T(128)} %bitcast.16.odd_ref, f32[1]{0:T(128)} %dynamic_slice.81.backdrop_ref, f32[9216,128]{1,0:T(8,128)S(1)} %blur_inner.6.inner_ref, ...), custom_call_target="tpu_custom_call" | custom-call | flops 10000000000 | bytes 16000000 | tf_op jit(solution)/shard_map/blur_quotient/pallas_call | solution.py:390
  188.8 2.4 collective-permute-start.35
  192.0 4.6 %collective-permute-start.38 = (bf16[16,16,128]{2,1,0:T(8,128)(2,1)S(1)}, bf16[16,16,128]{2,1,0:T(8,128)(2,1)S(1)}, u32[]{:S(2)}, u32[]{:S(2)}) collective-permute-start(bf16[16,16,128]{2,1,0:T(8,128)(2,1)S(1)} %constant_dynamic-slice_fusion), channel_id=1, source_target_pairs={{1,18},{2,17},{3,20},{4,19},{5,22},{6,21},{9,26},{10,25},{11,28},{... | collective-permute-start | bytes 196616 | tf_op jit(solution)/shard_map/ppermute | solution.py:431
  196.6 6.6 %blur_inner.7.inner_ref = f32[9216,128]{1,0:T(8,128)S(1)} custom-call(bf16[128,64,128]{2,1,0:T(8,128)(2,1)S(1)} %get-tuple-element.234.own_ref, bf16[256,128]{1,0:T(8,128)(2,1)S(1)} %get-tuple-element.285.mx_ref, bf16[128,256]{1,0:T(8,128)(2,1)S(1)} %bitcast.158, bf16[128,384]{1,0:T(8,128)(2,1)S(1)} %get-tuple-element.281.my_ref), custom_call_target="tpu_custom_call" | custom-call | flops 20000000000 | bytes 8000000 | tf_op jit(solution)/shard_map/blur_inner/pallas_call | solution.py:368
  203.3 1.3 collective-permute-start.18
  204.6 8.7 %blur_estimate.3 = (f32[128,64,128]{2,1,0:T(8,128)S(1)}, f32[64,128]{1,0:T(8,128)S(1)}, bf16[128,64,128]{2,1,0:T(8,128)(2,1)}, bf16[128,16,128]{2,1,0:T(8,128)(2,1)}, bf16[128,16,128]{2,1,0:T(8,128)(2,1)}) custom-call(s32[1]{0:T(128)} %bitcast.16.odd_ref, f32[1]{0:T(128)} %dynamic_slice.81.backdrop_ref, f32[9216,128]{1,0:T(8,128)S(1)} %blur_inner.7.inner_ref, ...), custom_call_target="tpu_custom_call" | custom-call | flops 10000000000 | bytes 16000000 | tf_op jit(solution)/shard_map/blur_estimate/pallas_call | solution.py:390
  213.2 2.0 copy-done.2
  216.6 1.9 divide_convert_fusion
  218.8 52.4 %collective-permute-start.40 = (f32[]{:T(128)}, f32[]{:T(128)}, u32[]{:S(2)}, u32[]{:S(2)}) collective-permute-start(f32[]{:T(128)} %exp2.7), channel_id=1, source_target_pairs={{0,8},{8,0},{16,24},{24,16},{1,9},{9,1},{17,25},{25,17},{2,10},{10... | collective-permute-start | bytes 20 | tf_op jit(solution)/shard_map/ppermute | solution.py:483
  271.3 2.2 copy-done.1
  273.5 2.1 place_halves.2
  275.6 1.5 convert_multiply_fusion.other_ref
  277.2 2.0 place_halves.3
  (180 shorter events, 22.4 us)
Async XLA Ops:
  4.0 1.3 copy-start.4
  5.3 20.3 %collective-permute-start.9 = (bf16[2,4,64,128]{3,2,1,0:T(8,128)(2,1)S(1)}, bf16[2,4,64,128]{3,2,1,0:T(8,128)(2,1)}, u32[]{:S(2)}, u32[]{:S(2)}) collective-permute-start(bf16[2,4,64,128]{3,2,1,0:T(8,128)(2,1)S(1)} %get-tuple-element.280), channel_id=1, source_target_pairs={{0,8},{1,9},{2,10},{3,11},{4,12},{5,13},{6,14},{7,15},{8,0},{9,1},... | collective-permute-start | bytes 393224 | tf_op jit(solution)/shard_map/ppermute | solution.py:496
  7.4 24.5 %collective-permute-start.11 = (bf16[2,4,64,128]{3,2,1,0:T(8,128)(2,1)S(1)}, bf16[2,4,64,128]{3,2,1,0:T(8,128)(2,1)S(1)}, u32[]{:S(2)}, u32[]{:S(2)}) collective-permute-start(bf16[2,4,64,128]{3,2,1,0:T(8,128)(2,1)S(1)} %get-tuple-element.280), channel_id=1, source_target_pairs={{0,10},{1,11},{2,8},{3,9},{4,14},{5,15},{6,12},{7,13},{8,2},{9,3},... | collective-permute-start | bytes 393224 | tf_op jit(solution)/shard_map/ppermute | solution.py:496
  8.7 21.1 %collective-permute-start.10 = (bf16[2,4,64,128]{3,2,1,0:T(8,128)(2,1)S(1)}, bf16[2,4,64,128]{3,2,1,0:T(8,128)(2,1)}, u32[]{:S(2)}, u32[]{:S(2)}) collective-permute-start(bf16[2,4,64,128]{3,2,1,0:T(8,128)(2,1)S(1)} %get-tuple-element.278), channel_id=1, source_target_pairs={{0,2},{1,3},{2,0},{3,1},{4,6},{5,7},{6,4},{7,5},{8,10},{9,11},{10,... | collective-permute-start | bytes 393224 | tf_op jit(solution)/shard_map/ppermute | solution.py:496
  8.7 23.2 %collective-permute-start.12 = (bf16[2,4,64,128]{3,2,1,0:T(8,128)(2,1)S(1)}, bf16[2,4,64,128]{3,2,1,0:T(8,128)(2,1)}, u32[]{:S(2)}, u32[]{:S(2)}) collective-permute-start(bf16[2,4,64,128]{3,2,1,0:T(8,128)(2,1)S(1)} %get-tuple-element.278), channel_id=1, source_target_pairs={{0,4},{1,5},{2,6},{3,7},{4,0},{5,1},{6,2},{7,3},{8,12},{9,13},{10,... | collective-permute-start | bytes 393224 | tf_op jit(solution)/shard_map/ppermute | solution.py:496
  11.2 21.7 %collective-permute-start.13 = (bf16[2,4,64,128]{3,2,1,0:T(8,128)(2,1)S(1)}, bf16[2,4,64,128]{3,2,1,0:T(8,128)(2,1)}, u32[]{:S(2)}, u32[]{:S(2)}) collective-permute-start(bf16[2,4,64,128]{3,2,1,0:T(8,128)(2,1)S(1)} %get-tuple-element.280), channel_id=1, source_target_pairs={{0,12},{1,13},{2,14},{3,15},{4,8},{5,9},{6,10},{7,11},{8,4},{9,5},... | collective-permute-start | bytes 393224 | tf_op jit(solution)/shard_map/ppermute | solution.py:496
  12.2 7.6 %copy-start.5 = (s32[128,1]{0,1:T(1,128)S(1)}, s32[128,1]{0,1:T(1,128)}, u32[]{:S(2)}) copy-start(s32[128,1]{0,1:T(1,128)} %param.12) | copy-start | bytes 1540
  12.2 60.3 %all-to-all-start = ((bf16[16,2,4,64,128]{4,3,2,1,0:T(8,128)(2,1)}), bf16[16,2,4,64,128]{4,3,2,1,0:T(8,128)(2,1)S(1)}, u32[]{:S(2)}, u32[]{:S(2)}) async-start(bf16[16,2,4,64,128]{4,3,2,1,0:T(8,128)(2,1)} %bitcast.152), calls=%async_computation | async-start | bytes 4194304 | tf_op jit(solution)/shard_map/all_to_all | solution.py:514
  21.5 1.4 copy-start.7
  25.7 34.3 %collective-permute-start.14 = (bf16[2,4,64,128]{3,2,1,0:T(8,128)(2,1)S(1)}, bf16[2,4,64,128]{3,2,1,0:T(8,128)(2,1)S(1)}, u32[]{:S(2)}, u32[]{:S(2)}) collective-permute-start(bf16[2,4,64,128]{3,2,1,0:T(8,128)(2,1)S(1)} %get-tuple-element.278), channel_id=1, source_target_pairs={{0,6},{1,7},{2,4},{3,5},{4,2},{5,3},{6,0},{7,1},{8,14},{9,15},{10,... | collective-permute-start | bytes 393224 | tf_op jit(solution)/shard_map/ppermute | solution.py:496
  29.7 34.0 %collective-permute-start.15 = (bf16[2,4,64,128]{3,2,1,0:T(8,128)(2,1)S(1)}, bf16[2,4,64,128]{3,2,1,0:T(8,128)(2,1)S(1)}, u32[]{:S(2)}, u32[]{:S(2)}) collective-permute-start(bf16[2,4,64,128]{3,2,1,0:T(8,128)(2,1)S(1)} %get-tuple-element.280), channel_id=1, source_target_pairs={{0,14},{1,15},{2,12},{3,13},{4,10},{5,11},{6,8},{7,9},{8,6},{9,7},... | collective-permute-start | bytes 393224 | tf_op jit(solution)/shard_map/ppermute | solution.py:496
  63.7 6.6 %collective-permute-start.16 = (bf16[4,2,2,4,64,128]{5,4,3,2,1,0:T(8,128)(2,1)S(1)}, bf16[4,2,2,4,64,128]{5,4,3,2,1,0:T(8,128)(2,1)}, u32[]{:S(2)}, u32[]{:S(2)}) collective-permute-start(bf16[4,2,2,4,64,128]{5,4,3,2,1,0:T(8,128)(2,1)S(1)} %bitcast.153), channel_id=1, source_target_pairs={{0,1},{1,0},{2,3},{3,2},{4,5},{5,4},{6,7},{7,6},{8,9},{9,8},{10,11... | collective-permute-start | bytes 3145736 | tf_op jit(solution)/shard_map/ppermute | solution.py:499
  72.4 4.7 %copy-start.6 = (s32[128,1]{0,1:T(1,128)S(1)}, s32[128,1]{0,1:T(1,128)}, u32[]{:S(2)}) copy-start(s32[128,1]{0,1:T(1,128)} %param.12) | copy-start | bytes 1540
  72.4 4.7 %copy-start.8 = (pred[8,16]{1,0:T(8,128)(4,1)S(1)}, pred[8,16]{1,0:T(8,128)(4,1)}, u32[]{:S(2)}) copy-start(pred[8,16]{1,0:T(8,128)(4,1)} %copy-done.7) | copy-start | bytes 388
  72.4 4.7 %copy-start.11 = (s32[128]{0:T(128)S(1)}, s32[128]{0:T(128)}, u32[]{:S(2)}) copy-start(s32[128]{0:T(128)} %param.13) | copy-start | bytes 1540
  77.1 1.6 copy-start.9
  77.1 3.5 %copy-start.12 = (f32[2]{0:T(128)S(1)}, f32[2]{0:T(128)}, u32[]{:S(2)}) copy-start(f32[2]{0:T(128)} %param.17) | copy-start | bytes 28
  77.1 26.7 %collective-permute-start.8 = (f32[64,3]{0,1:T(4,128)S(1)}, f32[64,3]{0,1:T(4,128)S(1)}, u32[]{:S(2)}, u32[]{:S(2)}) collective-permute-start(f32[64,3]{0,1:T(4,128)S(1)} %pad_maximum_fusion.8), channel_id=1, source_target_pairs={{0,8},{8,0},{16,24},{24,16},{1,9},{9,1},{17,25},{25,17},{2,10},{10... | collective-permute-start | bytes 2312 | tf_op jit(solution)/shard_map/ppermute | solution.py:483
  84.1 3.0 %copy-start.10 = (f32[12,128,128]{2,1,0:T(8,128)S(1)}, f32[12,128,128]{2,1,0:T(8,128)}, u32[]{:S(2)}) copy-start(f32[12,128,128]{2,1,0:T(8,128)} %get-tuple-element.223) | copy-start | bytes 2359300
  87.1 25.2 %collective-permute-start.17 = (f32[12,128,128]{2,1,0:T(8,128)S(1)}, f32[12,128,128]{2,1,0:T(8,128)S(1)}, u32[]{:S(2)}, u32[]{:S(2)}) collective-permute-start(f32[12,128,128]{2,1,0:T(8,128)S(1)} %copy-done.10), channel_id=1, source_target_pairs={{0,1},{1,2},{2,3},{3,4},{4,5},{5,6},{6,7},{8,9},{9,10},{10,11},{11... | collective-permute-start | bytes 2359304 | tf_op jit(solution)/shard_map/ppermute | solution.py:573
  117.9 63.7 %copy-start = (f32[128,64,128]{2,1,0:T(8,128)}, f32[128,64,128]{2,1,0:T(8,128)S(1)}, u32[]{:S(2)}) copy-start(f32[128,64,128]{2,1,0:T(8,128)S(1)} %get-tuple-element.224.own_ref.point_ref) | copy-start | bytes 12582916
  117.9 19.6 %collective-permute-start.19 = (bf16[128,16,128]{2,1,0:T(8,128)(2,1)S(1)}, bf16[128,16,128]{2,1,0:T(8,128)(2,1)S(1)}, u32[]{:S(2)}, u32[]{:S(2)}) collective-permute-start(bf16[128,16,128]{2,1,0:T(8,128)(2,1)S(1)} %get-tuple-element.226), channel_id=1, source_target_pairs={{0,1},{1,0},{2,3},{3,2},{4,5},{5,4},{6,7},{7,6},{8,9},{9,8},{10,11... | collective-permute-start | bytes 1572872 | tf_op jit(solution)/shard_map/ppermute | solution.py:432
  118.0 19.5 %collective-permute-start.20 = (bf16[128,16,128]{2,1,0:T(8,128)(2,1)S(1)}, bf16[128,16,128]{2,1,0:T(8,128)(2,1)S(1)}, u32[]{:S(2)}, u32[]{:S(2)}) collective-permute-start(bf16[128,16,128]{2,1,0:T(8,128)(2,1)S(1)} %get-tuple-element.227), channel_id=1, source_target_pairs={{1,2},{2,1},{3,4},{4,3},{5,6},{6,5},{9,10},{10,9},{11,12},{12,11},... | collective-permute-start | bytes 1572872 | tf_op jit(solution)/shard_map/ppermute | solution.py:432
  122.6 14.9 %collective-permute-start.21 = (bf16[16,64,128]{2,1,0:T(8,128)(2,1)S(1)}, bf16[16,64,128]{2,1,0:T(8,128)(2,1)S(1)}, u32[]{:S(2)}, u32[]{:S(2)}) collective-permute-start(bf16[16,64,128]{2,1,0:T(8,128)(2,1)S(1)} %constant_dynamic-slice_fusion.11), channel_id=1, source_target_pairs={{0,16},{8,24},{16,0},{24,8},{1,17},{9,25},{17,1},{25,9},{2,18},{10... | collective-permute-start | bytes 786440 | tf_op jit(solution)/shard_map/ppermute | solution.py:428
  124.0 13.5 %collective-permute-start.22 = (bf16[16,16,128]{2,1,0:T(8,128)(2,1)S(1)}, bf16[16,16,128]{2,1,0:T(8,128)(2,1)S(1)}, u32[]{:S(2)}, u32[]{:S(2)}) collective-permute-start(bf16[16,16,128]{2,1,0:T(8,128)(2,1)S(1)} %constant_dynamic-slice_fusion.10), channel_id=1, source_target_pairs={{0,17},{1,16},{2,19},{3,18},{4,21},{5,20},{6,23},{7,22},{8,25},{9,... | collective-permute-start | bytes 196616 | tf_op jit(solution)/shard_map/ppermute | solution.py:431
  124.0 13.5 %collective-permute-start.23 = (bf16[16,16,128]{2,1,0:T(8,128)(2,1)S(1)}, bf16[16,16,128]{2,1,0:T(8,128)(2,1)S(1)}, u32[]{:S(2)}, u32[]{:S(2)}) collective-permute-start(bf16[16,16,128]{2,1,0:T(8,128)(2,1)S(1)} %constant_dynamic-slice_fusion.9), channel_id=1, source_target_pairs={{1,18},{2,17},{3,20},{4,19},{5,22},{6,21},{9,26},{10,25},{11,28},{... | collective-permute-start | bytes 196616 | tf_op jit(solution)/shard_map/ppermute | solution.py:431
  144.6 14.3 %collective-permute-start.24 = (bf16[128,16,128]{2,1,0:T(8,128)(2,1)S(1)}, bf16[128,16,128]{2,1,0:T(8,128)(2,1)S(1)}, u32[]{:S(2)}, u32[]{:S(2)}) collective-permute-start(bf16[128,16,128]{2,1,0:T(8,128)(2,1)S(1)} %get-tuple-element.229), channel_id=1, source_target_pairs={{0,1},{1,0},{2,3},{3,2},{4,5},{5,4},{6,7},{7,6},{8,9},{9,8},{10,11... | collective-permute-start | bytes 1572872 | tf_op jit(solution)/shard_map/ppermute | solution.py:432
  144.7 14.2 %collective-permute-start.25 = (bf16[128,16,128]{2,1,0:T(8,128)(2,1)S(1)}, bf16[128,16,128]{2,1,0:T(8,128)(2,1)S(1)}, u32[]{:S(2)}, u32[]{:S(2)}) collective-permute-start(bf16[128,16,128]{2,1,0:T(8,128)(2,1)S(1)} %get-tuple-element.230), channel_id=1, source_target_pairs={{1,2},{2,1},{3,4},{4,3},{5,6},{6,5},{9,10},{10,9},{11,12},{12,11},... | collective-permute-start | bytes 1572872 | tf_op jit(solution)/shard_map/ppermute | solution.py:432
  147.1 11.8 %collective-permute-start.26 = (bf16[16,64,128]{2,1,0:T(8,128)(2,1)S(1)}, bf16[16,64,128]{2,1,0:T(8,128)(2,1)S(1)}, u32[]{:S(2)}, u32[]{:S(2)}) collective-permute-start(bf16[16,64,128]{2,1,0:T(8,128)(2,1)S(1)} %constant_dynamic-slice_fusion.8), channel_id=1, source_target_pairs={{0,16},{8,24},{16,0},{24,8},{1,17},{9,25},{17,1},{25,9},{2,18},{10... | collective-permute-start | bytes 786440 | tf_op jit(solution)/shard_map/ppermute | solution.py:428
  147.4 11.5 %collective-permute-start.27 = (bf16[16,16,128]{2,1,0:T(8,128)(2,1)S(1)}, bf16[16,16,128]{2,1,0:T(8,128)(2,1)S(1)}, u32[]{:S(2)}, u32[]{:S(2)}) collective-permute-start(bf16[16,16,128]{2,1,0:T(8,128)(2,1)S(1)} %constant_dynamic-slice_fusion.7), channel_id=1, source_target_pairs={{0,17},{1,16},{2,19},{3,18},{4,21},{5,20},{6,23},{7,22},{8,25},{9,... | collective-permute-start | bytes 196616 | tf_op jit(solution)/shard_map/ppermute | solution.py:431
  147.7 11.3 %collective-permute-start.28 = (bf16[16,16,128]{2,1,0:T(8,128)(2,1)S(1)}, bf16[16,16,128]{2,1,0:T(8,128)(2,1)S(1)}, u32[]{:S(2)}, u32[]{:S(2)}) collective-permute-start(bf16[16,16,128]{2,1,0:T(8,128)(2,1)S(1)} %constant_dynamic-slice_fusion.6), channel_id=1, source_target_pairs={{1,18},{2,17},{3,20},{4,19},{5,22},{6,21},{9,26},{10,25},{11,28},{... | collective-permute-start | bytes 196616 | tf_op jit(solution)/shard_map/ppermute | solution.py:431
  166.7 14.9 %collective-permute-start.29 = (bf16[128,16,128]{2,1,0:T(8,128)(2,1)S(1)}, bf16[128,16,128]{2,1,0:T(8,128)(2,1)S(1)}, u32[]{:S(2)}, u32[]{:S(2)}) collective-permute-start(bf16[128,16,128]{2,1,0:T(8,128)(2,1)S(1)} %get-tuple-element.232), channel_id=1, source_target_pairs={{0,1},{1,0},{2,3},{3,2},{4,5},{5,4},{6,7},{7,6},{8,9},{9,8},{10,11... | collective-permute-start | bytes 1572872 | tf_op jit(solution)/shard_map/ppermute | solution.py:432
  166.8 14.8 %collective-permute-start.30 = (bf16[128,16,128]{2,1,0:T(8,128)(2,1)S(1)}, bf16[128,16,128]{2,1,0:T(8,128)(2,1)S(1)}, u32[]{:S(2)}, u32[]{:S(2)}) collective-permute-start(bf16[128,16,128]{2,1,0:T(8,128)(2,1)S(1)} %get-tuple-element.233), channel_id=1, source_target_pairs={{1,2},{2,1},{3,4},{4,3},{5,6},{6,5},{9,10},{10,9},{11,12},{12,11},... | collective-permute-start | bytes 1572872 | tf_op jit(solution)/shard_map/ppermute | solution.py:432
  168.9 12.6 %collective-permute-start.31 = (bf16[16,64,128]{2,1,0:T(8,128)(2,1)S(1)}, bf16[16,64,128]{2,1,0:T(8,128)(2,1)S(1)}, u32[]{:S(2)}, u32[]{:S(2)}) collective-permute-start(bf16[16,64,128]{2,1,0:T(8,128)(2,1)S(1)} %constant_dynamic-slice_fusion.5), channel_id=1, source_target_pairs={{0,16},{8,24},{16,0},{24,8},{1,17},{9,25},{17,1},{25,9},{2,18},{10... | collective-permute-start | bytes 786440 | tf_op jit(solution)/shard_map/ppermute | solution.py:428
  170.2 11.4 %collective-permute-start.32 = (bf16[16,16,128]{2,1,0:T(8,128)(2,1)S(1)}, bf16[16,16,128]{2,1,0:T(8,128)(2,1)S(1)}, u32[]{:S(2)}, u32[]{:S(2)}) collective-permute-start(bf16[16,16,128]{2,1,0:T(8,128)(2,1)S(1)} %constant_dynamic-slice_fusion.4), channel_id=1, source_target_pairs={{0,17},{1,16},{2,19},{3,18},{4,21},{5,20},{6,23},{7,22},{8,25},{9,... | collective-permute-start | bytes 196616 | tf_op jit(solution)/shard_map/ppermute | solution.py:431
  170.2 11.4 %collective-permute-start.33 = (bf16[16,16,128]{2,1,0:T(8,128)(2,1)S(1)}, bf16[16,16,128]{2,1,0:T(8,128)(2,1)S(1)}, u32[]{:S(2)}, u32[]{:S(2)}) collective-permute-start(bf16[16,16,128]{2,1,0:T(8,128)(2,1)S(1)} %constant_dynamic-slice_fusion.3), channel_id=1, source_target_pairs={{1,18},{2,17},{3,20},{4,19},{5,22},{6,21},{9,26},{10,25},{11,28},{... | collective-permute-start | bytes 196616 | tf_op jit(solution)/shard_map/ppermute | solution.py:431
  188.7 15.8 %collective-permute-start.34 = (bf16[128,16,128]{2,1,0:T(8,128)(2,1)S(1)}, bf16[128,16,128]{2,1,0:T(8,128)(2,1)S(1)}, u32[]{:S(2)}, u32[]{:S(2)}) collective-permute-start(bf16[128,16,128]{2,1,0:T(8,128)(2,1)S(1)} %get-tuple-element.235), channel_id=1, source_target_pairs={{0,1},{1,0},{2,3},{3,2},{4,5},{5,4},{6,7},{7,6},{8,9},{9,8},{10,11... | collective-permute-start | bytes 1572872 | tf_op jit(solution)/shard_map/ppermute | solution.py:432
  188.8 15.7 %collective-permute-start.35 = (bf16[128,16,128]{2,1,0:T(8,128)(2,1)S(1)}, bf16[128,16,128]{2,1,0:T(8,128)(2,1)S(1)}, u32[]{:S(2)}, u32[]{:S(2)}) collective-permute-start(bf16[128,16,128]{2,1,0:T(8,128)(2,1)S(1)} %get-tuple-element.236), channel_id=1, source_target_pairs={{1,2},{2,1},{3,4},{4,3},{5,6},{6,5},{9,10},{10,9},{11,12},{12,11},... | collective-permute-start | bytes 1572872 | tf_op jit(solution)/shard_map/ppermute | solution.py:432
  191.2 13.3 %collective-permute-start.36 = (bf16[16,64,128]{2,1,0:T(8,128)(2,1)S(1)}, bf16[16,64,128]{2,1,0:T(8,128)(2,1)S(1)}, u32[]{:S(2)}, u32[]{:S(2)}) collective-permute-start(bf16[16,64,128]{2,1,0:T(8,128)(2,1)S(1)} %constant_dynamic-slice_fusion.2), channel_id=1, source_target_pairs={{0,16},{8,24},{16,0},{24,8},{1,17},{9,25},{17,1},{25,9},{2,18},{10... | collective-permute-start | bytes 786440 | tf_op jit(solution)/shard_map/ppermute | solution.py:428
  192.0 11.3 %collective-permute-start.37 = (bf16[16,16,128]{2,1,0:T(8,128)(2,1)S(1)}, bf16[16,16,128]{2,1,0:T(8,128)(2,1)S(1)}, u32[]{:S(2)}, u32[]{:S(2)}) collective-permute-start(bf16[16,16,128]{2,1,0:T(8,128)(2,1)S(1)} %constant_dynamic-slice_fusion.1), channel_id=1, source_target_pairs={{0,17},{1,16},{2,19},{3,18},{4,21},{5,20},{6,23},{7,22},{8,25},{9,... | collective-permute-start | bytes 196616 | tf_op jit(solution)/shard_map/ppermute | solution.py:431
  192.0 12.6 %collective-permute-start.38 = (bf16[16,16,128]{2,1,0:T(8,128)(2,1)S(1)}, bf16[16,16,128]{2,1,0:T(8,128)(2,1)S(1)}, u32[]{:S(2)}, u32[]{:S(2)}) collective-permute-start(bf16[16,16,128]{2,1,0:T(8,128)(2,1)S(1)} %constant_dynamic-slice_fusion), channel_id=1, source_target_pairs={{1,18},{2,17},{3,20},{4,19},{5,22},{6,21},{9,26},{10,25},{11,28},{... | collective-permute-start | bytes 196616 | tf_op jit(solution)/shard_map/ppermute | solution.py:431
  203.3 68.0 %collective-permute-start.18 = (f32[64,64,128]{2,1,0:T(8,128)}, f32[64,64,128]{2,1,0:T(8,128)S(1)}, u32[]{:S(2)}, u32[]{:S(2)}) collective-permute-start(f32[64,64,128]{2,1,0:T(8,128)} %constant_dynamic-slice_fusion.13), channel_id=1, source_target_pairs={{0,8},{8,0},{16,24},{24,16},{1,9},{9,1},{17,25},{25,17},{2,10},{10... | collective-permute-start | bytes 6291464 | tf_op jit(solution)/shard_map/ppermute | solution.py:483
  213.2 2.0 copy-start.2
  218.5 57.1 %collective-permute-start.39 = (f16[64,64,128]{2,1,0:T(8,128)(2,1)S(1)}, f16[64,64,128]{2,1,0:T(8,128)(2,1)S(1)}, u32[]{:S(2)}, u32[]{:S(2)}) collective-permute-start(f16[64,64,128]{2,1,0:T(8,128)(2,1)S(1)} %divide_convert_fusion), channel_id=1, source_target_pairs={{0,8},{8,0},{16,24},{24,16},{1,9},{9,1},{17,25},{25,17},{2,10},{10... | collective-permute-start | bytes 3145736 | tf_op jit(solution)/shard_map/ppermute | solution.py:483
  218.8 56.8 %collective-permute-start.40 = (f32[]{:T(128)}, f32[]{:T(128)}, u32[]{:S(2)}, u32[]{:S(2)}) collective-permute-start(f32[]{:T(128)} %exp2.7), channel_id=1, source_target_pairs={{0,8},{8,0},{16,24},{24,16},{1,9},{9,1},{17,25},{25,17},{2,10},{10... | collective-permute-start | bytes 20 | tf_op jit(solution)/shard_map/ppermute | solution.py:483
  271.3 2.2 copy-start.1
  273.5 3.7 %copy-start.3 = (f32[128,64,128]{2,1,0:T(8,128)S(1)}, f32[128,64,128]{2,1,0:T(8,128)}, u32[]{:S(2)}) copy-start(f32[128,64,128]{2,1,0:T(8,128)} %copy-done.2) | copy-start | bytes 12582916

commit v2 on v1

--- a/solution.py
+++ b/solution.py
@@ -21,34 +21,51 @@
     return [pl.BlockSpec(memory_space=pltpu.VMEM) for _ in range(count)]
 
 
-def place_kernel(channel_ref, own_ref, other_ref, out_ref, sems):
-    rows = other_ref.shape[0]
+def place_own_kernel(channel_ref, both_ref, out_ref, sem):
+    rows = out_ref.shape[1]
     channel = channel_ref[0]
-    copies = [
-        pltpu.make_async_copy(own_ref.at[pl.ds(channel * rows, rows)], out_ref.at[channel], sems.at[0]),
-        pltpu.make_async_copy(other_ref, out_ref.at[1 - channel], sems.at[1]),
-    ]
-    for copy in copies:
-        copy.start()
-    for copy in copies:
-        copy.wait()
-
-
-def place_halves(channel, both_rows, other):
-    return pl.pallas_call(
-        place_kernel,
-        out_shape=jax.ShapeDtypeStruct((2,) + other.shape, other.dtype),
-        in_specs=[pl.BlockSpec(memory_space=pltpu.SMEM)] + in_vmem(2),
+    copy = pltpu.make_async_copy(
+        both_ref.at[pl.ds(pl.multiple_of(channel * rows, 8), rows)], out_ref.at[channel], sem
+    )
+    copy.start()
+    copy.wait()
+
+
+def place_other_kernel(channel_ref, other_ref, partial_ref, out_ref, sem):
+    copy = pltpu.make_async_copy(other_ref, out_ref.at[1 - channel_ref[0]], sem)
+    copy.start()
+    copy.wait()
+
+
+def place_own(channel, both_rows):
+    rows = both_rows.shape[0] // 2
+    return pl.pallas_call(
+        place_own_kernel,
+        out_shape=jax.ShapeDtypeStruct((2, rows) + both_rows.shape[1:], both_rows.dtype),
+        in_specs=[pl.BlockSpec(memory_space=pltpu.SMEM)] + in_vmem(1),
         out_specs=pl.BlockSpec(memory_space=pl.ANY),
-        scratch_shapes=[pltpu.SemaphoreType.DMA((2,))],
-        compiler_params=pltpu.CompilerParams(vmem_limit_bytes=12 << 20),
-        name="place_halves",
-    )(channel[None], both_rows, other)
-
-
-def pack_kernel(own_ref, turn_ref, block_ref, tiles_ref, *rest, base, count):
-    *based, spill_ref, seen_ref = rest
-    channels, spill = spill_ref.shape[:2]
+        scratch_shapes=[pltpu.SemaphoreType.DMA(())],
+        compiler_params=pltpu.CompilerParams(vmem_limit_bytes=8 << 20),
+        name="place_own",
+    )(channel[None], both_rows)
+
+
+def place_other(channel, other, partial):
+    return pl.pallas_call(
+        place_other_kernel,
+        out_shape=jax.ShapeDtypeStruct(partial.shape, partial.dtype),
+        in_specs=[pl.BlockSpec(memory_space=pltpu.SMEM)] + in_vmem(1) + [pl.BlockSpec(memory_space=pl.ANY)],
+        out_specs=pl.BlockSpec(memory_space=pl.ANY),
+        scratch_shapes=[pltpu.SemaphoreType.DMA(())],
+        input_output_aliases={2: 0},
+        compiler_params=pltpu.CompilerParams(vmem_limit_bytes=8 << 20),
+        name="place_other",
+    )(channel[None], other, partial)
+
+
+def pack_kernel(own_ref, channel_ref, turn_ref, block_ref, tiles_ref, *rest, base, count):
+    *based, keep_ref, flip_ref, seen_ref = rest
+    channels, spill = tiles_ref.shape[1], keep_ref.shape[0]
     blocks = seen_ref.shape[0]
     for block in range(blocks):
         seen_ref[block] = 0
@@ -70,8 +87,8 @@
 
         @pl.when(late & (spilled // spill == turn_ref[0]))
         def _():
-            for c in range(channels):
-                spill_ref[c, spilled % spill] = jnp.swapaxes(tiles_ref[t, c], 0, 1)
+            keep_ref[spilled % spill] = jnp.swapaxes(tiles_ref[t, channel_ref[0]], 0, 1)
+            flip_ref[spilled % spill] = jnp.swapaxes(tiles_ref[t, 1 - channel_ref[0]], 0, 1)
 
         return spilled + late.astype(jnp.int32)
 
@@ -82,18 +99,18 @@
     count, channels, rows, planes, nx = camera_tiles.shape
     blocks = lax.axis_size("bz")
     shape = lambda *lead: jax.ShapeDtypeStruct(lead + (planes, rows, nx), camera_tiles.dtype)
-    outs = [shape(channels, SPILL)]
+    outs = [shape(SPILL), shape(SPILL)]
     if with_base:
         outs = [shape(channels * blocks * base)] + outs
     return pl.pallas_call(
         functools.partial(pack_kernel, base=base, count=count),
         out_shape=outs,
-        in_specs=[pl.BlockSpec(memory_space=pltpu.SMEM)] * 3 + in_vmem(1),
+        in_specs=[pl.BlockSpec(memory_space=pltpu.SMEM)] * 4 + in_vmem(1),
         out_specs=in_vmem(len(outs)),
         scratch_shapes=[pltpu.SMEM((blocks,), jnp.int32)],
         compiler_params=pltpu.CompilerParams(vmem_limit_bytes=12 << 20),
         name="pack_tiles" if with_base else "pack_spill",
-    )(lax.axis_index("bz")[None], turn[None], tile_block, camera_tiles)
+    )(lax.axis_index("bz")[None], (lax.axis_index("by") % 2)[None], turn[None], tile_block, camera_tiles)
 
 
 def add_tile(planes_ref, here, start, tile):
@@ -173,21 +190,16 @@
     )(channel[None], spill_starts, *spills, planes)
 
 
-def deskew_kernel(odd_ref, backdrop_ref, band_ref, near_ref, far_ref, planes_ref, before_ref,
+def deskew_kernel(odd_ref, backdrop_ref, band_ref, near_ref, far_ref, planes_ref,
                   out_ref, cast_ref, out_a_ref, out_b_ref, all_ref, *, pitch):
     ny, nz = out_ref.shape[:2]
-    reach = before_ref.shape[0]
     ahead = SHIFT + 1
     backdrop = backdrop_ref[0]
     odd = odd_ref[0] == 1
-    for z in range(ahead + nz):
-        if z < ahead:
-            plane = before_ref[z]
-        elif z < reach:
-            plane = before_ref[z] + planes_ref[z - ahead]
-        else:
-            plane = planes_ref[z - ahead]
-        all_ref[pl.ds(z * pitch, ny), :] = plane
+    for z in range(ahead):
+        all_ref[pl.ds(z * pitch, ny), :] = jnp.zeros((ny, all_ref.shape[1]), F32)
+    for z in range(nz):
+        all_ref[pl.ds((z + ahead) * pitch, ny), :] = planes_ref[z]
 
     def row(y, carry):
         first = (ahead - band_ref[y]) * pitch + y
@@ -204,7 +216,33 @@
     lax.fori_loop(0, ny, row, 0, unroll=4)
 
 
-def deskew(backdrop, band, near, far, planes, before):
+def deskew_more_kernel(odd_ref, backdrop_ref, band_ref, near_ref, far_ref, before_ref,
+                       value_ref, cast_in_ref, a_ref, b_ref, out_ref, cast_ref, out_a_ref, out_b_ref, all_ref, *, pitch):
+    ny = value_ref.shape[0]
+    reach = before_ref.shape[0]
+    ahead = SHIFT + 1
+    backdrop = backdrop_ref[0]
+    odd = odd_ref[0] == 1
+    for z in range(ahead + HALO):
+        plane = before_ref[z] if z < reach else jnp.zeros(before_ref.shape[1:], F32)
+        all_ref[pl.ds(z * pitch, ny), :] = plane
+
+    def row(y, carry):
+        first = (ahead - band_ref[y]) * pitch + y
+        value = near_ref[y] * all_ref[pl.ds(first, HALO, stride=pitch), :]
+        value = value + far_ref[y] * all_ref[pl.ds(first - pitch, HALO, stride=pitch), :]
+        value = value + value_ref[y, :HALO]
+        out_ref[y, :HALO] = value
+        cast = (value + backdrop).astype(BF16)
+        cast_ref[y, :HALO] = cast
+        out_a_ref[y] = jnp.where(odd, cast, a_ref[y])
+        out_b_ref[y] = jnp.where(odd, b_ref[y], cast)
+        return carry
+
+    lax.fori_loop(0, ny, row, 0, unroll=8)
+
+
+def deskew(backdrop, band, near, far, planes):
     ny, nx = planes.shape[1:]
     pitch = ny + 8
     smem = [pl.BlockSpec(memory_space=pltpu.SMEM)] * 5
@@ -216,12 +254,29 @@
             jax.ShapeDtypeStruct((ny, HALO, nx), BF16),
             jax.ShapeDtypeStruct((ny, HALO, nx), BF16),
         ],
-        in_specs=smem + in_vmem(2),
+        in_specs=smem + in_vmem(1),
         out_specs=in_vmem(4),
         scratch_shapes=[pltpu.VMEM(((Z_DEV + SHIFT + 1) * pitch, nx), F32)],
         compiler_params=pltpu.CompilerParams(vmem_limit_bytes=24 << 20),
+        cost_estimate=pl.CostEstimate(flops=5_000_000_000, transcendentals=0, bytes_accessed=12_000_000),
         name="deskew",
-    )(odd_block(), backdrop, band, near, far, planes, before)
+    )(odd_block(), backdrop, band, near, far, planes)
+
+
+def deskew_more(backdrop, band, near, far, before, parts):
+    ny, nx = before.shape[1:]
+    pitch = ny + 8
+    smem = [pl.BlockSpec(memory_space=pltpu.SMEM)] * 5
+    return pl.pallas_call(
+        functools.partial(deskew_more_kernel, pitch=pitch),
+        out_shape=[jax.ShapeDtypeStruct(part.shape, part.dtype) for part in parts],
+        in_specs=smem + in_vmem(5),
+        out_specs=in_vmem(4),
+        scratch_shapes=[pltpu.VMEM(((HALO + SHIFT + 1) * pitch, nx), F32)],
+        input_output_aliases={6 + i: i for i in range(4)},
+        compiler_params=pltpu.CompilerParams(vmem_limit_bytes=16 << 20),
+        name="deskew_more",
+    )(odd_block(), backdrop, band, near, far, before, *parts)
 
 
 def pair_lanes(x, index, height):
@@ -235,21 +290,23 @@
     return jnp.dot(jnp.concatenate([stack, stack], axis=1), mx, preferred_element_type=F32).astype(BF16)
 
 
-def three_terms(column):
+def terms_of(column, coarse):
     head = column.astype(BF16)
+    if coarse:
+        return jnp.concatenate([head, head], axis=0)
     tail = (column - head.astype(F32)).astype(BF16)
     return jnp.concatenate([head, tail, head], axis=0)
 
 
-def inner_kernel(own_ref, mx_ref, mz_ref, my_ref, out_ref, mid_ref):
+def inner_kernel(own_ref, mx_ref, mz_ref, my_ref, out_ref, mid_ref, *, coarse):
     ny, nz, lanes = own_ref.shape
-    mx, mz, my = mx_ref[...], mz_ref[...], my_ref[...]
     pitch = nz + 8
     group = 16
     ahead = 8
 
     def planes(g, carry):
-        alongx = blur_x([own_ref[g * group + k] for k in range(group)], mx)
+        mz = mz_ref[...]
+        alongx = blur_x([own_ref[g * group + k] for k in range(group)], mx_ref[...])
         for k in range(0, group, 4):
             first, second = pair_lanes(alongx, k, nz), pair_lanes(alongx, k + 2, nz)
             both = jnp.dot(
@@ -265,9 +322,10 @@
     lax.fori_loop(0, ny // group, planes, 0)
 
     def columns(g, carry):
+        my = my_ref[:, ny:] if coarse else my_ref[...]
         for k in range(ahead):
             z = (g * ahead + k) * 2
-            terms = [three_terms(mid_ref[pl.ds(z + i, ny, stride=pitch), :]) for i in range(2)]
+            terms = [terms_of(mid_ref[pl.ds(z + i, ny, stride=pitch), :], coarse) for i in range(2)]
             both = jnp.dot(my, jnp.concatenate(terms, axis=1), preferred_element_type=F32)
             out_ref[pl.ds(z, ny, stride=pitch), :] = both[:, :lanes]
             out_ref[pl.ds(z + 1, ny, stride=pitch), :] = both[:, lanes:]
@@ -283,8 +341,7 @@
     else:
         full_ref, peak_ref, cast_ref, out_a_ref, out_b_ref, edge_ref, rim_ref, more_ref = rest
     nside = side_ref.shape[0]
-    mx, mze, mzs, mye, mys = mx_ref[...], mze_ref[...], mzs_ref[...], mye_ref[...], mys_ref[...]
-    lanes = mx.shape[1]
+    lanes = mx_ref.shape[1]
     pitch = nz + 8
     faces = 2 * HALO
     edge_pitch = faces + 8
@@ -295,7 +352,8 @@
         pieces = []
         for k in range(group):
             pieces += [a_ref[g * group + k], b_ref[g * group + k]]
-        alongx = blur_x(pieces, mx)
+        mze = mze_ref[...]
+        alongx = blur_x(pieces, mx_ref[...])
         for k in range(0, group, 8):
             pairs = []
             for p in range(4):
@@ -314,10 +372,10 @@
         for k in range(group):
             y = g * group + k
             pieces += [side_a_ref[y], side_ref[y], side_b_ref[y]]
-        alongx = blur_x(pieces, mx)
+        alongx = blur_x(pieces, mx_ref[...])
         for k in range(0, group, 2):
             pair = pair_lanes(alongx, k, width)
-            both = jnp.dot(mzs, jnp.concatenate([pair, pair], axis=0), preferred_element_type=F32)
+            both = jnp.dot(mzs_ref[...], jnp.concatenate([pair, pair], axis=0), preferred_element_type=F32)
             row = (g * group + k) * pitch
             rim_ref[pl.ds(row, nz), :] = both[:, :lanes]
             rim_ref[pl.ds(row + pitch, nz), :] = both[:, lanes:]
@@ -329,12 +387,16 @@
         if z < HALO or z >= nz - HALO:
             e = z if z < HALO else z - nz + faces
             terms = [
-                three_terms(jnp.concatenate([edge_ref[pl.ds(e + i, ny, stride=edge_pitch), :], rim(z + i)], axis=0))
+                terms_of(
+                    jnp.concatenate([edge_ref[pl.ds(e + i, ny, stride=edge_pitch), :], rim(z + i)], axis=0), quotient
+                )
                 for i in range(2)
             ]
+            mye = mye_ref[:, ny + nside:] if quotient else mye_ref[...]
             both = jnp.dot(mye, jnp.concatenate(terms, axis=1), preferred_element_type=F32)
         else:
-            terms = [three_terms(rim(z + i)) for i in range(2)]
+            terms = [terms_of(rim(z + i), quotient) for i in range(2)]
+            mys = mys_ref[:, nside:] if quotient else mys_ref[...]
             both = jnp.dot(mys, jnp.concatenate(terms, axis=1), preferred_element_type=F32)
         more_ref[pl.ds(z, ny, stride=pitch), :] = both[:, :lanes]
         more_ref[pl.ds(z + 1, ny, stride=pitch), :] = both[:, lanes:]
@@ -363,10 +425,10 @@
         peak_ref[...] = peak
 
 
-def blur_inner(block, matrices):
+def blur_inner(coarse, block, matrices):
     ny, nz, nx = block.shape
     return pl.pallas_call(
-        inner_kernel,
+        functools.partial(inner_kernel, coarse=coarse),
         out_shape=jax.ShapeDtypeStruct((ny * (nz + 8), nx), F32),
         in_specs=in_vmem(4),
         out_specs=in_vmem(1)[0],
@@ -434,72 +496,152 @@
     return *across, join(sides), *[join(found) for found in corners]
 
 
-def head_tail(matrix):
-    head = lax.reduce_precision(matrix, 8, 7)
-    return head.astype(BF16), (matrix - head).astype(BF16)
-
-
-def band(taps, out_place, in_place):
-    count = taps.shape[0]
-    offset = in_place[None, :] - out_place[:, None] + count // 2
-    matches = (offset[:, :, None] == jnp.arange(count)[None, None, :]).astype(F32)
-    return jnp.einsum("ijw,cw->cij", matches, jnp.stack([taps, taps[::-1]]), precision=lax.Precision.HIGHEST)
-
-
-def band_matrices(taps, ny, nz, nx):
-    near = jnp.arange(HALO)
-    odd_y = (lax.axis_index("by") // 2) % 2 == 1
-    odd_z = lax.axis_index("bz") % 2 == 1
-    sides = [jnp.where(odd_y, near - HALO, near + ny), jnp.where(odd_y, near + ny, near - HALO)]
-    sides = sides[: len(partners(lax.axis_size("by") // 2))]
-    face_a = jnp.where(odd_z, near - HALO, near + nz)
-    face_b = jnp.where(odd_z, near + nz, near - HALO)
-    along, depth, height = jnp.arange(nx), jnp.arange(nz), jnp.arange(ny)
-    side = jnp.concatenate(sides)
-    edge = jnp.concatenate([near, near + nz - HALO])
-    face = jnp.concatenate([face_a, face_b])
-
-    def spread(matrix, count):
-        eye = jnp.eye(count, dtype=matrix.dtype)[None, :, None, :, None]
-        blocks = eye * matrix[:, None, :, None, :]
-        return blocks.reshape(2, count * matrix.shape[1], count * matrix.shape[2])
-
-    mx = jnp.concatenate(head_tail(band(taps[2], along, along)[::-1]), axis=1)
-    mz = spread(jnp.concatenate(head_tail(band(taps[1], depth, depth)), axis=2), 2)
-    mze = spread(jnp.concatenate(head_tail(band(taps[1], edge, face)), axis=2), 4)
-    mzs = jnp.concatenate(
-        head_tail(band(taps[1], depth, jnp.concatenate([face_a, depth, face_b]))), axis=2
-    )
-
-    def three(columns):
-        head, tail = head_tail(band(taps[0], height, columns))
-        return jnp.concatenate([head, head, tail], axis=2)
-
-    my, mye, mys = three(height), three(jnp.concatenate([height, side])), three(side)
-    return [((mx[i], mz[i], my[i]), (mx[i], mze[i], mzs[i], mye[i], mys[i])) for i in range(2)]
+def cut(index, size, count):
+    block = jnp.zeros(index.shape, jnp.int32)
+    for k in range(1, count):
+        block = block + (index >= k * size).astype(jnp.int32)
+    return block, index - block * size
+
+
+def matrix_kernel(place_ref, taps_ref, *refs, nx, ny, nz, sides):
+    count = taps_ref.shape[0] // 3
+    odd_y, odd_z = place_ref[0] == 1, place_ref[1] == 1
+    face_a = jnp.where(odd_z, -HALO, nz)
+    face_b = jnp.where(odd_z, nz, -HALO)
+    side_places = [jnp.where(odd_y, -HALO, ny), jnp.where(odd_y, ny, -HALO)][:sides]
+
+    def fill(ref, axis, reverse, places):
+        row = lax.broadcasted_iota(jnp.int32, ref.shape, 0)
+        lane = lax.broadcasted_iota(jnp.int32, ref.shape, 1)
+        offset, tail, kept = places(row, lane)
+        offset = offset + count // 2
+        matrix = jnp.zeros(ref.shape, F32)
+        for t in range(count):
+            tap = taps_ref[axis * count + (count - 1 - t if reverse else t)]
+            matrix = jnp.where(offset == t, tap, matrix)
+        if kept is not None:
+            matrix = jnp.where(kept, matrix, 0.0)
+        head = matrix.astype(BF16).astype(F32)
+        ref[...] = jnp.where(tail, matrix - head, head).astype(BF16)
+
+    def along_x(row, lane):
+        part, source = cut(row, nx, 2)
+        return source - lane, part == 1, None
+
+    def along_z(row, lane):
+        block, out = cut(row, nz, 2)
+        lane_block, rest = cut(lane, 2 * nz, 2)
+        part, source = cut(rest, nz, 2)
+        return source - out, part == 1, block == lane_block
+
+    def face_place(face):
+        return jnp.where(face < HALO, face + face_a, face - HALO + face_b)
+
+    def along_edges(row, lane):
+        faces = 2 * HALO
+        block, edge = cut(row, faces, 4)
+        lane_block, rest = cut(lane, 2 * faces, 4)
+        part, face = cut(rest, faces, 2)
+        out = jnp.where(edge < HALO, edge, edge - faces + nz)
+        return face_place(face) - out, part == 1, block == lane_block
+
+    def along_rim(row, lane):
+        part, column = cut(lane, nz + 2 * HALO, 2)
+        source = jnp.where(
+            column < HALO,
+            column + face_a,
+            jnp.where(column < HALO + nz, column - HALO, column - HALO - nz + face_b),
+        )
+        return source - row, part == 1, None
+
+    def side_place(column):
+        place = column + side_places[0]
+        for k in range(1, sides):
+            place = jnp.where(column >= k * HALO, column - k * HALO + side_places[k], place)
+        return place
+
+    def along_y(row, lane):
+        part, column = cut(lane, ny, 3)
+        return column - row, part == 2, None
+
+    def along_y_edges(row, lane):
+        part, column = cut(lane, ny + sides * HALO, 3)
+        source = jnp.where(column < ny, column, side_place(column - ny))
+        return source - row, part == 2, None
+
+    def along_y_sides(row, lane):
+        part, column = cut(lane, sides * HALO, 3)
+        return side_place(column) - row, part == 2, None
+
+    plan = ((2, along_x), (1, along_z), (0, along_y), (1, along_edges), (1, along_rim),
+            (0, along_y_edges), (0, along_y_sides))
+    for index, (axis, places) in enumerate(plan):
+        for turn in range(2):
+            fill(refs[turn * len(plan) + index], axis, turn == 1, places)
+
+
+def band_matrices(kernels, ny, nz, nx):
+    place = jnp.stack([(lax.axis_index("by") // 2) % 2, lax.axis_index("bz") % 2])
+    sides = len(partners(lax.axis_size("by") // 2))
+    shapes = [
+        (2 * nx, nx),
+        (2 * nz, 4 * nz),
+        (ny, 3 * ny),
+        (8 * HALO, 16 * HALO),
+        (nz, 2 * (nz + 2 * HALO)),
+        (ny, 3 * (ny + sides * HALO)),
+        (ny, 3 * sides * HALO),
+    ]
+    found = pl.pallas_call(
+        functools.partial(matrix_kernel, nx=nx, ny=ny, nz=nz, sides=sides),
+        out_shape=[jax.ShapeDtypeStruct(shape, BF16) for shape in shapes * 2],
+        in_specs=[pl.BlockSpec(memory_space=pltpu.SMEM)] * 2,
+        out_specs=in_vmem(2 * len(shapes)),
+        compiler_params=pltpu.CompilerParams(vmem_limit_bytes=8 << 20),
+        name="band_matrices",
+    )(place, kernels.reshape(-1))
+    turns = [found[: len(shapes)], found[len(shapes):]]
+    return [((mx, mz, my), (mx, mze, mzs, mye, mys)) for mx, mz, my, mze, mzs, mye, mys in turns]
 
 
 def swap_pair(x):
     return lax.ppermute(x, "by", [(i, i ^ 1) for i in range(lax.axis_size("by"))])
+
+
+def stack_kernel(*refs):
+    *parts, out_ref = refs
+    for i, part in enumerate(parts):
+        out_ref[i] = part[...]
+
+
+def stack_parts(parts):
+    return pl.pallas_call(
+        stack_kernel,
+        out_shape=jax.ShapeDtypeStruct((len(parts),) + parts[0].shape, parts[0].dtype),
+        in_specs=in_vmem(len(parts)),
+        out_specs=in_vmem(1)[0],
+        compiler_params=pltpu.CompilerParams(vmem_limit_bytes=12 << 20),
+        name="stack_parts",
+    )(*parts)
 
 
 def share_spill(spill):
     blocks = lax.axis_size("bz")
     wide = lax.axis_size("by")
-    channel = lax.axis_index("by") % 2
     found = []
     for m in range(0, blocks, 2):
         for flip in range(2):
-            piece = lax.dynamic_index_in_dim(spill, channel ^ flip, 0, keepdims=False)
+            piece = spill[flip]
             if m or flip:
                 pairs = [(b * blocks + z, (b ^ flip) * blocks + (z ^ m)) for b in range(wide) for z in range(blocks)]
                 piece = lax.ppermute(piece, ("by", "bz"), pairs)
             found.append(piece)
-    line = jnp.stack(found).reshape((blocks // 2, 2) + spill.shape[1:])
+    line = stack_parts(found)
+    line = line.reshape((blocks // 2, 2) + line.shape[1:])
     return line, lax.ppermute(line, "bz", [(z, z ^ 1) for z in range(blocks)])
 
 
-def route_tiles(camera_tiles, tile_block, tile_offset):
+def route_tiles(camera_tiles, tile_block, tile_offset, prepared):
     count = camera_tiles.shape[0]
     blocks = lax.axis_size("bz")
     wide = lax.axis_size("by")
@@ -507,7 +649,7 @@
     own = lax.axis_index("bz")
     channel = lax.axis_index("by") % 2
     named = tile_block[:, 0]
-    outgoing, spill = pack_tiles(camera_tiles, named, jnp.int32(0), base, True)
+    outgoing, *spill = pack_tiles(camera_tiles, named, jnp.int32(0), base, True)
     groups = [
         [(2 * j + c) * blocks + z for c in range(2) for z in range(blocks)] for j in range(wide // 2)
     ]
@@ -533,11 +675,12 @@
     turns = (jnp.max(jnp.sum(late.astype(jnp.int32), axis=1)) + SPILL - 1) // SPILL
     spills = share_spill(spill)
     arrived = arrived.reshape((2, blocks * base) + arrived.shape[2:])
+    starts, prepared = lax.optimization_barrier((starts, prepared))
     planes, tail = gather_planes(channel, starts, spill_starts(0), arrived, spills)
 
     def turn_step(carry):
         turn, planes, tail = carry
-        again = pack_tiles(camera_tiles, named, turn, base, False)[0]
+        again = pack_tiles(camera_tiles, named, turn, base, False)
         planes, tail = more_planes(channel, spill_starts(turn), share_spill(again), planes, tail)
         return turn + 1, planes, tail
 
@@ -548,7 +691,7 @@
         planes,
         tail,
     )
-    return planes, tail
+    return planes, tail, prepared
 
 
 def pair_stack(first_is_own, own, other):
@@ -568,11 +711,15 @@
     forward, backward = band_matrices(kernels, 2 * rows, Z_DEV, nx)
     backdrop = lax.dynamic_slice_in_dim(background, channel, 1, 0)
 
-    planes, over = route_tiles(camera_tiles, tile_block, tile_offset)
+    table = table.reshape(2 * rows, 3)
+    table = (table[:, 0].astype(jnp.int32), table[:, 1], table[:, 2])
+    planes, over, (forward, backward, backdrop, table) = route_tiles(
+        camera_tiles, tile_block, tile_offset, (forward, backward, backdrop, table)
+    )
     blocks = lax.axis_size("bz")
-    before = lax.ppermute(over, "bz", [(i, i + 1) for i in range(blocks - 1)])
-    table = table.reshape(2 * rows, 3)
-    deskewed, *field = deskew(backdrop, table[:, 0].astype(jnp.int32), table[:, 1], table[:, 2], planes, before)
+    before = lax.ppermute(over.astype(jnp.float16), "bz", [(i, i + 1) for i in range(blocks - 1)])
+    parts = deskew(backdrop, *table, planes)
+    deskewed, *field = deskew_more(backdrop, *table, before.astype(F32), parts)
 
     half = lambda x, start: lax.dynamic_slice_in_dim(x, start, rows, 0)
     other_start = (1 - channel) * rows
@@ -581,19 +728,23 @@
     estimate = deskewed
     for iteration in range(ITERS):
         halos = halo_exchange(field)
-        inner = blur_inner(field[0], forward[0])
+        inner = blur_inner(True, field[0], forward[0])
         field = blur_outer(True, False, backdrop, inner, halos, forward[1], deskewed)
         halos = halo_exchange(field)
-        inner = blur_inner(field[0], backward[0])
+        inner = blur_inner(False, field[0], backward[0])
         estimate, peak, *field = blur_outer(
             False, iteration == 0, backdrop, inner, halos, backward[1], estimate
         )
-    deskewed_out = place_halves(channel, deskewed, deskewed_other)
-
     theirs = half(estimate, other_start)
-    scale = jnp.exp2(jnp.floor(jnp.log2(jnp.max(peak))) - 13.0)
-    got = swap_pair((theirs / scale).astype(jnp.float16)).astype(F32) * swap_pair(scale)
-    return deskewed_out, place_halves(channel, estimate, got)
+    power = jnp.floor(jnp.log2(jnp.max(peak))) - 13.0
+    message = jnp.concatenate(
+        [theirs * jnp.exp2(-power), jnp.full((1,) + theirs.shape[1:], power)], axis=0
+    ).astype(jnp.float16)
+    got = swap_pair(message)
+    deskewed_out = place_other(channel, deskewed_other, place_own(channel, deskewed))
+    partial = place_own(channel, estimate)
+    received = got[:rows].astype(F32) * jnp.exp2(got[rows, 0, 0].astype(F32))
+    return deskewed_out, place_other(channel, received, partial)
 
 
 def solution(mesh):

time: 280 us -> 279 us (level)
  starting transfers between devices: 126 us -> 63.3 us
  waiting for transfers between devices: 40.4 us -> 96.2 us
  Pallas kernels: 74.7 us -> 81.9 us
  local copies, waits for them, and re-layouts: 16.8 us -> 22.9 us
  matrix products: 4.62 us -> 0 us
  other arithmetic: 13.6 us -> 10.2 us
    ppermute x4 -> x3, starting transfers between devices: 55.5 us -> 2.76 us  [swap_pair(): lax.ppermute(x, 'by', [(i, i ^ 1) for i in range(lax.axis_size('by'))])]
    ppermute x4 -> x3, waiting for transfers between devices: 0.01 us -> 47.2 us  [swap_pair(): lax.ppermute(x, 'by', [(i, i ^ 1) for i in range(lax.axis_size('by'))])]
    ppermute x7, waiting for transfers between devices: 29.9 us -> 49 us  [share_spill(): piece = lax.ppermute(piece, ('by', 'bz'), pairs)]
    ppermute x1, starting transfers between devices: 16.3 us -> 5.83 us  [shards(): lax.ppermute(over.astype(jnp.float16), 'bz', [(i, i + 1) for i in range(b...]
    ppermute x1, waiting for transfers between devices: 8.42 us -> 0.01 us  [shards(): lax.ppermute(over.astype(jnp.float16), 'bz', [(i, i + 1) for i in range(b...]
    pallas_call x6 -> x11, Pallas kernels: 30.7 us -> 38.2 us  [the longest x4 25.3 us: blur_inner(): pl.pallas_call(functools.partial(inner_kernel, coarse=coarse), out_shape=...]
    unnamed x35 -> x83, local copies, waits for them, and re-layouts: 9.86 us -> 16.9 us
    dot_general x7 -> x0, matrix products: 4.62 us -> none  [band(): jnp.einsum('ijw,cw->cij', matches, jnp.stack([taps, taps[::-1]]), precisi...]
  transfers between devices with their start and end apart: 34 -> 33, of which waited for: 4 -> 6; matrix products, arithmetic and copies ran while one was open for 10% -> 5% of each run, Pallas kernels for 13% -> 18%
where the time goes in v2:
time: 279 us; the launch traced here: 278 us
  waiting for transfers between devices  96.2 us (34%)
  Pallas kernels  81.9 us (29%)
  starting transfers between devices  63.3 us (23%)
  local copies, waits for them, and re-layouts  22.9 us (8%)
  other arithmetic  10.2 us (4%)
  between operations  3.72 us (1%)
    ppermute x7, waiting for transfers between devices, share_spill(): piece = lax.ppermute(piece, ('by', 'bz'), pairs)  49 us
    ppermute x3, waiting for transfers between devices, swap_pair(): lax.ppermute(x, 'by', [(i, i ^ 1) for i in range(lax.axis_size('by'))])  47.2 us
    pallas_call x4, Pallas kernels, blur_outer(): pl.pallas_call(functools.partial(outer_kernel, quotient=quotient, first=f...  30.3 us
    pallas_call x4, Pallas kernels, blur_inner(): pl.pallas_call(functools.partial(inner_kernel, coarse=coarse), out_shape=...  25.3 us
    ppermute x8, starting transfers between devices, halo_exchange(): lax.ppermute(lax.dynamic_slice_in_dim(face, start, HALO, 0), ('by', 'bz')...  18.3 us
    unnamed x83, local copies, waits for them, and re-layouts  16.9 us
    ppermute x8, starting transfers between devices, halo_exchange(): lax.ppermute(face, 'bz', pairs)  12.2 us
    ppermute x7, starting transfers between devices, share_spill(): piece = lax.ppermute(piece, ('by', 'bz'), pairs)  11 us
  transfers between devices with their start and end apart: 33, of which 6 were waited for; matrix products, arithmetic and copies ran while one was open for 5% of the time, Pallas kernels for 18%

profile of v2, /device:TPU:1, one launch (start us, length us, event | category | flops | bytes accessed | tf_op | source)
XLA Modules:
  0.0 278.2 jit_solution(10250853646179045151)
XLA Ops:
  0.6 3.3 %pack_tiles.1 = (bf16[32,4,64,128]{3,2,1,0:T(8,128)(2,1)S(1)}, bf16[2,4,64,128]{3,2,1,0:T(8,128)(2,1)S(1)}, bf16[2,4,64,128]{3,2,1,0:T(8,128)(2,1)S(1)}) custom-call(s32[1]{0:T(128)} %bitcast.16.own_ref, s32[1]{0:T(128)} %bitcast.7.channel_ref, s32[1]{0:T(128)} %constant.158.clone.1.turn_ref, s32[128]{0:T(128)} %bitcast.51, ...), custom_call_target="tpu_custom_call" | custom-call | tf_op jit(solution)/shard_map/pack_tiles/pallas_call | solution.py:105
  4.0 1.3 copy-done.4
  5.3 7.5 %all-to-all-start = ((bf16[16,2,4,64,128]{4,3,2,1,0:T(8,128)(2,1)}), bf16[16,2,4,64,128]{4,3,2,1,0:T(8,128)(2,1)S(1)}, u32[]{:S(2)}, u32[]{:S(2)}) async-start(bf16[16,2,4,64,128]{4,3,2,1,0:T(8,128)(2,1)} %bitcast.49), calls=%async_computation | async-start | bytes 4194304 | tf_op jit(solution)/shard_map/all_to_all | solution.py:656
  12.7 1.4 collective-permute-start.10
  14.1 2.1 collective-permute-start.12
  17.5 3.2 %collective-permute-start.14 = (bf16[2,4,64,128]{3,2,1,0:T(8,128)(2,1)S(1)}, bf16[2,4,64,128]{3,2,1,0:T(8,128)(2,1)S(1)}, u32[]{:S(2)}, u32[]{:S(2)}) collective-permute-start(bf16[2,4,64,128]{3,2,1,0:T(8,128)(2,1)S(1)} %get-tuple-element.280.refs_0_), channel_id=1, source_target_pairs={{0,6},{1,7},{2,4},{3,5},{4,2},{5,3},{6,0},{7,1},{8,14},{9,15},{10,... | collective-permute-start | bytes 393224 | tf_op jit(solution)/shard_map/ppermute | solution.py:637
  24.0 26.7 %collective-permute-done.10.refs_2_ = bf16[2,4,64,128]{3,2,1,0:T(8,128)(2,1)S(1)} collective-permute-done((bf16[2,4,64,128]{3,2,1,0:T(8,128)(2,1)S(1)}, bf16[2,4,64,128]{3,2,1,0:T(8,128)(2,1)S(1)}, u32[]{:S(2)}, u32[]{:S(2)}) %collective-permute-start.10) | collective-permute-done | bytes 131104 | tf_op jit(solution)/shard_map/ppermute | solution.py:637
  50.7 3.0 %collective-permute-start.15 = (bf16[2,4,64,128]{3,2,1,0:T(8,128)(2,1)S(1)}, bf16[2,4,64,128]{3,2,1,0:T(8,128)(2,1)S(1)}, u32[]{:S(2)}, u32[]{:S(2)}) collective-permute-start(bf16[2,4,64,128]{3,2,1,0:T(8,128)(2,1)S(1)} %get-tuple-element.281), channel_id=1, source_target_pairs={{0,14},{1,15},{2,12},{3,13},{4,10},{5,11},{6,8},{7,9},{8,6},{9,7},... | collective-permute-start | bytes 393224 | tf_op jit(solution)/shard_map/ppermute | solution.py:637
  53.7 3.0 %collective-permute-done.11.refs_3_ = bf16[2,4,64,128]{3,2,1,0:T(8,128)(2,1)S(1)} collective-permute-done((bf16[2,4,64,128]{3,2,1,0:T(8,128)(2,1)S(1)}, bf16[2,4,64,128]{3,2,1,0:T(8,128)(2,1)S(1)}, u32[]{:S(2)}, u32[]{:S(2)}) %collective-permute-start.11) | collective-permute-done | bytes 131104 | tf_op jit(solution)/shard_map/ppermute | solution.py:637
  58.1 16.7 %collective-permute-done.12.refs_4_ = bf16[2,4,64,128]{3,2,1,0:T(8,128)(2,1)S(1)} collective-permute-done((bf16[2,4,64,128]{3,2,1,0:T(8,128)(2,1)S(1)}, bf16[2,4,64,128]{3,2,1,0:T(8,128)(2,1)S(1)}, u32[]{:S(2)}, u32[]{:S(2)}) %collective-permute-start.12) | collective-permute-done | bytes 131104 | tf_op jit(solution)/shard_map/ppermute | solution.py:637
  76.0 2.5 collective-permute-done.13.refs_5_
  82.7 1.6 collective-permute-start.16
  87.3 1.3 dynamic_slice.50.backdrop_ref
  90.1 5.1 %band_matrices.1 = (bf16[256,128]{1,0:T(8,128)(2,1)S(1)}, bf16[128,256]{1,0:T(8,128)(2,1)S(1)}, bf16[128,384]{1,0:T(8,128)(2,1)S(1)}, bf16[128,256]{1,0:T(8,128)...) custom-call(s32[2]{0:T(128)S(1)} %pad_add_fusion.place_ref, ...), custom_call_target="tpu_custom_call" | custom-call | tf_op jit(solution)/shard_map/band_matrices/pallas_call | solution.py:595
  102.8 4.6 %gather_planes.1 = (f32[67,128,128]{2,1,0:T(8,128)}, f32[12,128,128]{2,1,0:T(8,128)}) custom-call(s32[1]{0:T(128)} %bitcast.7.channel_ref, s32[16]{0:T(128)S(1)} %sub.32.starts_ref, s32[16]{0:T(128)S(1)} %reshape.105.spill_starts_ref, bf16[2,16,4,64,128]{4,3,2,1,0:T(8,128)(2,1)S(1)} %bitcast.46, bf16[4,2,2,4,64,128]{5,4,3,2,1,0:T(8,128)(2,1)S(1)} %bitcast.48, ...), custom_call_target="tpu_custom_call" | custom-call | tf_op jit(solution)/shard_map/gather_planes/pallas_call | solution.py:163
  108.6 5.8 %collective-permute-start.17 = (f16[12,128,128]{2,1,0:T(8,128)(2,1)S(1)}, f16[12,128,128]{2,1,0:T(8,128)(2,1)S(1)}, u32[]{:S(2)}, u32[]{:S(2)}) collective-permute-start(f16[12,128,128]{2,1,0:T(8,128)(2,1)S(1)} %convert_element_type.46), channel_id=1, source_target_pairs={{0,1},{1,2},{2,3},{3,4},{4,5},{5,6},{6,7},{8,9},{9,10},{10,11},{11... | collective-permute-start | bytes 1179656 | tf_op jit(solution)/shard_map/ppermute | solution.py:720
  114.4 5.5 %deskew.1 = (f32[128,64,128]{2,1,0:T(8,128)S(1)}, bf16[128,64,128]{2,1,0:T(8,128)(2,1)S(1)}, bf16[128,16,128]{2,1,0:T(8,128)(2,1)S(1)}, bf16[128,16,128]{2,1,0:T(8,128)(2,1)S(1)}) custom-call(s32[1]{0:T(128)} %bitcast.8.odd_ref, f32[1]{0:T(128)} %dynamic_slice.50.backdrop_ref, s32[128]{0:T(128)S(1)} %get-tuple-element.275.band_ref, ...), custom_call_target="tpu_custom_call" | custom-call | flops 5000000000 | bytes 12000000 | tf_op jit(solution)/shard_map/deskew/pallas_call | solution.py:249
  120.1 2.4 deskew_more.1
  122.5 4.9 %collective-permute-start.20 = (bf16[128,16,128]{2,1,0:T(8,128)(2,1)S(1)}, bf16[128,16,128]{2,1,0:T(8,128)(2,1)S(1)}, u32[]{:S(2)}, u32[]{:S(2)}) collective-permute-start(bf16[128,16,128]{2,1,0:T(8,128)(2,1)S(1)} %get-tuple-element.296), channel_id=1, source_target_pairs={{1,2},{2,1},{3,4},{4,3},{5,6},{6,5},{9,10},{10,9},{11,12},{12,11},... | collective-permute-start | bytes 1572872 | tf_op jit(solution)/shard_map/ppermute | solution.py:494
  127.5 1.3 collective-permute-start.21
  128.8 4.8 %collective-permute-start.23 = (bf16[16,16,128]{2,1,0:T(8,128)(2,1)S(1)}, bf16[16,16,128]{2,1,0:T(8,128)(2,1)S(1)}, u32[]{:S(2)}, u32[]{:S(2)}) collective-permute-start(bf16[16,16,128]{2,1,0:T(8,128)(2,1)S(1)} %constant_dynamic-slice_fusion.9), channel_id=1, source_target_pairs={{1,18},{2,17},{3,20},{4,19},{5,22},{6,21},{9,26},{10,25},{11,28},{... | collective-permute-start | bytes 196616 | tf_op jit(solution)/shard_map/ppermute | solution.py:493
  133.7 5.9 %blur_inner.4.inner_ref = f32[9216,128]{1,0:T(8,128)S(1)} custom-call(bf16[128,64,128]{2,1,0:T(8,128)(2,1)S(1)} %get-tuple-element.291.own_ref, bf16[256,128]{1,0:T(8,128)(2,1)S(1)} %copy-done.20, bf16[128,256]{1,0:T(8,128)(2,1)S(1)} %copy-done.24, bf16[128,384]{1,0:T(8,128)(2,1)S(1)} %copy-done.12), custom_call_target="tpu_custom_call" | custom-call | flops 20000000000 | bytes 8000000 | tf_op jit(solution)/shard_map/blur_inner/pallas_call | solution.py:430
  139.7 1.6 constant_dynamic-slice_fusion.12
  141.4 7.0 %blur_quotient.2 = (bf16[128,64,128]{2,1,0:T(8,128)(2,1)S(1)}, bf16[128,16,128]{2,1,0:T(8,128)(2,1)S(1)}, bf16[128,16,128]{2,1,0:T(8,128)(2,1)S(1)}) custom-call(s32[1]{0:T(128)} %bitcast.8.odd_ref, f32[1]{0:T(128)} %dynamic_slice.50.backdrop_ref, f32[9216,128]{1,0:T(8,128)S(1)} %blur_inner.4.inner_ref, ...), custom_call_target="tpu_custom_call" | custom-call | flops 10000000000 | bytes 16000000 | tf_op jit(solution)/shard_map/blur_quotient/pallas_call | solution.py:452
  148.4 2.4 collective-permute-start.25
  151.4 4.7 %collective-permute-start.28 = (bf16[16,16,128]{2,1,0:T(8,128)(2,1)S(1)}, bf16[16,16,128]{2,1,0:T(8,128)(2,1)S(1)}, u32[]{:S(2)}, u32[]{:S(2)}) collective-permute-start(bf16[16,16,128]{2,1,0:T(8,128)(2,1)S(1)} %constant_dynamic-slice_fusion.6), channel_id=1, source_target_pairs={{1,18},{2,17},{3,20},{4,19},{5,22},{6,21},{9,26},{10,25},{11,28},{... | collective-permute-start | bytes 196616 | tf_op jit(solution)/shard_map/ppermute | solution.py:493
  156.1 6.7 %blur_inner.5.inner_ref = f32[9216,128]{1,0:T(8,128)S(1)} custom-call(bf16[128,64,128]{2,1,0:T(8,128)(2,1)S(1)} %get-tuple-element.302.own_ref, bf16[256,128]{1,0:T(8,128)(2,1)S(1)} %copy-done.14, bf16[128,256]{1,0:T(8,128)(2,1)S(1)} %copy-done.18, bf16[128,384]{1,0:T(8,128)(2,1)S(1)} %get-tuple-element.305.my_ref), custom_call_target="tpu_custom_call" | custom-call | flops 20000000000 | bytes 8000000 | tf_op jit(solution)/shard_map/blur_inner/pallas_call | solution.py:430
  162.9 7.6 %blur_estimate.2 = (f32[128,64,128]{2,1,0:T(8,128)S(1)}, f32[64,128]{1,0:T(8,128)}, bf16[128,64,128]{2,1,0:T(8,128)(2,1)S(1)}, bf16[128,16,128]{2,1,0:T(8,128)(2,1)S(1)}, bf16[128,16,128]{2,1,0:T(8,128)(2,1)S(1)}) custom-call(s32[1]{0:T(128)} %bitcast.8.odd_ref, f32[1]{0:T(128)} %dynamic_slice.50.backdrop_ref, f32[9216,128]{1,0:T(8,128)S(1)} %blur_inner.5.inner_ref, ...), custom_call_target="tpu_custom_call" | custom-call | flops 10000000000 | bytes 16000000 | tf_op jit(solution)/shard_map/blur_estimate/pallas_call | solution.py:452
  170.5 2.2 collective-permute-start.30
  172.8 1.3 collective-permute-start.31
  174.1 4.6 %collective-permute-start.33 = (bf16[16,16,128]{2,1,0:T(8,128)(2,1)S(1)}, bf16[16,16,128]{2,1,0:T(8,128)(2,1)S(1)}, u32[]{:S(2)}, u32[]{:S(2)}) collective-permute-start(bf16[16,16,128]{2,1,0:T(8,128)(2,1)S(1)} %constant_dynamic-slice_fusion.3), channel_id=1, source_target_pairs={{1,18},{2,17},{3,20},{4,19},{5,22},{6,21},{9,26},{10,25},{11,28},{... | collective-permute-start | bytes 196616 | tf_op jit(solution)/shard_map/ppermute | solution.py:493
  178.7 5.9 %blur_inner.6.inner_ref = f32[9216,128]{1,0:T(8,128)S(1)} custom-call(bf16[128,64,128]{2,1,0:T(8,128)(2,1)S(1)} %get-tuple-element.313.own_ref, bf16[256,128]{1,0:T(8,128)(2,1)S(1)} %copy-done.20, bf16[128,256]{1,0:T(8,128)(2,1)S(1)} %copy-done.24, bf16[128,384]{1,0:T(8,128)(2,1)S(1)} %copy-done.12), custom_call_target="tpu_custom_call" | custom-call | flops 20000000000 | bytes 8000000 | tf_op jit(solution)/shard_map/blur_inner/pallas_call | solution.py:430
  184.7 6.9 %blur_quotient.3 = (bf16[128,64,128]{2,1,0:T(8,128)(2,1)S(1)}, bf16[128,16,128]{2,1,0:T(8,128)(2,1)S(1)}, bf16[128,16,128]{2,1,0:T(8,128)(2,1)S(1)}) custom-call(s32[1]{0:T(128)} %bitcast.8.odd_ref, f32[1]{0:T(128)} %dynamic_slice.50.backdrop_ref, f32[9216,128]{1,0:T(8,128)S(1)} %blur_inner.6.inner_ref, ...), custom_call_target="tpu_custom_call" | custom-call | flops 10000000000 | bytes 16000000 | tf_op jit(solution)/shard_map/blur_quotient/pallas_call | solution.py:452
  191.8 2.5 collective-permute-start.35
  194.3 1.3 collective-permute-start.36
  195.7 3.9 %collective-permute-start.38 = (bf16[16,16,128]{2,1,0:T(8,128)(2,1)S(1)}, bf16[16,16,128]{2,1,0:T(8,128)(2,1)S(1)}, u32[]{:S(2)}, u32[]{:S(2)}) collective-permute-start(bf16[16,16,128]{2,1,0:T(8,128)(2,1)S(1)} %constant_dynamic-slice_fusion), channel_id=1, source_target_pairs={{1,18},{2,17},{3,20},{4,19},{5,22},{6,21},{9,26},{10,25},{11,28},{... | collective-permute-start | bytes 196616 | tf_op jit(solution)/shard_map/ppermute | solution.py:493
  199.6 6.7 %blur_inner.7.inner_ref = f32[9216,128]{1,0:T(8,128)S(1)} custom-call(bf16[128,64,128]{2,1,0:T(8,128)(2,1)S(1)} %get-tuple-element.316.own_ref, bf16[256,128]{1,0:T(8,128)(2,1)S(1)} %copy-done.14, bf16[128,256]{1,0:T(8,128)(2,1)S(1)} %copy-done.18, bf16[128,384]{1,0:T(8,128)(2,1)S(1)} %get-tuple-element.305.my_ref), custom_call_target="tpu_custom_call" | custom-call | flops 20000000000 | bytes 8000000 | tf_op jit(solution)/shard_map/blur_inner/pallas_call | solution.py:430
  206.5 8.7 %blur_estimate.3 = (f32[128,64,128]{2,1,0:T(8,128)S(1)}, f32[64,128]{1,0:T(8,128)S(1)}, bf16[128,64,128]{2,1,0:T(8,128)(2,1)}, bf16[128,16,128]{2,1,0:T(8,128)(2,1)}, bf16[128,16,128]{2,1,0:T(8,128)(2,1)}) custom-call(s32[1]{0:T(128)} %bitcast.8.odd_ref, f32[1]{0:T(128)} %dynamic_slice.50.backdrop_ref, f32[9216,128]{1,0:T(8,128)S(1)} %blur_inner.7.inner_ref, ...), custom_call_target="tpu_custom_call" | custom-call | flops 10000000000 | bytes 16000000 | tf_op jit(solution)/shard_map/blur_estimate/pallas_call | solution.py:452
  215.2 2.0 copy-done.2
  218.5 2.0 multiply_convert_fusion
  220.9 1.5 collective-permute-start.39
  222.4 1.3 place_own.2.partial_ref
  223.7 1.6 copy-done.3
  225.3 1.3 place_own.3.partial_ref
  226.7 27.6 %collective-permute-done.18.other_ref = f32[64,64,128]{2,1,0:T(8,128)S(1)} collective-permute-done((f32[64,64,128]{2,1,0:T(8,128)}, f32[64,64,128]{2,1,0:T(8,128)S(1)}, u32[]{:S(2)}, u32[]{:S(2)}) %collective-permute-start.18) | collective-permute-done | bytes 2097184 | tf_op jit(solution)/shard_map/ppermute | solution.py:608
  254.3 1.3 place_other.2
  255.6 19.6 %collective-permute-done.39 = f16[65,64,128]{2,1,0:T(8,128)(2,1)S(1)} collective-permute-done((f16[65,64,128]{2,1,0:T(8,128)(2,1)S(1)}, f16[65,64,128]{2,1,0:T(8,128)(2,1)S(1)}, u32[]{:S(2)}, u32[]{:S(2)}) %collective-permute-start.39) | collective-permute-done | bytes 1064992 | tf_op jit(solution)/shard_map/ppermute | solution.py:608
  276.7 1.3 place_other.3
  (178 shorter events, 26.8 us)
Async XLA Ops:
  5.3 15.9 %copy-start.33 = (s32[128,1]{0,1:T(1,128)S(1)}, s32[128,1]{0,1:T(1,128)}, u32[]{:S(2)}) copy-start(s32[128,1]{0,1:T(1,128)} %param.12) | copy-start | bytes 1540
  5.3 16.6 %copy-start.40 = (s32[128]{0:T(128)S(1)}, s32[128]{0:T(128)}, u32[]{:S(2)}) copy-start(s32[128]{0:T(128)} %param.13) | copy-start | bytes 1540
  5.3 18.8 %copy-start.38 = (s32[64]{0:T(128)S(1)}, s32[64]{0:T(128)}, u32[]{:S(2)}) copy-start(s32[64]{0:T(128)} %param.14) | copy-start | bytes 772
  5.3 52.3 %copy-start.39 = (bf16[64,2]{0,1:T(2,128)(2,1)S(1)}, bf16[64,2]{0,1:T(2,128)(2,1)}, u32[]{:S(2)}) copy-start(bf16[64,2]{0,1:T(2,128)(2,1)} %param.15) | copy-start | bytes 772
  5.3 97.5 %all-to-all-start = ((bf16[16,2,4,64,128]{4,3,2,1,0:T(8,128)(2,1)}), bf16[16,2,4,64,128]{4,3,2,1,0:T(8,128)(2,1)S(1)}, u32[]{:S(2)}, u32[]{:S(2)}) async-start(bf16[16,2,4,64,128]{4,3,2,1,0:T(8,128)(2,1)} %bitcast.49), calls=%async_computation | async-start | bytes 4194304 | tf_op jit(solution)/shard_map/all_to_all | solution.py:656
  12.7 38.0 %collective-permute-start.10 = (bf16[2,4,64,128]{3,2,1,0:T(8,128)(2,1)S(1)}, bf16[2,4,64,128]{3,2,1,0:T(8,128)(2,1)S(1)}, u32[]{:S(2)}, u32[]{:S(2)}) collective-permute-start(bf16[2,4,64,128]{3,2,1,0:T(8,128)(2,1)S(1)} %get-tuple-element.280.refs_0_), channel_id=1, source_target_pairs={{0,2},{1,3},{2,0},{3,1},{4,6},{5,7},{6,4},{7,5},{8,10},{9,11},{10,... | collective-permute-start | bytes 393224 | tf_op jit(solution)/shard_map/ppermute | solution.py:637
  14.1 60.8 %collective-permute-start.12 = (bf16[2,4,64,128]{3,2,1,0:T(8,128)(2,1)S(1)}, bf16[2,4,64,128]{3,2,1,0:T(8,128)(2,1)S(1)}, u32[]{:S(2)}, u32[]{:S(2)}) collective-permute-start(bf16[2,4,64,128]{3,2,1,0:T(8,128)(2,1)S(1)} %get-tuple-element.280.refs_0_), channel_id=1, source_target_pairs={{0,4},{1,5},{2,6},{3,7},{4,0},{5,1},{6,2},{7,3},{8,12},{9,13},{10,... | collective-permute-start | bytes 393224 | tf_op jit(solution)/shard_map/ppermute | solution.py:637
  16.2 40.6 %collective-permute-start.11 = (bf16[2,4,64,128]{3,2,1,0:T(8,128)(2,1)S(1)}, bf16[2,4,64,128]{3,2,1,0:T(8,128)(2,1)S(1)}, u32[]{:S(2)}, u32[]{:S(2)}) collective-permute-start(bf16[2,4,64,128]{3,2,1,0:T(8,128)(2,1)S(1)} %get-tuple-element.281), channel_id=1, source_target_pairs={{0,10},{1,11},{2,8},{3,9},{4,14},{5,15},{6,12},{7,13},{8,2},{9,3},... | collective-permute-start | bytes 393224 | tf_op jit(solution)/shard_map/ppermute | solution.py:637
  17.4 61.2 %collective-permute-start.13 = (bf16[2,4,64,128]{3,2,1,0:T(8,128)(2,1)S(1)}, bf16[2,4,64,128]{3,2,1,0:T(8,128)(2,1)S(1)}, u32[]{:S(2)}, u32[]{:S(2)}) collective-permute-start(bf16[2,4,64,128]{3,2,1,0:T(8,128)(2,1)S(1)} %get-tuple-element.281), channel_id=1, source_target_pairs={{0,12},{1,13},{2,14},{3,15},{4,8},{5,9},{6,10},{7,11},{8,4},{9,5},... | collective-permute-start | bytes 393224 | tf_op jit(solution)/shard_map/ppermute | solution.py:637
  17.5 61.7 %collective-permute-start.14 = (bf16[2,4,64,128]{3,2,1,0:T(8,128)(2,1)S(1)}, bf16[2,4,64,128]{3,2,1,0:T(8,128)(2,1)S(1)}, u32[]{:S(2)}, u32[]{:S(2)}) collective-permute-start(bf16[2,4,64,128]{3,2,1,0:T(8,128)(2,1)S(1)} %get-tuple-element.280.refs_0_), channel_id=1, source_target_pairs={{0,6},{1,7},{2,4},{3,5},{4,2},{5,3},{6,0},{7,1},{8,14},{9,15},{10,... | collective-permute-start | bytes 393224 | tf_op jit(solution)/shard_map/ppermute | solution.py:637
  23.0 56.9 %copy-start.34 = (pred[8,16]{1,0:T(8,128)(4,1)}, pred[8,16]{1,0:T(8,128)(4,1)S(1)}, u32[]{:S(2)}) copy-start(pred[8,16]{1,0:T(8,128)(4,1)S(1)} %get-tuple-element.349) | copy-start | bytes 388
  24.0 55.8 %copy-start.37 = (f32[64,1]{0,1:T(1,128)}, f32[64,1]{0,1:T(1,128)S(1)}, u32[]{:S(2)}) copy-start(f32[64,1]{0,1:T(1,128)S(1)} %convert_bitcast_fusion.1) | copy-start | bytes 772
  50.7 29.1 %collective-permute-start.15 = (bf16[2,4,64,128]{3,2,1,0:T(8,128)(2,1)S(1)}, bf16[2,4,64,128]{3,2,1,0:T(8,128)(2,1)S(1)}, u32[]{:S(2)}, u32[]{:S(2)}) collective-permute-start(bf16[2,4,64,128]{3,2,1,0:T(8,128)(2,1)S(1)} %get-tuple-element.281), channel_id=1, source_target_pairs={{0,14},{1,15},{2,12},{3,13},{4,10},{5,11},{6,8},{7,9},{8,6},{9,7},... | collective-permute-start | bytes 393224 | tf_op jit(solution)/shard_map/ppermute | solution.py:637
  57.4 22.5 %collective-permute-start.9 = (bf16[2,4,64,128]{3,2,1,0:T(8,128)(2,1)S(1)}, bf16[2,4,64,128]{3,2,1,0:T(8,128)(2,1)S(1)}, u32[]{:S(2)}, u32[]{:S(2)}) collective-permute-start(bf16[2,4,64,128]{3,2,1,0:T(8,128)(2,1)S(1)} %get-tuple-element.281), channel_id=1, source_target_pairs={{0,8},{1,9},{2,10},{3,11},{4,12},{5,13},{6,14},{7,15},{8,0},{9,1},... | collective-permute-start | bytes 393224 | tf_op jit(solution)/shard_map/ppermute | solution.py:637
  57.6 22.3 %copy-start.36 = (f32[64,2]{0,1:T(2,128)}, f32[64,2]{0,1:T(2,128)S(1)}, u32[]{:S(2)}) copy-start(f32[64,2]{0,1:T(2,128)S(1)} %convert_element_type.41) | copy-start | bytes 1540
  74.8 27.1 %collective-permute-start.8 = (f32[64,3]{0,1:T(4,128)}, f32[64,3]{0,1:T(4,128)}, u32[]{:S(2)}, u32[]{:S(2)}) collective-permute-start(f32[64,3]{0,1:T(4,128)} %pad_maximum_fusion.1), channel_id=1, source_target_pairs={{0,8},{8,0},{16,24},{24,16},{1,9},{9,1},{17,25},{25,17},{2,10},{10... | collective-permute-start | bytes 2312 | tf_op jit(solution)/shard_map/ppermute | solution.py:608
  82.7 20.1 %collective-permute-start.16 = (bf16[4,2,2,4,64,128]{5,4,3,2,1,0:T(8,128)(2,1)S(1)}, bf16[4,2,2,4,64,128]{5,4,3,2,1,0:T(8,128)(2,1)}, u32[]{:S(2)}, u32[]{:S(2)}) collective-permute-start(bf16[4,2,2,4,64,128]{5,4,3,2,1,0:T(8,128)(2,1)S(1)} %bitcast.47), channel_id=1, source_target_pairs={{0,1},{1,0},{2,3},{3,2},{4,5},{5,4},{6,7},{7,6},{8,9},{9,8},{10,11... | collective-permute-start | bytes 3145736 | tf_op jit(solution)/shard_map/ppermute | solution.py:641
  108.6 11.3 %collective-permute-start.17 = (f16[12,128,128]{2,1,0:T(8,128)(2,1)S(1)}, f16[12,128,128]{2,1,0:T(8,128)(2,1)S(1)}, u32[]{:S(2)}, u32[]{:S(2)}) collective-permute-start(f16[12,128,128]{2,1,0:T(8,128)(2,1)S(1)} %convert_element_type.46), channel_id=1, source_target_pairs={{0,1},{1,2},{2,3},{3,4},{4,5},{5,6},{6,7},{8,9},{9,10},{10,11},{11... | collective-permute-start | bytes 1179656 | tf_op jit(solution)/shard_map/ppermute | solution.py:720
  120.0 13.7 %copy-start.12 = (bf16[128,384]{1,0:T(8,128)(2,1)S(1)}, bf16[128,384]{1,0:T(8,128)(2,1)}, u32[]{:S(2)}) copy-start(bf16[128,384]{1,0:T(8,128)(2,1)} %copy-done.11) | copy-start | bytes 294916
  120.0 13.7 %copy-start.20 = (bf16[256,128]{1,0:T(8,128)(2,1)S(1)}, bf16[256,128]{1,0:T(8,128)(2,1)}, u32[]{:S(2)}) copy-start(bf16[256,128]{1,0:T(8,128)(2,1)} %copy-done.19) | copy-start | bytes 196612
  120.0 13.7 %copy-start.24 = (bf16[128,256]{1,0:T(8,128)(2,1)S(1)}, bf16[128,256]{1,0:T(8,128)(2,1)}, u32[]{:S(2)}) copy-start(bf16[128,256]{1,0:T(8,128)(2,1)} %copy-done.23) | copy-start | bytes 196612
  122.4 62.3 %copy-start = (f32[128,64,128]{2,1,0:T(8,128)}, f32[128,64,128]{2,1,0:T(8,128)S(1)}, u32[]{:S(2)}) copy-start(f32[128,64,128]{2,1,0:T(8,128)S(1)} %get-tuple-element.290.both_ref.point_ref) | copy-start | bytes 12582916
  122.4 18.9 %collective-permute-start.19 = (bf16[128,16,128]{2,1,0:T(8,128)(2,1)S(1)}, bf16[128,16,128]{2,1,0:T(8,128)(2,1)S(1)}, u32[]{:S(2)}, u32[]{:S(2)}) collective-permute-start(bf16[128,16,128]{2,1,0:T(8,128)(2,1)S(1)} %get-tuple-element.295), channel_id=1, source_target_pairs={{0,1},{1,0},{2,3},{3,2},{4,5},{5,4},{6,7},{7,6},{8,9},{9,8},{10,11... | collective-permute-start | bytes 1572872 | tf_op jit(solution)/shard_map/ppermute | solution.py:494
  122.5 18.8 %collective-permute-start.20 = (bf16[128,16,128]{2,1,0:T(8,128)(2,1)S(1)}, bf16[128,16,128]{2,1,0:T(8,128)(2,1)S(1)}, u32[]{:S(2)}, u32[]{:S(2)}) collective-permute-start(bf16[128,16,128]{2,1,0:T(8,128)(2,1)S(1)} %get-tuple-element.296), channel_id=1, source_target_pairs={{1,2},{2,1},{3,4},{4,3},{5,6},{6,5},{9,10},{10,9},{11,12},{12,11},... | collective-permute-start | bytes 1572872 | tf_op jit(solution)/shard_map/ppermute | solution.py:494
  127.5 13.8 %collective-permute-start.21 = (bf16[16,64,128]{2,1,0:T(8,128)(2,1)S(1)}, bf16[16,64,128]{2,1,0:T(8,128)(2,1)S(1)}, u32[]{:S(2)}, u32[]{:S(2)}) collective-permute-start(bf16[16,64,128]{2,1,0:T(8,128)(2,1)S(1)} %constant_dynamic-slice_fusion.11), channel_id=1, source_target_pairs={{0,16},{8,24},{16,0},{24,8},{1,17},{9,25},{17,1},{25,9},{2,18},{10... | collective-permute-start | bytes 786440 | tf_op jit(solution)/shard_map/ppermute | solution.py:490
  128.8 12.5 %collective-permute-start.22 = (bf16[16,16,128]{2,1,0:T(8,128)(2,1)S(1)}, bf16[16,16,128]{2,1,0:T(8,128)(2,1)S(1)}, u32[]{:S(2)}, u32[]{:S(2)}) collective-permute-start(bf16[16,16,128]{2,1,0:T(8,128)(2,1)S(1)} %constant_dynamic-slice_fusion.10), channel_id=1, source_target_pairs={{0,17},{1,16},{2,19},{3,18},{4,21},{5,20},{6,23},{7,22},{8,25},{9,... | collective-permute-start | bytes 196616 | tf_op jit(solution)/shard_map/ppermute | solution.py:493
  128.8 12.5 %collective-permute-start.23 = (bf16[16,16,128]{2,1,0:T(8,128)(2,1)S(1)}, bf16[16,16,128]{2,1,0:T(8,128)(2,1)S(1)}, u32[]{:S(2)}, u32[]{:S(2)}) collective-permute-start(bf16[16,16,128]{2,1,0:T(8,128)(2,1)S(1)} %constant_dynamic-slice_fusion.9), channel_id=1, source_target_pairs={{1,18},{2,17},{3,20},{4,19},{5,22},{6,21},{9,26},{10,25},{11,28},{... | collective-permute-start | bytes 196616 | tf_op jit(solution)/shard_map/ppermute | solution.py:493
  141.3 14.8 %copy-start.14 = (bf16[256,128]{1,0:T(8,128)(2,1)S(1)}, bf16[256,128]{1,0:T(8,128)(2,1)}, u32[]{:S(2)}) copy-start(bf16[256,128]{1,0:T(8,128)(2,1)} %copy-done.13) | copy-start | bytes 196612
  141.3 14.8 %copy-start.18 = (bf16[128,256]{1,0:T(8,128)(2,1)S(1)}, bf16[128,256]{1,0:T(8,128)(2,1)}, u32[]{:S(2)}) copy-start(bf16[128,256]{1,0:T(8,128)(2,1)} %copy-done.17) | copy-start | bytes 196612
  148.3 14.5 %collective-permute-start.24 = (bf16[128,16,128]{2,1,0:T(8,128)(2,1)S(1)}, bf16[128,16,128]{2,1,0:T(8,128)(2,1)S(1)}, u32[]{:S(2)}, u32[]{:S(2)}) collective-permute-start(bf16[128,16,128]{2,1,0:T(8,128)(2,1)S(1)} %get-tuple-element.306), channel_id=1, source_target_pairs={{0,1},{1,0},{2,3},{3,2},{4,5},{5,4},{6,7},{7,6},{8,9},{9,8},{10,11... | collective-permute-start | bytes 1572872 | tf_op jit(solution)/shard_map/ppermute | solution.py:494
  148.4 14.4 %collective-permute-start.25 = (bf16[128,16,128]{2,1,0:T(8,128)(2,1)S(1)}, bf16[128,16,128]{2,1,0:T(8,128)(2,1)S(1)}, u32[]{:S(2)}, u32[]{:S(2)}) collective-permute-start(bf16[128,16,128]{2,1,0:T(8,128)(2,1)S(1)} %get-tuple-element.307), channel_id=1, source_target_pairs={{1,2},{2,1},{3,4},{4,3},{5,6},{6,5},{9,10},{10,9},{11,12},{12,11},... | collective-permute-start | bytes 1572872 | tf_op jit(solution)/shard_map/ppermute | solution.py:494
  150.9 12.0 %copy-start.16 = (bf16[128,256]{1,0:T(8,128)(2,1)S(1)}, bf16[128,256]{1,0:T(8,128)(2,1)}, u32[]{:S(2)}) copy-start(bf16[128,256]{1,0:T(8,128)(2,1)} %copy-done.15) | copy-start | bytes 196612
  150.9 12.0 %copy-start.26 = (bf16[64,192]{1,0:T(8,128)(2,1)S(1)}, bf16[64,192]{1,0:T(8,128)(2,1)}, u32[]{:S(2)}) copy-start(bf16[64,192]{1,0:T(8,128)(2,1)} %copy-done.25) | copy-start | bytes 73732
  150.9 11.9 %collective-permute-start.26 = (bf16[16,64,128]{2,1,0:T(8,128)(2,1)S(1)}, bf16[16,64,128]{2,1,0:T(8,128)(2,1)S(1)}, u32[]{:S(2)}, u32[]{:S(2)}) collective-permute-start(bf16[16,64,128]{2,1,0:T(8,128)(2,1)S(1)} %constant_dynamic-slice_fusion.8), channel_id=1, source_target_pairs={{0,16},{8,24},{16,0},{24,8},{1,17},{9,25},{17,1},{25,9},{2,18},{10... | collective-permute-start | bytes 786440 | tf_op jit(solution)/shard_map/ppermute | solution.py:490
  151.2 11.7 %collective-permute-start.27 = (bf16[16,16,128]{2,1,0:T(8,128)(2,1)S(1)}, bf16[16,16,128]{2,1,0:T(8,128)(2,1)S(1)}, u32[]{:S(2)}, u32[]{:S(2)}) collective-permute-start(bf16[16,16,128]{2,1,0:T(8,128)(2,1)S(1)} %constant_dynamic-slice_fusion.7), channel_id=1, source_target_pairs={{0,17},{1,16},{2,19},{3,18},{4,21},{5,20},{6,23},{7,22},{8,25},{9,... | collective-permute-start | bytes 196616 | tf_op jit(solution)/shard_map/ppermute | solution.py:493
  151.4 11.4 %collective-permute-start.28 = (bf16[16,16,128]{2,1,0:T(8,128)(2,1)S(1)}, bf16[16,16,128]{2,1,0:T(8,128)(2,1)S(1)}, u32[]{:S(2)}, u32[]{:S(2)}) collective-permute-start(bf16[16,16,128]{2,1,0:T(8,128)(2,1)S(1)} %constant_dynamic-slice_fusion.6), channel_id=1, source_target_pairs={{1,18},{2,17},{3,20},{4,19},{5,22},{6,21},{9,26},{10,25},{11,28},{... | collective-permute-start | bytes 196616 | tf_op jit(solution)/shard_map/ppermute | solution.py:493
  170.5 14.1 %collective-permute-start.29 = (bf16[128,16,128]{2,1,0:T(8,128)(2,1)S(1)}, bf16[128,16,128]{2,1,0:T(8,128)(2,1)S(1)}, u32[]{:S(2)}, u32[]{:S(2)}) collective-permute-start(bf16[128,16,128]{2,1,0:T(8,128)(2,1)S(1)} %get-tuple-element.314), channel_id=1, source_target_pairs={{0,1},{1,0},{2,3},{3,2},{4,5},{5,4},{6,7},{7,6},{8,9},{9,8},{10,11... | collective-permute-start | bytes 1572872 | tf_op jit(solution)/shard_map/ppermute | solution.py:494
  170.5 14.1 %collective-permute-start.30 = (bf16[128,16,128]{2,1,0:T(8,128)(2,1)S(1)}, bf16[128,16,128]{2,1,0:T(8,128)(2,1)S(1)}, u32[]{:S(2)}, u32[]{:S(2)}) collective-permute-start(bf16[128,16,128]{2,1,0:T(8,128)(2,1)S(1)} %get-tuple-element.315), channel_id=1, source_target_pairs={{1,2},{2,1},{3,4},{4,3},{5,6},{6,5},{9,10},{10,9},{11,12},{12,11},... | collective-permute-start | bytes 1572872 | tf_op jit(solution)/shard_map/ppermute | solution.py:494
  172.8 11.9 %collective-permute-start.31 = (bf16[16,64,128]{2,1,0:T(8,128)(2,1)S(1)}, bf16[16,64,128]{2,1,0:T(8,128)(2,1)S(1)}, u32[]{:S(2)}, u32[]{:S(2)}) collective-permute-start(bf16[16,64,128]{2,1,0:T(8,128)(2,1)S(1)} %constant_dynamic-slice_fusion.5), channel_id=1, source_target_pairs={{0,16},{8,24},{16,0},{24,8},{1,17},{9,25},{17,1},{25,9},{2,18},{10... | collective-permute-start | bytes 786440 | tf_op jit(solution)/shard_map/ppermute | solution.py:490
  174.1 10.6 %collective-permute-start.32 = (bf16[16,16,128]{2,1,0:T(8,128)(2,1)S(1)}, bf16[16,16,128]{2,1,0:T(8,128)(2,1)S(1)}, u32[]{:S(2)}, u32[]{:S(2)}) collective-permute-start(bf16[16,16,128]{2,1,0:T(8,128)(2,1)S(1)} %constant_dynamic-slice_fusion.4), channel_id=1, source_target_pairs={{0,17},{1,16},{2,19},{3,18},{4,21},{5,20},{6,23},{7,22},{8,25},{9,... | collective-permute-start | bytes 196616 | tf_op jit(solution)/shard_map/ppermute | solution.py:493
  174.1 10.6 %collective-permute-start.33 = (bf16[16,16,128]{2,1,0:T(8,128)(2,1)S(1)}, bf16[16,16,128]{2,1,0:T(8,128)(2,1)S(1)}, u32[]{:S(2)}, u32[]{:S(2)}) collective-permute-start(bf16[16,16,128]{2,1,0:T(8,128)(2,1)S(1)} %constant_dynamic-slice_fusion.3), channel_id=1, source_target_pairs={{1,18},{2,17},{3,20},{4,19},{5,22},{6,21},{9,26},{10,25},{11,28},{... | collective-permute-start | bytes 196616 | tf_op jit(solution)/shard_map/ppermute | solution.py:493
  191.6 14.8 %collective-permute-start.34 = (bf16[128,16,128]{2,1,0:T(8,128)(2,1)S(1)}, bf16[128,16,128]{2,1,0:T(8,128)(2,1)S(1)}, u32[]{:S(2)}, u32[]{:S(2)}) collective-permute-start(bf16[128,16,128]{2,1,0:T(8,128)(2,1)S(1)} %get-tuple-element.317), channel_id=1, source_target_pairs={{0,1},{1,0},{2,3},{3,2},{4,5},{5,4},{6,7},{7,6},{8,9},{9,8},{10,11... | collective-permute-start | bytes 1572872 | tf_op jit(solution)/shard_map/ppermute | solution.py:494
  191.8 14.7 %collective-permute-start.35 = (bf16[128,16,128]{2,1,0:T(8,128)(2,1)S(1)}, bf16[128,16,128]{2,1,0:T(8,128)(2,1)S(1)}, u32[]{:S(2)}, u32[]{:S(2)}) collective-permute-start(bf16[128,16,128]{2,1,0:T(8,128)(2,1)S(1)} %get-tuple-element.318), channel_id=1, source_target_pairs={{1,2},{2,1},{3,4},{4,3},{5,6},{6,5},{9,10},{10,9},{11,12},{12,11},... | collective-permute-start | bytes 1572872 | tf_op jit(solution)/shard_map/ppermute | solution.py:494
  194.3 12.1 %collective-permute-start.36 = (bf16[16,64,128]{2,1,0:T(8,128)(2,1)S(1)}, bf16[16,64,128]{2,1,0:T(8,128)(2,1)S(1)}, u32[]{:S(2)}, u32[]{:S(2)}) collective-permute-start(bf16[16,64,128]{2,1,0:T(8,128)(2,1)S(1)} %constant_dynamic-slice_fusion.2), channel_id=1, source_target_pairs={{0,16},{8,24},{16,0},{24,8},{1,17},{9,25},{17,1},{25,9},{2,18},{10... | collective-permute-start | bytes 786440 | tf_op jit(solution)/shard_map/ppermute | solution.py:490
  195.7 10.7 %collective-permute-start.37 = (bf16[16,16,128]{2,1,0:T(8,128)(2,1)S(1)}, bf16[16,16,128]{2,1,0:T(8,128)(2,1)S(1)}, u32[]{:S(2)}, u32[]{:S(2)}) collective-permute-start(bf16[16,16,128]{2,1,0:T(8,128)(2,1)S(1)} %constant_dynamic-slice_fusion.1), channel_id=1, source_target_pairs={{0,17},{1,16},{2,19},{3,18},{4,21},{5,20},{6,23},{7,22},{8,25},{9,... | collective-permute-start | bytes 196616 | tf_op jit(solution)/shard_map/ppermute | solution.py:493
  195.7 10.8 %collective-permute-start.38 = (bf16[16,16,128]{2,1,0:T(8,128)(2,1)S(1)}, bf16[16,16,128]{2,1,0:T(8,128)(2,1)S(1)}, u32[]{:S(2)}, u32[]{:S(2)}) collective-permute-start(bf16[16,16,128]{2,1,0:T(8,128)(2,1)S(1)} %constant_dynamic-slice_fusion), channel_id=1, source_target_pairs={{1,18},{2,17},{3,20},{4,19},{5,22},{6,21},{9,26},{10,25},{11,28},{... | collective-permute-start | bytes 196616 | tf_op jit(solution)/shard_map/ppermute | solution.py:493
  206.3 47.9 %collective-permute-start.18 = (f32[64,64,128]{2,1,0:T(8,128)}, f32[64,64,128]{2,1,0:T(8,128)S(1)}, u32[]{:S(2)}, u32[]{:S(2)}) collective-permute-start(f32[64,64,128]{2,1,0:T(8,128)} %constant_dynamic-slice_fusion.12), channel_id=1, source_target_pairs={{0,8},{8,0},{16,24},{24,16},{1,9},{9,1},{17,25},{25,17},{2,10},{10... | collective-permute-start | bytes 6291464 | tf_op jit(solution)/shard_map/ppermute | solution.py:608
  220.9 54.3 %collective-permute-start.39 = (f16[65,64,128]{2,1,0:T(8,128)(2,1)S(1)}, f16[65,64,128]{2,1,0:T(8,128)(2,1)S(1)}, u32[]{:S(2)}, u32[]{:S(2)}) collective-permute-start(f16[65,64,128]{2,1,0:T(8,128)(2,1)S(1)} %concatenate.11), channel_id=1, source_target_pairs={{0,8},{8,0},{16,24},{24,16},{1,9},{9,1},{17,25},{25,17},{2,10},{10... | collective-permute-start | bytes 3194888 | tf_op jit(solution)/shard_map/ppermute | solution.py:608
  (26 other events, 43.2 us)

commit v3 on v2

--- a/solution.py
+++ b/solution.py
@@ -21,11 +21,11 @@
     return [pl.BlockSpec(memory_space=pltpu.VMEM) for _ in range(count)]
 
 
-def place_own_kernel(channel_ref, both_ref, out_ref, sem):
+def place_own_kernel(channel_ref, part_ref, both_ref, out_ref, sem):
     rows = out_ref.shape[1]
     channel = channel_ref[0]
     copy = pltpu.make_async_copy(
-        both_ref.at[pl.ds(pl.multiple_of(channel * rows, 8), rows)], out_ref.at[channel], sem
+        both_ref.at[pl.ds(pl.multiple_of(part_ref[0] * rows, 8), rows)], out_ref.at[channel], sem
     )
     copy.start()
     copy.wait()
@@ -37,17 +37,17 @@
     copy.wait()
 
 
-def place_own(channel, both_rows):
+def place_own(channel, part, both_rows):
     rows = both_rows.shape[0] // 2
     return pl.pallas_call(
         place_own_kernel,
         out_shape=jax.ShapeDtypeStruct((2, rows) + both_rows.shape[1:], both_rows.dtype),
-        in_specs=[pl.BlockSpec(memory_space=pltpu.SMEM)] + in_vmem(1),
+        in_specs=[pl.BlockSpec(memory_space=pltpu.SMEM)] * 2 + in_vmem(1),
         out_specs=pl.BlockSpec(memory_space=pl.ANY),
         scratch_shapes=[pltpu.SemaphoreType.DMA(())],
         compiler_params=pltpu.CompilerParams(vmem_limit_bytes=8 << 20),
         name="place_own",
-    )(channel[None], both_rows)
+    )(channel[None], part[None], both_rows)
 
 
 def place_other(channel, other, partial):
@@ -301,8 +301,8 @@
 def inner_kernel(own_ref, mx_ref, mz_ref, my_ref, out_ref, mid_ref, *, coarse):
     ny, nz, lanes = own_ref.shape
     pitch = nz + 8
-    group = 16
-    ahead = 8
+    group = ny // 2
+    ahead = 16
 
     def planes(g, carry):
         mz = mz_ref[...]
@@ -334,7 +334,7 @@
     lax.fori_loop(0, nz // (2 * ahead), columns, 0)
 
 
-def outer_kernel(odd_ref, backdrop_ref, inner_ref, a_ref, b_ref, side_ref, side_a_ref, side_b_ref,
+def outer_kernel(odd_ref, swap_ref, backdrop_ref, inner_ref, a_ref, b_ref, side_ref, side_a_ref, side_b_ref,
                  mx_ref, mze_ref, mzs_ref, mye_ref, mys_ref, point_ref, *rest, quotient, first, ny, nz):
     if quotient:
         cast_ref, out_a_ref, out_b_ref, edge_ref, rim_ref, more_ref = rest
@@ -346,26 +346,27 @@
     faces = 2 * HALO
     edge_pitch = faces + 8
     width = nz + faces
-    group = 16
+    many = ny // 2
 
     def face_planes(g, carry):
         pieces = []
-        for k in range(group):
-            pieces += [a_ref[g * group + k], b_ref[g * group + k]]
+        for k in range(many):
+            pieces += [a_ref[g * many + k], b_ref[g * many + k]]
         mze = mze_ref[...]
         alongx = blur_x(pieces, mx_ref[...])
-        for k in range(0, group, 8):
+        for k in range(0, many, 8):
             pairs = []
             for p in range(4):
                 pairs += [pair_lanes(alongx, k + 2 * p, faces)] * 2
             both = jnp.dot(mze, jnp.concatenate(pairs, axis=0), preferred_element_type=F32)
             for p in range(4):
-                row = pl.multiple_of((g * group + k + 2 * p) * edge_pitch, 8)
+                row = pl.multiple_of((g * many + k + 2 * p) * edge_pitch, 8)
                 edge_ref[pl.ds(row, faces), :] = both[p * faces:(p + 1) * faces, :lanes]
                 edge_ref[pl.ds(row + edge_pitch, faces), :] = both[p * faces:(p + 1) * faces, lanes:]
         return carry
 
-    lax.fori_loop(0, ny // group, face_planes, 0)
+    lax.fori_loop(0, ny // many, face_planes, 0)
+    group = 16
 
     for g in range(nside // group):
         pieces = []
@@ -403,6 +404,7 @@
 
     backdrop = backdrop_ref[0]
     odd = odd_ref[0] == 1
+    swap = swap_ref[0]
 
     def finish(y, carry):
         row = pl.multiple_of(y * pitch, 8)
@@ -411,7 +413,7 @@
             value = point_ref[y] / (blurred + backdrop)
         else:
             value = (point_ref[y] + backdrop if first else point_ref[y]) * blurred
-            full_ref[y] = value
+            full_ref[y ^ swap] = value
             carry = jnp.maximum(carry, value)
         cast = value.astype(BF16)
         cast_ref[y] = cast
@@ -439,7 +441,7 @@
     )(block, *matrices)
 
 
-def blur_outer(quotient, first, backdrop, inner, halos, matrices, point):
+def blur_outer(quotient, first, swap, backdrop, inner, halos, matrices, point):
     ny, nz, nx = point.shape
     nside = halos[2].shape[0]
     outs = [
@@ -452,7 +454,7 @@
     return pl.pallas_call(
         functools.partial(outer_kernel, quotient=quotient, first=first, ny=ny, nz=nz),
         out_shape=outs,
-        in_specs=[pl.BlockSpec(memory_space=pltpu.SMEM)] * 2 + in_vmem(12),
+        in_specs=[pl.BlockSpec(memory_space=pltpu.SMEM)] * 3 + in_vmem(12),
         out_specs=in_vmem(len(outs)),
         scratch_shapes=[
             pltpu.VMEM((ny * (2 * HALO + 8), nx), F32),
@@ -462,7 +464,7 @@
         compiler_params=pltpu.CompilerParams(vmem_limit_bytes=32 << 20),
         cost_estimate=pl.CostEstimate(flops=10_000_000_000, transcendentals=0, bytes_accessed=16_000_000),
         name="blur_quotient" if quotient else "blur_estimate",
-    )(odd_block(), backdrop, inner, *halos, *matrices, point)
+    )(odd_block(), swap[None], backdrop, inner, *halos, *matrices, point)
 
 
 def odd_block():
@@ -485,13 +487,15 @@
     ends = [jnp.where(odd == 1, 0, rows - HALO), jnp.where(odd == 1, rows - HALO, 0)]
     sides = []
     corners = [[] for _ in z_phases]
+    across = []
+    for face, z_pairs in zip(faces, z_phases):
+        across.append(lax.ppermute(face, "bz", z_pairs))
     for start, pairs in zip(ends, partners(lax.axis_size("by") // 2)):
         pairs = [(2 * a + c, 2 * b + c) for a, b in pairs for c in range(2)]
         sides.append(lax.ppermute(lax.dynamic_slice_in_dim(block, start, HALO, 0), "by", pairs))
         for face, z_pairs, found in zip(faces, z_phases, corners):
             both = [(a * blocks + p, b * blocks + q) for a, b in pairs for p, q in z_pairs]
             found.append(lax.ppermute(lax.dynamic_slice_in_dim(face, start, HALO, 0), ("by", "bz"), both))
-    across = [lax.ppermute(face, "bz", pairs) for face, pairs in zip(faces, z_phases)]
     join = lambda parts: parts[0] if len(parts) == 1 else jnp.concatenate(parts, axis=0)
     return *across, join(sides), *[join(found) for found in corners]
 
@@ -729,20 +733,19 @@
     for iteration in range(ITERS):
         halos = halo_exchange(field)
         inner = blur_inner(True, field[0], forward[0])
-        field = blur_outer(True, False, backdrop, inner, halos, forward[1], deskewed)
+        field = blur_outer(True, False, jnp.int32(0), backdrop, inner, halos, forward[1], deskewed)
         halos = halo_exchange(field)
+        swap = channel * rows if iteration == ITERS - 1 else jnp.int32(0)
         inner = blur_inner(False, field[0], backward[0])
-        estimate, peak, *field = blur_outer(
-            False, iteration == 0, backdrop, inner, halos, backward[1], estimate
-        )
-    theirs = half(estimate, other_start)
+        estimate, peak, *field = blur_outer(False, iteration == 0, swap, backdrop, inner, halos, backward[1], estimate)
+    theirs = estimate[rows:]
     power = jnp.floor(jnp.log2(jnp.max(peak))) - 13.0
     message = jnp.concatenate(
         [theirs * jnp.exp2(-power), jnp.full((1,) + theirs.shape[1:], power)], axis=0
     ).astype(jnp.float16)
     got = swap_pair(message)
-    deskewed_out = place_other(channel, deskewed_other, place_own(channel, deskewed))
-    partial = place_own(channel, estimate)
+    deskewed_out = place_other(channel, deskewed_other, place_own(channel, channel, deskewed))
+    partial = place_own(channel, jnp.int32(0), estimate)
     received = got[:rows].astype(F32) * jnp.exp2(got[rows, 0, 0].astype(F32))
     return deskewed_out, place_other(channel, received, partial)
 

time: 279 us -> 285 us (1.022)
  starting transfers between devices: 63.3 us -> 78.4 us
  Pallas kernels: 81.9 us -> 67.5 us
  local copies, waits for them, and re-layouts: 22.9 us -> 26.8 us
    ppermute x7, starting transfers between devices: 11 us -> 31.3 us  [share_spill(): piece = lax.ppermute(piece, ('by', 'bz'), pairs)]
    ppermute x7, waiting for transfers between devices: 49 us -> 35.6 us  [share_spill(): piece = lax.ppermute(piece, ('by', 'bz'), pairs)]
    ppermute x4, waiting for transfers between devices: 0.01 us -> 11.7 us  [halo_exchange(): lax.ppermute(lax.dynamic_slice_in_dim(block, start, HALO, 0), 'by', pairs)]
    ppermute x8, starting transfers between devices: 12.2 us -> 21.9 us  [halo_exchange(): across.append(lax.ppermute(face, 'bz', z_pairs))]
    pallas_call x4, Pallas kernels: 25.3 us -> 17.4 us  [blur_inner(): pl.pallas_call(functools.partial(inner_kernel, coarse=coarse), out_shape=...]
    ppermute x8, starting transfers between devices: 18.3 us -> 10.9 us  [halo_exchange(): lax.ppermute(lax.dynamic_slice_in_dim(face, start, HALO, 0), ('by', 'bz')...]
    pallas_call x4, Pallas kernels: 30.3 us -> 23.6 us  [blur_outer(): pl.pallas_call(functools.partial(outer_kernel, quotient=quotient, first=f...]
    ppermute x1, starting transfers between devices: 5.83 us -> 1.92 us  [shards(): lax.ppermute(over.astype(jnp.float16), 'bz', [(i, i + 1) for i in range(b...]
  transfers between devices with their start and end apart: 33 -> 33, of which waited for: 6 -> 11; matrix products, arithmetic and copies ran while one was open for 5% -> 6% of each run, Pallas kernels for 18% -> 14%
where the time goes in v3:
time: 285 us; the launch traced here: 283 us
  waiting for transfers between devices  95.7 us (34%)
  starting transfers between devices  78.4 us (28%)
  Pallas kernels  67.5 us (24%)
  local copies, waits for them, and re-layouts  26.8 us (9%)
  other arithmetic  10.9 us (4%)
  between operations  3.5 us (1%)
    ppermute x3, waiting for transfers between devices, swap_pair(): lax.ppermute(x, 'by', [(i, i ^ 1) for i in range(lax.axis_size('by'))])  47.3 us
    ppermute x7, waiting for transfers between devices, share_spill(): piece = lax.ppermute(piece, ('by', 'bz'), pairs)  35.6 us
    ppermute x7, starting transfers between devices, share_spill(): piece = lax.ppermute(piece, ('by', 'bz'), pairs)  31.3 us
    pallas_call x4, Pallas kernels, blur_outer(): pl.pallas_call(functools.partial(outer_kernel, quotient=quotient, first=f...  23.6 us
    ppermute x8, starting transfers between devices, halo_exchange(): across.append(lax.ppermute(face, 'bz', z_pairs))  21.9 us
    unnamed x91, local copies, waits for them, and re-layouts  20.1 us
    pallas_call x4, Pallas kernels, blur_inner(): pl.pallas_call(functools.partial(inner_kernel, coarse=coarse), out_shape=...  17.4 us
    ppermute x4, waiting for transfers between devices, halo_exchange(): lax.ppermute(lax.dynamic_slice_in_dim(block, start, HALO, 0), 'by', pairs)  11.7 us
  transfers between devices with their start and end apart: 33, of which 11 were waited for; matrix products, arithmetic and copies ran while one was open for 6% of the time, Pallas kernels for 14%

profile of v3, /device:TPU:1, one launch (start us, length us, event | category | flops | bytes accessed | tf_op | source)
XLA Modules:
  0.0 282.6 jit_solution(4512405005482668201)
XLA Ops:
  0.6 3.3 %pack_tiles.1 = (bf16[32,4,64,128]{3,2,1,0:T(8,128)(2,1)S(1)}, bf16[2,4,64,128]{3,2,1,0:T(8,128)(2,1)S(1)}, bf16[2,4,64,128]{3,2,1,0:T(8,128)(2,1)S(1)}) custom-call(s32[1]{0:T(128)} %bitcast.16.own_ref, s32[1]{0:T(128)} %bitcast.7.channel_ref.part_ref, s32[1]{0:T(128)} %constant.158.clone.1.turn_ref.swap_ref.part_ref, s32[128]{0:T(128)} %bitcast.52, ...), custom_call_target="tpu_custom_call" | custom-call | tf_op jit(solution)/shard_map/pack_tiles/pallas_call | solution.py:105
  4.0 1.3 copy-done.4
  5.3 7.5 %all-to-all-start = ((bf16[16,2,4,64,128]{4,3,2,1,0:T(8,128)(2,1)}), bf16[16,2,4,64,128]{4,3,2,1,0:T(8,128)(2,1)S(1)}, u32[]{:S(2)}, u32[]{:S(2)}) async-start(bf16[16,2,4,64,128]{4,3,2,1,0:T(8,128)(2,1)} %bitcast.50), calls=%async_computation | async-start | bytes 4194304 | tf_op jit(solution)/shard_map/all_to_all | solution.py:660
  12.7 3.2 %collective-permute-start.14 = (bf16[2,4,64,128]{3,2,1,0:T(8,128)(2,1)S(1)}, bf16[2,4,64,128]{3,2,1,0:T(8,128)(2,1)S(1)}, u32[]{:S(2)}, u32[]{:S(2)}) collective-permute-start(bf16[2,4,64,128]{3,2,1,0:T(8,128)(2,1)S(1)} %get-tuple-element.280.refs_0_), channel_id=1, source_target_pairs={{0,6},{1,7},{2,4},{3,5},{4,2},{5,3},{6,0},{7,1},{8,14},{9,15},{10,... | collective-permute-start | bytes 393224 | tf_op jit(solution)/shard_map/ppermute | solution.py:641
  16.3 4.1 %collective-permute-start.15 = (bf16[2,4,64,128]{3,2,1,0:T(8,128)(2,1)S(1)}, bf16[2,4,64,128]{3,2,1,0:T(8,128)(2,1)S(1)}, u32[]{:S(2)}, u32[]{:S(2)}) collective-permute-start(bf16[2,4,64,128]{3,2,1,0:T(8,128)(2,1)S(1)} %get-tuple-element.281), channel_id=1, source_target_pairs={{0,14},{1,15},{2,12},{3,13},{4,10},{5,11},{6,8},{7,9},{8,6},{9,7},... | collective-permute-start | bytes 393224 | tf_op jit(solution)/shard_map/ppermute | solution.py:641
  23.6 30.0 %collective-permute-done.14.refs_6_ = bf16[2,4,64,128]{3,2,1,0:T(8,128)(2,1)S(1)} collective-permute-done((bf16[2,4,64,128]{3,2,1,0:T(8,128)(2,1)S(1)}, bf16[2,4,64,128]{3,2,1,0:T(8,128)(2,1)S(1)}, u32[]{:S(2)}, u32[]{:S(2)}) %collective-permute-start.14) | collective-permute-done | bytes 131104 | tf_op jit(solution)/shard_map/ppermute | solution.py:641
  53.5 22.5 %collective-permute-start.11 = (bf16[2,4,64,128]{3,2,1,0:T(8,128)(2,1)S(1)}, bf16[2,4,64,128]{3,2,1,0:T(8,128)(2,1)S(1)}, u32[]{:S(2)}, u32[]{:S(2)}) collective-permute-start(bf16[2,4,64,128]{3,2,1,0:T(8,128)(2,1)S(1)} %get-tuple-element.281), channel_id=1, source_target_pairs={{0,10},{1,11},{2,8},{3,9},{4,14},{5,15},{6,12},{7,13},{8,2},{9,3},... | collective-permute-start | bytes 393224 | tf_op jit(solution)/shard_map/ppermute | solution.py:641
  76.0 1.6 collective-permute-done.12.refs_4_
  81.8 3.6 %collective-permute-done.13.refs_5_ = bf16[2,4,64,128]{3,2,1,0:T(8,128)(2,1)S(1)} collective-permute-done((bf16[2,4,64,128]{3,2,1,0:T(8,128)(2,1)S(1)}, bf16[2,4,64,128]{3,2,1,0:T(8,128)(2,1)S(1)}, u32[]{:S(2)}, u32[]{:S(2)}) %collective-permute-start.13) | collective-permute-done | bytes 131104 | tf_op jit(solution)/shard_map/ppermute | solution.py:641
  95.3 1.3 dynamic_slice.47.backdrop_ref
  99.9 5.1 %band_matrices.1 = (bf16[256,128]{1,0:T(8,128)(2,1)S(1)}, bf16[128,256]{1,0:T(8,128)(2,1)S(1)}, bf16[128,384]{1,0:T(8,128)(2,1)S(1)}, bf16[128,256]{1,0:T(8,128)...) custom-call(s32[2]{0:T(128)S(1)} %pad_add_fusion.place_ref, ...), custom_call_target="tpu_custom_call" | custom-call | tf_op jit(solution)/shard_map/band_matrices/pallas_call | solution.py:599
  112.6 4.6 %gather_planes.1 = (f32[67,128,128]{2,1,0:T(8,128)}, f32[12,128,128]{2,1,0:T(8,128)}) custom-call(s32[1]{0:T(128)} %bitcast.7.channel_ref.part_ref, s32[16]{0:T(128)S(1)} %sub.32.starts_ref, s32[16]{0:T(128)S(1)} %reshape.105.spill_starts_ref, bf16[2,16,4,64,128]{4,3,2,1,0:T(8,128)(2,1)S(1)} %bitcast.47, bf16[4,2,2,4,64,128]{5,4,3,2,1,0:T(8,128)(2,1)S(1)} %bitcast.49, ...), custom_call_target="tpu_custom_call" | custom-call | tf_op jit(solution)/shard_map/gather_planes/pallas_call | solution.py:163
  118.5 1.9 collective-permute-start.17
  120.4 5.6 %deskew.1 = (f32[128,64,128]{2,1,0:T(8,128)S(1)}, bf16[128,64,128]{2,1,0:T(8,128)(2,1)S(1)}, bf16[128,16,128]{2,1,0:T(8,128)(2,1)S(1)}, bf16[128,16,128]{2,1,0:T(8,128)(2,1)S(1)}) custom-call(s32[1]{0:T(128)} %bitcast.8.odd_ref, f32[1]{0:T(128)} %dynamic_slice.47.backdrop_ref, s32[128]{0:T(128)S(1)} %get-tuple-element.275.band_ref, ...), custom_call_target="tpu_custom_call" | custom-call | flops 5000000000 | bytes 12000000 | tf_op jit(solution)/shard_map/deskew/pallas_call | solution.py:249
  126.0 2.4 deskew_more.1
  129.1 3.0 %collective-permute-start.20 = (bf16[128,16,128]{2,1,0:T(8,128)(2,1)S(1)}, bf16[128,16,128]{2,1,0:T(8,128)(2,1)S(1)}, u32[]{:S(2)}, u32[]{:S(2)}) collective-permute-start(bf16[128,16,128]{2,1,0:T(8,128)(2,1)S(1)} %get-tuple-element.296), channel_id=1, source_target_pairs={{1,2},{2,1},{3,4},{4,3},{5,6},{6,5},{9,10},{10,9},{11,12},{12,11},... | collective-permute-start | bytes 1572872 | tf_op jit(solution)/shard_map/ppermute | solution.py:492
  132.1 3.7 %collective-permute-start.23 = (bf16[16,16,128]{2,1,0:T(8,128)(2,1)S(1)}, bf16[16,16,128]{2,1,0:T(8,128)(2,1)S(1)}, u32[]{:S(2)}, u32[]{:S(2)}) collective-permute-start(bf16[16,16,128]{2,1,0:T(8,128)(2,1)S(1)} %constant_dynamic-slice_fusion.9), channel_id=1, source_target_pairs={{1,18},{2,17},{3,20},{4,19},{5,22},{6,21},{9,26},{10,25},{11,28},{... | collective-permute-start | bytes 196616 | tf_op jit(solution)/shard_map/ppermute | solution.py:498
  136.2 4.0 %blur_inner.4.inner_ref = f32[9216,128]{1,0:T(8,128)S(1)} custom-call(bf16[128,64,128]{2,1,0:T(8,128)(2,1)S(1)} %get-tuple-element.291.own_ref, bf16[256,128]{1,0:T(8,128)(2,1)S(1)} %copy-done.24, bf16[128,256]{1,0:T(8,128)(2,1)S(1)} %copy-done.28, bf16[128,384]{1,0:T(8,128)(2,1)S(1)} %copy-done.16), custom_call_target="tpu_custom_call" | custom-call | flops 20000000000 | bytes 8000000 | tf_op jit(solution)/shard_map/blur_inner/pallas_call | solution.py:432
  140.3 1.6 constant_dynamic-slice_fusion.12
  141.9 2.7 collective-permute-done.21.side_ref
  144.6 5.2 %blur_quotient.2 = (bf16[128,64,128]{2,1,0:T(8,128)(2,1)S(1)}, bf16[128,16,128]{2,1,0:T(8,128)(2,1)S(1)}, bf16[128,16,128]{2,1,0:T(8,128)(2,1)S(1)}) custom-call(s32[1]{0:T(128)} %bitcast.8.odd_ref, s32[1]{0:T(128)} %constant.158.clone.1.turn_ref.swap_ref.part_ref, f32[1]{0:T(128)} %dynamic_slice.47.backdrop_ref, f32[9216,128]{1,0:T(8,128)S(1)} %blur_inner.4.inner_ref, ...), custom_call_target="tpu_custom_call" | custom-call | flops 10000000000 | bytes 16000000 | tf_op jit(solution)/shard_map/blur_quotient/pallas_call | solution.py:454
  149.8 1.6 collective-permute-start.24
  151.4 4.3 %collective-permute-start.25 = (bf16[128,16,128]{2,1,0:T(8,128)(2,1)S(1)}, bf16[128,16,128]{2,1,0:T(8,128)(2,1)S(1)}, u32[]{:S(2)}, u32[]{:S(2)}) collective-permute-start(bf16[128,16,128]{2,1,0:T(8,128)(2,1)S(1)} %get-tuple-element.307), channel_id=1, source_target_pairs={{1,2},{2,1},{3,4},{4,3},{5,6},{6,5},{9,10},{10,9},{11,12},{12,11},... | collective-permute-start | bytes 1572872 | tf_op jit(solution)/shard_map/ppermute | solution.py:492
  155.7 1.9 collective-permute-start.28
  159.0 4.7 %blur_inner.5.inner_ref = f32[9216,128]{1,0:T(8,128)S(1)} custom-call(bf16[128,64,128]{2,1,0:T(8,128)(2,1)S(1)} %get-tuple-element.302.own_ref, bf16[256,128]{1,0:T(8,128)(2,1)S(1)} %copy-done.18, bf16[128,256]{1,0:T(8,128)(2,1)S(1)} %copy-done.22, bf16[128,384]{1,0:T(8,128)(2,1)S(1)} %get-tuple-element.305.my_ref), custom_call_target="tpu_custom_call" | custom-call | flops 20000000000 | bytes 8000000 | tf_op jit(solution)/shard_map/blur_inner/pallas_call | solution.py:432
  163.8 3.0 %collective-permute-done.26.side_ref = bf16[16,64,128]{2,1,0:T(8,128)(2,1)S(1)} collective-permute-done((bf16[16,64,128]{2,1,0:T(8,128)(2,1)S(1)}, bf16[16,64,128]{2,1,0:T(8,128)(2,1)S(1)}, u32[]{:S(2)}, u32[]{:S(2)}) %collective-permute-start.26) | collective-permute-done | bytes 262176 | tf_op jit(solution)/shard_map/ppermute | solution.py:495
  166.9 6.1 %blur_estimate.2 = (f32[128,64,128]{2,1,0:T(8,128)S(1)}, f32[64,128]{1,0:T(8,128)}, bf16[128,64,128]{2,1,0:T(8,128)(2,1)S(1)}, bf16[128,16,128]{2,1,0:T(8,128)(2,1)S(1)}, bf16[128,16,128]{2,1,0:T(8,128)(2,1)S(1)}) custom-call(s32[1]{0:T(128)} %bitcast.8.odd_ref, s32[1]{0:T(128)} %constant.158.clone.1.turn_ref.swap_ref.part_ref, ...), custom_call_target="tpu_custom_call" | custom-call | flops 10000000000 | bytes 16000000 | tf_op jit(solution)/shard_map/blur_estimate/pallas_call | solution.py:454
  172.9 1.4 collective-permute-start.29
  174.3 4.5 %collective-permute-start.30 = (bf16[128,16,128]{2,1,0:T(8,128)(2,1)S(1)}, bf16[128,16,128]{2,1,0:T(8,128)(2,1)S(1)}, u32[]{:S(2)}, u32[]{:S(2)}) collective-permute-start(bf16[128,16,128]{2,1,0:T(8,128)(2,1)S(1)} %get-tuple-element.315), channel_id=1, source_target_pairs={{1,2},{2,1},{3,4},{4,3},{5,6},{6,5},{9,10},{10,9},{11,12},{12,11},... | collective-permute-start | bytes 1572872 | tf_op jit(solution)/shard_map/ppermute | solution.py:492
  178.8 3.1 %collective-permute-start.33 = (bf16[16,16,128]{2,1,0:T(8,128)(2,1)S(1)}, bf16[16,16,128]{2,1,0:T(8,128)(2,1)S(1)}, u32[]{:S(2)}, u32[]{:S(2)}) collective-permute-start(bf16[16,16,128]{2,1,0:T(8,128)(2,1)S(1)} %constant_dynamic-slice_fusion.3), channel_id=1, source_target_pairs={{1,18},{2,17},{3,20},{4,19},{5,22},{6,21},{9,26},{10,25},{11,28},{... | collective-permute-start | bytes 196616 | tf_op jit(solution)/shard_map/ppermute | solution.py:498
  182.4 4.0 %blur_inner.6.inner_ref = f32[9216,128]{1,0:T(8,128)S(1)} custom-call(bf16[128,64,128]{2,1,0:T(8,128)(2,1)S(1)} %get-tuple-element.313.own_ref, bf16[256,128]{1,0:T(8,128)(2,1)S(1)} %copy-done.24, bf16[128,256]{1,0:T(8,128)(2,1)S(1)} %copy-done.28, bf16[128,384]{1,0:T(8,128)(2,1)S(1)} %copy-done.16), custom_call_target="tpu_custom_call" | custom-call | flops 20000000000 | bytes 8000000 | tf_op jit(solution)/shard_map/blur_inner/pallas_call | solution.py:432
  187.5 3.2 %collective-permute-done.31.side_ref = bf16[16,64,128]{2,1,0:T(8,128)(2,1)S(1)} collective-permute-done((bf16[16,64,128]{2,1,0:T(8,128)(2,1)S(1)}, bf16[16,64,128]{2,1,0:T(8,128)(2,1)S(1)}, u32[]{:S(2)}, u32[]{:S(2)}) %collective-permute-start.31) | collective-permute-done | bytes 262176 | tf_op jit(solution)/shard_map/ppermute | solution.py:495
  190.7 5.2 %blur_quotient.3 = (bf16[128,64,128]{2,1,0:T(8,128)(2,1)S(1)}, bf16[128,16,128]{2,1,0:T(8,128)(2,1)S(1)}, bf16[128,16,128]{2,1,0:T(8,128)(2,1)S(1)}) custom-call(s32[1]{0:T(128)} %bitcast.8.odd_ref, s32[1]{0:T(128)} %constant.158.clone.1.turn_ref.swap_ref.part_ref, f32[1]{0:T(128)} %dynamic_slice.47.backdrop_ref, f32[9216,128]{1,0:T(8,128)S(1)} %blur_inner.6.inner_ref, ...), custom_call_target="tpu_custom_call" | custom-call | flops 10000000000 | bytes 16000000 | tf_op jit(solution)/shard_map/blur_quotient/pallas_call | solution.py:454
  195.9 1.6 collective-permute-start.34
  197.5 4.8 %collective-permute-start.35 = (bf16[128,16,128]{2,1,0:T(8,128)(2,1)S(1)}, bf16[128,16,128]{2,1,0:T(8,128)(2,1)S(1)}, u32[]{:S(2)}, u32[]{:S(2)}) collective-permute-start(bf16[128,16,128]{2,1,0:T(8,128)(2,1)S(1)} %get-tuple-element.318), channel_id=1, source_target_pairs={{1,2},{2,1},{3,4},{4,3},{5,6},{6,5},{9,10},{10,9},{11,12},{12,11},... | collective-permute-start | bytes 1572872 | tf_op jit(solution)/shard_map/ppermute | solution.py:492
  202.4 1.9 collective-permute-start.38
  205.7 4.7 %blur_inner.7.inner_ref = f32[9216,128]{1,0:T(8,128)S(1)} custom-call(bf16[128,64,128]{2,1,0:T(8,128)(2,1)S(1)} %get-tuple-element.316.own_ref, bf16[256,128]{1,0:T(8,128)(2,1)S(1)} %copy-done.18, bf16[128,256]{1,0:T(8,128)(2,1)S(1)} %copy-done.22, bf16[128,384]{1,0:T(8,128)(2,1)S(1)} %get-tuple-element.305.my_ref), custom_call_target="tpu_custom_call" | custom-call | flops 20000000000 | bytes 8000000 | tf_op jit(solution)/shard_map/blur_inner/pallas_call | solution.py:432
  210.8 2.8 collective-permute-done.36.side_ref
  213.5 7.2 %blur_estimate.3 = (f32[128,64,128]{2,1,0:T(8,128)S(1)}, f32[64,128]{1,0:T(8,128)S(1)}, bf16[128,64,128]{2,1,0:T(8,128)(2,1)}, bf16[128,16,128]{2,1,0:T(8,128)(2,1)}, bf16[128,16,128]{2,1,0:T(8,128)(2,1)}) custom-call(s32[1]{0:T(128)} %bitcast.8.odd_ref, s32[1]{0:T(128)} %bitcast.21.swap_ref, f32[1]{0:T(128)} %dynamic_slice.47.backdrop_ref, ...), custom_call_target="tpu_custom_call" | custom-call | flops 10000000000 | bytes 16000000 | tf_op jit(solution)/shard_map/blur_estimate/pallas_call | solution.py:454
  220.7 2.0 copy-done.2
  224.1 2.0 multiply_convert_fusion
  226.9 1.3 place_own.2.partial_ref
  228.2 1.6 copy-done.3
  229.8 1.3 place_own.3.partial_ref
  231.2 25.8 %collective-permute-done.18.other_ref = f32[64,64,128]{2,1,0:T(8,128)S(1)} collective-permute-done((f32[64,64,128]{2,1,0:T(8,128)}, f32[64,64,128]{2,1,0:T(8,128)S(1)}, u32[]{:S(2)}, u32[]{:S(2)}) %collective-permute-start.18) | collective-permute-done | bytes 2097184 | tf_op jit(solution)/shard_map/ppermute | solution.py:612
  256.9 1.3 place_other.2
  258.3 21.5 %collective-permute-done.39 = f16[65,64,128]{2,1,0:T(8,128)(2,1)S(1)} collective-permute-done((f16[65,64,128]{2,1,0:T(8,128)(2,1)S(1)}, f16[65,64,128]{2,1,0:T(8,128)(2,1)S(1)}, u32[]{:S(2)}, u32[]{:S(2)}) %collective-permute-start.39) | collective-permute-done | bytes 1064992 | tf_op jit(solution)/shard_map/ppermute | solution.py:612
  281.1 1.3 place_other.3
  (186 shorter events, 36.7 us)
Async XLA Ops:
  5.3 15.6 %copy-start.37 = (s32[128,1]{0,1:T(1,128)S(1)}, s32[128,1]{0,1:T(1,128)}, u32[]{:S(2)}) copy-start(s32[128,1]{0,1:T(1,128)} %param.12) | copy-start | bytes 1540
  5.3 16.8 %copy-start.42 = (s32[64]{0:T(128)S(1)}, s32[64]{0:T(128)}, u32[]{:S(2)}) copy-start(s32[64]{0:T(128)} %param.14) | copy-start | bytes 772
  5.3 16.8 %copy-start.44 = (s32[128]{0:T(128)S(1)}, s32[128]{0:T(128)}, u32[]{:S(2)}) copy-start(s32[128]{0:T(128)} %param.13) | copy-start | bytes 1540
  5.3 18.1 %copy-start.43 = (bf16[64,2]{0,1:T(2,128)(2,1)S(1)}, bf16[64,2]{0,1:T(2,128)(2,1)}, u32[]{:S(2)}) copy-start(bf16[64,2]{0,1:T(2,128)(2,1)} %param.15) | copy-start | bytes 772
  5.3 107.3 %all-to-all-start = ((bf16[16,2,4,64,128]{4,3,2,1,0:T(8,128)(2,1)}), bf16[16,2,4,64,128]{4,3,2,1,0:T(8,128)(2,1)S(1)}, u32[]{:S(2)}, u32[]{:S(2)}) async-start(bf16[16,2,4,64,128]{4,3,2,1,0:T(8,128)(2,1)} %bitcast.50), calls=%async_computation | async-start | bytes 4194304 | tf_op jit(solution)/shard_map/all_to_all | solution.py:660
  12.7 40.8 %collective-permute-start.14 = (bf16[2,4,64,128]{3,2,1,0:T(8,128)(2,1)S(1)}, bf16[2,4,64,128]{3,2,1,0:T(8,128)(2,1)S(1)}, u32[]{:S(2)}, u32[]{:S(2)}) collective-permute-start(bf16[2,4,64,128]{3,2,1,0:T(8,128)(2,1)S(1)} %get-tuple-element.280.refs_0_), channel_id=1, source_target_pairs={{0,6},{1,7},{2,4},{3,5},{4,2},{5,3},{6,0},{7,1},{8,14},{9,15},{10,... | collective-permute-start | bytes 393224 | tf_op jit(solution)/shard_map/ppermute | solution.py:641
  15.9 61.8 %collective-permute-start.12 = (bf16[2,4,64,128]{3,2,1,0:T(8,128)(2,1)S(1)}, bf16[2,4,64,128]{3,2,1,0:T(8,128)(2,1)S(1)}, u32[]{:S(2)}, u32[]{:S(2)}) collective-permute-start(bf16[2,4,64,128]{3,2,1,0:T(8,128)(2,1)S(1)} %get-tuple-element.280.refs_0_), channel_id=1, source_target_pairs={{0,4},{1,5},{2,6},{3,7},{4,0},{5,1},{6,2},{7,3},{8,12},{9,13},{10,... | collective-permute-start | bytes 393224 | tf_op jit(solution)/shard_map/ppermute | solution.py:641
  15.9 64.4 %collective-permute-start.10 = (bf16[2,4,64,128]{3,2,1,0:T(8,128)(2,1)S(1)}, bf16[2,4,64,128]{3,2,1,0:T(8,128)(2,1)S(1)}, u32[]{:S(2)}, u32[]{:S(2)}) collective-permute-start(bf16[2,4,64,128]{3,2,1,0:T(8,128)(2,1)S(1)} %get-tuple-element.280.refs_0_), channel_id=1, source_target_pairs={{0,2},{1,3},{2,0},{3,1},{4,6},{5,7},{6,4},{7,5},{8,10},{9,11},{10,... | collective-permute-start | bytes 393224 | tf_op jit(solution)/shard_map/ppermute | solution.py:641
  16.3 64.9 %collective-permute-start.15 = (bf16[2,4,64,128]{3,2,1,0:T(8,128)(2,1)S(1)}, bf16[2,4,64,128]{3,2,1,0:T(8,128)(2,1)S(1)}, u32[]{:S(2)}, u32[]{:S(2)}) collective-permute-start(bf16[2,4,64,128]{3,2,1,0:T(8,128)(2,1)S(1)} %get-tuple-element.281), channel_id=1, source_target_pairs={{0,14},{1,15},{2,12},{3,13},{4,10},{5,11},{6,8},{7,9},{8,6},{9,7},... | collective-permute-start | bytes 393224 | tf_op jit(solution)/shard_map/ppermute | solution.py:641
  20.3 65.1 %collective-permute-start.13 = (bf16[2,4,64,128]{3,2,1,0:T(8,128)(2,1)S(1)}, bf16[2,4,64,128]{3,2,1,0:T(8,128)(2,1)S(1)}, u32[]{:S(2)}, u32[]{:S(2)}) collective-permute-start(bf16[2,4,64,128]{3,2,1,0:T(8,128)(2,1)S(1)} %get-tuple-element.281), channel_id=1, source_target_pairs={{0,12},{1,13},{2,14},{3,15},{4,8},{5,9},{6,10},{7,11},{8,4},{9,5},... | collective-permute-start | bytes 393224 | tf_op jit(solution)/shard_map/ppermute | solution.py:641
  22.1 64.0 %copy-start.41 = (f32[64,1]{0,1:T(1,128)}, f32[64,1]{0,1:T(1,128)S(1)}, u32[]{:S(2)}) copy-start(f32[64,1]{0,1:T(1,128)S(1)} %convert_bitcast_fusion.1) | copy-start | bytes 772
  22.8 63.4 %copy-start.38 = (pred[8,16]{1,0:T(8,128)(4,1)}, pred[8,16]{1,0:T(8,128)(4,1)S(1)}, u32[]{:S(2)}) copy-start(pred[8,16]{1,0:T(8,128)(4,1)S(1)} %get-tuple-element.349) | copy-start | bytes 388
  23.4 62.8 %copy-start.40 = (f32[64,2]{0,1:T(2,128)}, f32[64,2]{0,1:T(2,128)S(1)}, u32[]{:S(2)}) copy-start(f32[64,2]{0,1:T(2,128)S(1)} %convert_element_type.41) | copy-start | bytes 1540
  53.5 32.6 %collective-permute-start.11 = (bf16[2,4,64,128]{3,2,1,0:T(8,128)(2,1)S(1)}, bf16[2,4,64,128]{3,2,1,0:T(8,128)(2,1)S(1)}, u32[]{:S(2)}, u32[]{:S(2)}) collective-permute-start(bf16[2,4,64,128]{3,2,1,0:T(8,128)(2,1)S(1)} %get-tuple-element.281), channel_id=1, source_target_pairs={{0,10},{1,11},{2,8},{3,9},{4,14},{5,15},{6,12},{7,13},{8,2},{9,3},... | collective-permute-start | bytes 393224 | tf_op jit(solution)/shard_map/ppermute | solution.py:641
  77.7 9.5 %collective-permute-start.9 = (bf16[2,4,64,128]{3,2,1,0:T(8,128)(2,1)S(1)}, bf16[2,4,64,128]{3,2,1,0:T(8,128)(2,1)S(1)}, u32[]{:S(2)}, u32[]{:S(2)}) collective-permute-start(bf16[2,4,64,128]{3,2,1,0:T(8,128)(2,1)S(1)} %get-tuple-element.281), channel_id=1, source_target_pairs={{0,8},{1,9},{2,10},{3,11},{4,12},{5,13},{6,14},{7,15},{8,0},{9,1},... | collective-permute-start | bytes 393224 | tf_op jit(solution)/shard_map/ppermute | solution.py:641
  80.9 30.9 %collective-permute-start.8 = (f32[64,3]{0,1:T(4,128)}, f32[64,3]{0,1:T(4,128)}, u32[]{:S(2)}, u32[]{:S(2)}) collective-permute-start(f32[64,3]{0,1:T(4,128)} %pad_maximum_fusion.1), channel_id=1, source_target_pairs={{0,8},{8,0},{16,24},{24,16},{1,9},{9,1},{17,25},{25,17},{2,10},{10... | collective-permute-start | bytes 2312 | tf_op jit(solution)/shard_map/ppermute | solution.py:612
  92.4 20.2 %collective-permute-start.16 = (bf16[4,2,2,4,64,128]{5,4,3,2,1,0:T(8,128)(2,1)S(1)}, bf16[4,2,2,4,64,128]{5,4,3,2,1,0:T(8,128)(2,1)}, u32[]{:S(2)}, u32[]{:S(2)}) collective-permute-start(bf16[4,2,2,4,64,128]{5,4,3,2,1,0:T(8,128)(2,1)S(1)} %bitcast.48), channel_id=1, source_target_pairs={{0,1},{1,0},{2,3},{3,2},{4,5},{5,4},{6,7},{7,6},{8,9},{9,8},{10,11... | collective-permute-start | bytes 3145736 | tf_op jit(solution)/shard_map/ppermute | solution.py:645
  118.5 7.5 %collective-permute-start.17 = (f16[12,128,128]{2,1,0:T(8,128)(2,1)S(1)}, f16[12,128,128]{2,1,0:T(8,128)(2,1)S(1)}, u32[]{:S(2)}, u32[]{:S(2)}) collective-permute-start(f16[12,128,128]{2,1,0:T(8,128)(2,1)S(1)} %convert_element_type.46), channel_id=1, source_target_pairs={{0,1},{1,2},{2,3},{3,4},{4,5},{5,6},{6,7},{8,9},{9,10},{10,11},{11... | collective-permute-start | bytes 1179656 | tf_op jit(solution)/shard_map/ppermute | solution.py:724
  126.0 10.2 %copy-start.16 = (bf16[128,384]{1,0:T(8,128)(2,1)S(1)}, bf16[128,384]{1,0:T(8,128)(2,1)}, u32[]{:S(2)}) copy-start(bf16[128,384]{1,0:T(8,128)(2,1)} %copy-done.15) | copy-start | bytes 294916
  126.0 10.2 %copy-start.24 = (bf16[256,128]{1,0:T(8,128)(2,1)S(1)}, bf16[256,128]{1,0:T(8,128)(2,1)}, u32[]{:S(2)}) copy-start(bf16[256,128]{1,0:T(8,128)(2,1)} %copy-done.23) | copy-start | bytes 196612
  126.0 10.2 %copy-start.28 = (bf16[128,256]{1,0:T(8,128)(2,1)S(1)}, bf16[128,256]{1,0:T(8,128)(2,1)}, u32[]{:S(2)}) copy-start(bf16[128,256]{1,0:T(8,128)(2,1)} %copy-done.27) | copy-start | bytes 196612
  128.5 62.2 %copy-start = (f32[128,64,128]{2,1,0:T(8,128)}, f32[128,64,128]{2,1,0:T(8,128)S(1)}, u32[]{:S(2)}) copy-start(f32[128,64,128]{2,1,0:T(8,128)S(1)} %get-tuple-element.290.both_ref.point_ref) | copy-start | bytes 12582916
  128.5 16.1 %collective-permute-start.19 = (bf16[128,16,128]{2,1,0:T(8,128)(2,1)S(1)}, bf16[128,16,128]{2,1,0:T(8,128)(2,1)S(1)}, u32[]{:S(2)}, u32[]{:S(2)}) collective-permute-start(bf16[128,16,128]{2,1,0:T(8,128)(2,1)S(1)} %get-tuple-element.295), channel_id=1, source_target_pairs={{0,1},{1,0},{2,3},{3,2},{4,5},{5,4},{6,7},{7,6},{8,9},{9,8},{10,11... | collective-permute-start | bytes 1572872 | tf_op jit(solution)/shard_map/ppermute | solution.py:492
  129.1 15.5 %collective-permute-start.20 = (bf16[128,16,128]{2,1,0:T(8,128)(2,1)S(1)}, bf16[128,16,128]{2,1,0:T(8,128)(2,1)S(1)}, u32[]{:S(2)}, u32[]{:S(2)}) collective-permute-start(bf16[128,16,128]{2,1,0:T(8,128)(2,1)S(1)} %get-tuple-element.296), channel_id=1, source_target_pairs={{1,2},{2,1},{3,4},{4,3},{5,6},{6,5},{9,10},{10,9},{11,12},{12,11},... | collective-permute-start | bytes 1572872 | tf_op jit(solution)/shard_map/ppermute | solution.py:492
  132.1 9.7 %collective-permute-start.23 = (bf16[16,16,128]{2,1,0:T(8,128)(2,1)S(1)}, bf16[16,16,128]{2,1,0:T(8,128)(2,1)S(1)}, u32[]{:S(2)}, u32[]{:S(2)}) collective-permute-start(bf16[16,16,128]{2,1,0:T(8,128)(2,1)S(1)} %constant_dynamic-slice_fusion.9), channel_id=1, source_target_pairs={{1,18},{2,17},{3,20},{4,19},{5,22},{6,21},{9,26},{10,25},{11,28},{... | collective-permute-start | bytes 196616 | tf_op jit(solution)/shard_map/ppermute | solution.py:498
  135.8 6.1 %collective-permute-start.22 = (bf16[16,16,128]{2,1,0:T(8,128)(2,1)S(1)}, bf16[16,16,128]{2,1,0:T(8,128)(2,1)S(1)}, u32[]{:S(2)}, u32[]{:S(2)}) collective-permute-start(bf16[16,16,128]{2,1,0:T(8,128)(2,1)S(1)} %constant_dynamic-slice_fusion.10), channel_id=1, source_target_pairs={{0,17},{1,16},{2,19},{3,18},{4,21},{5,20},{6,23},{7,22},{8,25},{9,... | collective-permute-start | bytes 196616 | tf_op jit(solution)/shard_map/ppermute | solution.py:498
  135.9 8.6 %collective-permute-start.21 = (bf16[16,64,128]{2,1,0:T(8,128)(2,1)S(1)}, bf16[16,64,128]{2,1,0:T(8,128)(2,1)S(1)}, u32[]{:S(2)}, u32[]{:S(2)}) collective-permute-start(bf16[16,64,128]{2,1,0:T(8,128)(2,1)S(1)} %constant_dynamic-slice_fusion.11), channel_id=1, source_target_pairs={{0,16},{8,24},{16,0},{24,8},{1,17},{9,25},{17,1},{25,9},{2,18},{10... | collective-permute-start | bytes 786440 | tf_op jit(solution)/shard_map/ppermute | solution.py:495
  141.9 17.2 %copy-start.18 = (bf16[256,128]{1,0:T(8,128)(2,1)S(1)}, bf16[256,128]{1,0:T(8,128)(2,1)}, u32[]{:S(2)}) copy-start(bf16[256,128]{1,0:T(8,128)(2,1)} %copy-done.17) | copy-start | bytes 196612
  141.9 17.2 %copy-start.22 = (bf16[128,256]{1,0:T(8,128)(2,1)S(1)}, bf16[128,256]{1,0:T(8,128)(2,1)}, u32[]{:S(2)}) copy-start(bf16[128,256]{1,0:T(8,128)(2,1)} %copy-done.21) | copy-start | bytes 196612
  149.8 17.0 %collective-permute-start.24 = (bf16[128,16,128]{2,1,0:T(8,128)(2,1)S(1)}, bf16[128,16,128]{2,1,0:T(8,128)(2,1)S(1)}, u32[]{:S(2)}, u32[]{:S(2)}) collective-permute-start(bf16[128,16,128]{2,1,0:T(8,128)(2,1)S(1)} %get-tuple-element.306), channel_id=1, source_target_pairs={{0,1},{1,0},{2,3},{3,2},{4,5},{5,4},{6,7},{7,6},{8,9},{9,8},{10,11... | collective-permute-start | bytes 1572872 | tf_op jit(solution)/shard_map/ppermute | solution.py:492
  151.4 15.4 %collective-permute-start.25 = (bf16[128,16,128]{2,1,0:T(8,128)(2,1)S(1)}, bf16[128,16,128]{2,1,0:T(8,128)(2,1)S(1)}, u32[]{:S(2)}, u32[]{:S(2)}) collective-permute-start(bf16[128,16,128]{2,1,0:T(8,128)(2,1)S(1)} %get-tuple-element.307), channel_id=1, source_target_pairs={{1,2},{2,1},{3,4},{4,3},{5,6},{6,5},{9,10},{10,9},{11,12},{12,11},... | collective-permute-start | bytes 1572872 | tf_op jit(solution)/shard_map/ppermute | solution.py:492
  155.7 8.1 %collective-permute-start.28 = (bf16[16,16,128]{2,1,0:T(8,128)(2,1)S(1)}, bf16[16,16,128]{2,1,0:T(8,128)(2,1)S(1)}, u32[]{:S(2)}, u32[]{:S(2)}) collective-permute-start(bf16[16,16,128]{2,1,0:T(8,128)(2,1)S(1)} %constant_dynamic-slice_fusion.6), channel_id=1, source_target_pairs={{1,18},{2,17},{3,20},{4,19},{5,22},{6,21},{9,26},{10,25},{11,28},{... | collective-permute-start | bytes 196616 | tf_op jit(solution)/shard_map/ppermute | solution.py:498
  157.6 6.1 %collective-permute-start.27 = (bf16[16,16,128]{2,1,0:T(8,128)(2,1)S(1)}, bf16[16,16,128]{2,1,0:T(8,128)(2,1)S(1)}, u32[]{:S(2)}, u32[]{:S(2)}) collective-permute-start(bf16[16,16,128]{2,1,0:T(8,128)(2,1)S(1)} %constant_dynamic-slice_fusion.7), channel_id=1, source_target_pairs={{0,17},{1,16},{2,19},{3,18},{4,21},{5,20},{6,23},{7,22},{8,25},{9,... | collective-permute-start | bytes 196616 | tf_op jit(solution)/shard_map/ppermute | solution.py:498
  157.7 9.1 %copy-start.20 = (bf16[128,256]{1,0:T(8,128)(2,1)S(1)}, bf16[128,256]{1,0:T(8,128)(2,1)}, u32[]{:S(2)}) copy-start(bf16[128,256]{1,0:T(8,128)(2,1)} %copy-done.19) | copy-start | bytes 196612
  157.8 9.1 %copy-start.30 = (bf16[64,192]{1,0:T(8,128)(2,1)S(1)}, bf16[64,192]{1,0:T(8,128)(2,1)}, u32[]{:S(2)}) copy-start(bf16[64,192]{1,0:T(8,128)(2,1)} %copy-done.29) | copy-start | bytes 73732
  157.8 9.0 %collective-permute-start.26 = (bf16[16,64,128]{2,1,0:T(8,128)(2,1)S(1)}, bf16[16,64,128]{2,1,0:T(8,128)(2,1)S(1)}, u32[]{:S(2)}, u32[]{:S(2)}) collective-permute-start(bf16[16,64,128]{2,1,0:T(8,128)(2,1)S(1)} %constant_dynamic-slice_fusion.8), channel_id=1, source_target_pairs={{0,16},{8,24},{16,0},{24,8},{1,17},{9,25},{17,1},{25,9},{2,18},{10... | collective-permute-start | bytes 786440 | tf_op jit(solution)/shard_map/ppermute | solution.py:495
  172.9 17.8 %collective-permute-start.29 = (bf16[128,16,128]{2,1,0:T(8,128)(2,1)S(1)}, bf16[128,16,128]{2,1,0:T(8,128)(2,1)S(1)}, u32[]{:S(2)}, u32[]{:S(2)}) collective-permute-start(bf16[128,16,128]{2,1,0:T(8,128)(2,1)S(1)} %get-tuple-element.314), channel_id=1, source_target_pairs={{0,1},{1,0},{2,3},{3,2},{4,5},{5,4},{6,7},{7,6},{8,9},{9,8},{10,11... | collective-permute-start | bytes 1572872 | tf_op jit(solution)/shard_map/ppermute | solution.py:492
  174.3 16.3 %collective-permute-start.30 = (bf16[128,16,128]{2,1,0:T(8,128)(2,1)S(1)}, bf16[128,16,128]{2,1,0:T(8,128)(2,1)S(1)}, u32[]{:S(2)}, u32[]{:S(2)}) collective-permute-start(bf16[128,16,128]{2,1,0:T(8,128)(2,1)S(1)} %get-tuple-element.315), channel_id=1, source_target_pairs={{1,2},{2,1},{3,4},{4,3},{5,6},{6,5},{9,10},{10,9},{11,12},{12,11},... | collective-permute-start | bytes 1572872 | tf_op jit(solution)/shard_map/ppermute | solution.py:492
  178.8 8.6 %collective-permute-start.33 = (bf16[16,16,128]{2,1,0:T(8,128)(2,1)S(1)}, bf16[16,16,128]{2,1,0:T(8,128)(2,1)S(1)}, u32[]{:S(2)}, u32[]{:S(2)}) collective-permute-start(bf16[16,16,128]{2,1,0:T(8,128)(2,1)S(1)} %constant_dynamic-slice_fusion.3), channel_id=1, source_target_pairs={{1,18},{2,17},{3,20},{4,19},{5,22},{6,21},{9,26},{10,25},{11,28},{... | collective-permute-start | bytes 196616 | tf_op jit(solution)/shard_map/ppermute | solution.py:498
  181.9 5.5 %collective-permute-start.32 = (bf16[16,16,128]{2,1,0:T(8,128)(2,1)S(1)}, bf16[16,16,128]{2,1,0:T(8,128)(2,1)S(1)}, u32[]{:S(2)}, u32[]{:S(2)}) collective-permute-start(bf16[16,16,128]{2,1,0:T(8,128)(2,1)S(1)} %constant_dynamic-slice_fusion.4), channel_id=1, source_target_pairs={{0,17},{1,16},{2,19},{3,18},{4,21},{5,20},{6,23},{7,22},{8,25},{9,... | collective-permute-start | bytes 196616 | tf_op jit(solution)/shard_map/ppermute | solution.py:498
  182.1 8.6 %collective-permute-start.31 = (bf16[16,64,128]{2,1,0:T(8,128)(2,1)S(1)}, bf16[16,64,128]{2,1,0:T(8,128)(2,1)S(1)}, u32[]{:S(2)}, u32[]{:S(2)}) collective-permute-start(bf16[16,64,128]{2,1,0:T(8,128)(2,1)S(1)} %constant_dynamic-slice_fusion.5), channel_id=1, source_target_pairs={{0,16},{8,24},{16,0},{24,8},{1,17},{9,25},{17,1},{25,9},{2,18},{10... | collective-permute-start | bytes 786440 | tf_op jit(solution)/shard_map/ppermute | solution.py:495
  195.9 17.6 %collective-permute-start.34 = (bf16[128,16,128]{2,1,0:T(8,128)(2,1)S(1)}, bf16[128,16,128]{2,1,0:T(8,128)(2,1)S(1)}, u32[]{:S(2)}, u32[]{:S(2)}) collective-permute-start(bf16[128,16,128]{2,1,0:T(8,128)(2,1)S(1)} %get-tuple-element.317), channel_id=1, source_target_pairs={{0,1},{1,0},{2,3},{3,2},{4,5},{5,4},{6,7},{7,6},{8,9},{9,8},{10,11... | collective-permute-start | bytes 1572872 | tf_op jit(solution)/shard_map/ppermute | solution.py:492
  197.5 16.0 %collective-permute-start.35 = (bf16[128,16,128]{2,1,0:T(8,128)(2,1)S(1)}, bf16[128,16,128]{2,1,0:T(8,128)(2,1)S(1)}, u32[]{:S(2)}, u32[]{:S(2)}) collective-permute-start(bf16[128,16,128]{2,1,0:T(8,128)(2,1)S(1)} %get-tuple-element.318), channel_id=1, source_target_pairs={{1,2},{2,1},{3,4},{4,3},{5,6},{6,5},{9,10},{10,9},{11,12},{12,11},... | collective-permute-start | bytes 1572872 | tf_op jit(solution)/shard_map/ppermute | solution.py:492
  202.4 8.0 %collective-permute-start.38 = (bf16[16,16,128]{2,1,0:T(8,128)(2,1)S(1)}, bf16[16,16,128]{2,1,0:T(8,128)(2,1)S(1)}, u32[]{:S(2)}, u32[]{:S(2)}) collective-permute-start(bf16[16,16,128]{2,1,0:T(8,128)(2,1)S(1)} %constant_dynamic-slice_fusion), channel_id=1, source_target_pairs={{1,18},{2,17},{3,20},{4,19},{5,22},{6,21},{9,26},{10,25},{11,28},{... | collective-permute-start | bytes 196616 | tf_op jit(solution)/shard_map/ppermute | solution.py:498
  204.3 6.4 %collective-permute-start.37 = (bf16[16,16,128]{2,1,0:T(8,128)(2,1)S(1)}, bf16[16,16,128]{2,1,0:T(8,128)(2,1)S(1)}, u32[]{:S(2)}, u32[]{:S(2)}) collective-permute-start(bf16[16,16,128]{2,1,0:T(8,128)(2,1)S(1)} %constant_dynamic-slice_fusion.1), channel_id=1, source_target_pairs={{0,17},{1,16},{2,19},{3,18},{4,21},{5,20},{6,23},{7,22},{8,25},{9,... | collective-permute-start | bytes 196616 | tf_op jit(solution)/shard_map/ppermute | solution.py:498
  204.4 9.1 %collective-permute-start.36 = (bf16[16,64,128]{2,1,0:T(8,128)(2,1)S(1)}, bf16[16,64,128]{2,1,0:T(8,128)(2,1)S(1)}, u32[]{:S(2)}, u32[]{:S(2)}) collective-permute-start(bf16[16,64,128]{2,1,0:T(8,128)(2,1)S(1)} %constant_dynamic-slice_fusion.2), channel_id=1, source_target_pairs={{0,16},{8,24},{16,0},{24,8},{1,17},{9,25},{17,1},{25,9},{2,18},{10... | collective-permute-start | bytes 786440 | tf_op jit(solution)/shard_map/ppermute | solution.py:495
  210.4 46.5 %collective-permute-start.18 = (f32[64,64,128]{2,1,0:T(8,128)}, f32[64,64,128]{2,1,0:T(8,128)S(1)}, u32[]{:S(2)}, u32[]{:S(2)}) collective-permute-start(f32[64,64,128]{2,1,0:T(8,128)} %constant_dynamic-slice_fusion.12), channel_id=1, source_target_pairs={{0,8},{8,0},{16,24},{24,16},{1,9},{9,1},{17,25},{25,17},{2,10},{10... | collective-permute-start | bytes 6291464 | tf_op jit(solution)/shard_map/ppermute | solution.py:612
  226.4 53.3 %collective-permute-start.39 = (f16[65,64,128]{2,1,0:T(8,128)(2,1)S(1)}, f16[65,64,128]{2,1,0:T(8,128)(2,1)S(1)}, u32[]{:S(2)}, u32[]{:S(2)}) collective-permute-start(f16[65,64,128]{2,1,0:T(8,128)(2,1)S(1)} %concatenate.11), channel_id=1, source_target_pairs={{0,8},{8,0},{16,24},{24,16},{1,9},{9,1},{17,25},{25,17},{2,10},{10... | collective-permute-start | bytes 3194888 | tf_op jit(solution)/shard_map/ppermute | solution.py:612
  (30 other events, 50.3 us)

commit v4 on v3

--- a/solution.py
+++ b/solution.py
@@ -37,8 +37,7 @@
     copy.wait()
 
 
-def place_own(channel, part, both_rows):
-    rows = both_rows.shape[0] // 2
+def place_own(channel, part, both_rows, rows):
     return pl.pallas_call(
         place_own_kernel,
         out_shape=jax.ShapeDtypeStruct((2, rows) + both_rows.shape[1:], both_rows.dtype),
@@ -335,9 +334,11 @@
 
 
 def outer_kernel(odd_ref, swap_ref, backdrop_ref, inner_ref, a_ref, b_ref, side_ref, side_a_ref, side_b_ref,
-                 mx_ref, mze_ref, mzs_ref, mye_ref, mys_ref, point_ref, *rest, quotient, first, ny, nz):
+                 mx_ref, mze_ref, mzs_ref, mye_ref, mys_ref, point_ref, *rest, quotient, first, last, ny, nz):
     if quotient:
         cast_ref, out_a_ref, out_b_ref, edge_ref, rim_ref, more_ref = rest
+    elif last:
+        mine_ref, theirs_ref, peak_ref, edge_ref, rim_ref, more_ref = rest
     else:
         full_ref, peak_ref, cast_ref, out_a_ref, out_b_ref, edge_ref, rim_ref, more_ref = rest
     nside = side_ref.shape[0]
@@ -422,6 +423,24 @@
         out_b_ref[y] = jnp.where(odd, top, bottom)
         return carry
 
+    if last:
+        half = ny // 2
+
+        def finish_half(ref, start):
+            def step(i, carry):
+                y = i + start
+                row = pl.multiple_of(y * pitch, 8)
+                blurred = inner_ref[pl.ds(row, nz), :] + more_ref[pl.ds(row, nz), :]
+                value = (point_ref[y] + backdrop if first else point_ref[y]) * blurred
+                ref[i] = value
+                return jnp.maximum(carry, value)
+
+            return lax.fori_loop(0, half, step, jnp.zeros((nz, lanes), F32), unroll=8)
+
+        peak_ref[...] = finish_half(theirs_ref, half - swap)
+        finish_half(mine_ref, swap)
+        return
+
     peak = lax.fori_loop(0, ny, finish, 0 if quotient else jnp.zeros((nz, lanes), F32), unroll=8)
     if not quotient:
         peak_ref[...] = peak
@@ -441,7 +460,7 @@
     )(block, *matrices)
 
 
-def blur_outer(quotient, first, swap, backdrop, inner, halos, matrices, point):
+def blur_outer(quotient, first, last, swap, backdrop, inner, halos, matrices, point):
     ny, nz, nx = point.shape
     nside = halos[2].shape[0]
     outs = [
@@ -449,10 +468,13 @@
         jax.ShapeDtypeStruct((ny, HALO, nx), BF16),
         jax.ShapeDtypeStruct((ny, HALO, nx), BF16),
     ]
-    if not quotient:
+    if last:
+        part = jax.ShapeDtypeStruct((ny // 2, nz, nx), F32)
+        outs = [part, part, jax.ShapeDtypeStruct((nz, nx), F32)]
+    elif not quotient:
         outs = [jax.ShapeDtypeStruct((ny, nz, nx), F32), jax.ShapeDtypeStruct((nz, nx), F32)] + outs
     return pl.pallas_call(
-        functools.partial(outer_kernel, quotient=quotient, first=first, ny=ny, nz=nz),
+        functools.partial(outer_kernel, quotient=quotient, first=first, last=last, ny=ny, nz=nz),
         out_shape=outs,
         in_specs=[pl.BlockSpec(memory_space=pltpu.SMEM)] * 3 + in_vmem(12),
         out_specs=in_vmem(len(outs)),
@@ -733,19 +755,22 @@
     for iteration in range(ITERS):
         halos = halo_exchange(field)
         inner = blur_inner(True, field[0], forward[0])
-        field = blur_outer(True, False, jnp.int32(0), backdrop, inner, halos, forward[1], deskewed)
+        field = blur_outer(True, False, False, jnp.int32(0), backdrop, inner, halos, forward[1], deskewed)
         halos = halo_exchange(field)
         swap = channel * rows if iteration == ITERS - 1 else jnp.int32(0)
         inner = blur_inner(False, field[0], backward[0])
-        estimate, peak, *field = blur_outer(False, iteration == 0, swap, backdrop, inner, halos, backward[1], estimate)
-    theirs = estimate[rows:]
+        last = iteration == ITERS - 1
+        estimate, peak, *field = blur_outer(
+            False, iteration == 0, last, swap, backdrop, inner, halos, backward[1], estimate
+        )
+    mine, theirs, peak = estimate, peak, field[0]
     power = jnp.floor(jnp.log2(jnp.max(peak))) - 13.0
     message = jnp.concatenate(
         [theirs * jnp.exp2(-power), jnp.full((1,) + theirs.shape[1:], power)], axis=0
     ).astype(jnp.float16)
     got = swap_pair(message)
-    deskewed_out = place_other(channel, deskewed_other, place_own(channel, channel, deskewed))
-    partial = place_own(channel, jnp.int32(0), estimate)
+    deskewed_out = place_other(channel, deskewed_other, place_own(channel, channel, deskewed, rows))
+    partial = place_own(channel, jnp.int32(0), mine, rows)
     received = got[:rows].astype(F32) * jnp.exp2(got[rows, 0, 0].astype(F32))
     return deskewed_out, place_other(channel, received, partial)
 

time: 285 us -> 270 us (0.947)
  starting transfers between devices: 78.4 us -> 64.9 us
  local copies, waits for them, and re-layouts: 26.8 us -> 20.6 us
  waiting for transfers between devices: 95.7 us -> 101 us
    ppermute x7, starting transfers between devices: 31.3 us -> 11 us  [share_spill(): piece = lax.ppermute(piece, ('by', 'bz'), pairs)]
    ppermute x7, waiting for transfers between devices: 35.6 us -> 48.9 us  [share_spill(): piece = lax.ppermute(piece, ('by', 'bz'), pairs)]
    ppermute x4, waiting for transfers between devices: 11.7 us -> 0.01 us  [halo_exchange(): lax.ppermute(lax.dynamic_slice_in_dim(block, start, HALO, 0), 'by', pairs)]
    unnamed x91 -> x81, local copies, waits for them, and re-layouts: 20.1 us -> 14.7 us
    ppermute x8, starting transfers between devices: 21.9 us -> 16.5 us  [halo_exchange(): across.append(lax.ppermute(face, 'bz', z_pairs))]
    ppermute x3, waiting for transfers between devices: 47.3 us -> 52.2 us  [swap_pair(): lax.ppermute(x, 'by', [(i, i ^ 1) for i in range(lax.axis_size('by'))])]
    ppermute x8, starting transfers between devices: 10.9 us -> 15.8 us  [halo_exchange(): lax.ppermute(lax.dynamic_slice_in_dim(face, start, HALO, 0), ('by', 'bz')...]
    ppermute x1, starting transfers between devices: 1.92 us -> 5.82 us  [shards(): lax.ppermute(over.astype(jnp.float16), 'bz', [(i, i + 1) for i in range(b...]
  transfers between devices with their start and end apart: 33 -> 33, of which waited for: 11 -> 6; matrix products, arithmetic and copies ran while one was open for 6% -> 6% of each run, Pallas kernels for 14% -> 14%
where the time goes in v4:
time: 270 us; the launch traced here: 268 us
  waiting for transfers between devices  101 us (37%)
  Pallas kernels  67 us (25%)
  starting transfers between devices  64.9 us (24%)
  local copies, waits for them, and re-layouts  20.6 us (8%)
  other arithmetic  10.5 us (4%)
  between operations  3.78 us (1%)
    ppermute x3, waiting for transfers between devices, swap_pair(): lax.ppermute(x, 'by', [(i, i ^ 1) for i in range(lax.axis_size('by'))])  52.2 us
    ppermute x7, waiting for transfers between devices, share_spill(): piece = lax.ppermute(piece, ('by', 'bz'), pairs)  48.9 us
    pallas_call x4, Pallas kernels, blur_outer(): pl.pallas_call(functools.partial(outer_kernel, quotient=quotient, first=f...  21.6 us
    pallas_call x4, Pallas kernels, blur_inner(): pl.pallas_call(functools.partial(inner_kernel, coarse=coarse), out_shape=...  17.4 us
    ppermute x8, starting transfers between devices, halo_exchange(): across.append(lax.ppermute(face, 'bz', z_pairs))  16.5 us
    ppermute x8, starting transfers between devices, halo_exchange(): lax.ppermute(lax.dynamic_slice_in_dim(face, start, HALO, 0), ('by', 'bz')...  15.8 us
    unnamed x81, local copies, waits for them, and re-layouts  14.7 us
    ppermute x7, starting transfers between devices, share_spill(): piece = lax.ppermute(piece, ('by', 'bz'), pairs)  11 us
  transfers between devices with their start and end apart: 33, of which 6 were waited for; matrix products, arithmetic and copies ran while one was open for 6% of the time, Pallas kernels for 14%

profile of v4, /device:TPU:1, one launch (start us, length us, event | category | flops | bytes accessed | tf_op | source)
XLA Modules:
  0.0 268.0 jit_solution(16848625491821150328)
XLA Ops:
  0.6 3.3 %pack_tiles.1 = (bf16[32,4,64,128]{3,2,1,0:T(8,128)(2,1)S(1)}, bf16[2,4,64,128]{3,2,1,0:T(8,128)(2,1)S(1)}, bf16[2,4,64,128]{3,2,1,0:T(8,128)(2,1)S(1)}) custom-call(s32[1]{0:T(128)} %bitcast.16.own_ref, s32[1]{0:T(128)} %bitcast.7.channel_ref.part_ref, s32[1]{0:T(128)} %constant.158.clone.1.turn_ref.swap_ref.part_ref, s32[128]{0:T(128)} %bitcast.52, ...), custom_call_target="tpu_custom_call" | custom-call | tf_op jit(solution)/shard_map/pack_tiles/pallas_call | solution.py:104
  4.0 1.3 copy-done.2
  5.3 7.5 %all-to-all-start = ((bf16[16,2,4,64,128]{4,3,2,1,0:T(8,128)(2,1)}), bf16[16,2,4,64,128]{4,3,2,1,0:T(8,128)(2,1)S(1)}, u32[]{:S(2)}, u32[]{:S(2)}) async-start(bf16[16,2,4,64,128]{4,3,2,1,0:T(8,128)(2,1)} %bitcast.50), calls=%async_computation | async-start | bytes 4194304 | tf_op jit(solution)/shard_map/all_to_all | solution.py:682
  12.7 1.4 collective-permute-start.10
  14.1 2.1 collective-permute-start.12
  17.5 3.2 %collective-permute-start.14 = (bf16[2,4,64,128]{3,2,1,0:T(8,128)(2,1)S(1)}, bf16[2,4,64,128]{3,2,1,0:T(8,128)(2,1)S(1)}, u32[]{:S(2)}, u32[]{:S(2)}) collective-permute-start(bf16[2,4,64,128]{3,2,1,0:T(8,128)(2,1)S(1)} %get-tuple-element.281.refs_0_), channel_id=1, source_target_pairs={{0,6},{1,7},{2,4},{3,5},{4,2},{5,3},{6,0},{7,1},{8,14},{9,15},{10,... | collective-permute-start | bytes 393224 | tf_op jit(solution)/shard_map/ppermute | solution.py:663
  24.1 26.6 %collective-permute-done.10.refs_2_ = bf16[2,4,64,128]{3,2,1,0:T(8,128)(2,1)S(1)} collective-permute-done((bf16[2,4,64,128]{3,2,1,0:T(8,128)(2,1)S(1)}, bf16[2,4,64,128]{3,2,1,0:T(8,128)(2,1)S(1)}, u32[]{:S(2)}, u32[]{:S(2)}) %collective-permute-start.10) | collective-permute-done | bytes 131104 | tf_op jit(solution)/shard_map/ppermute | solution.py:663
  50.7 3.0 %collective-permute-start.15 = (bf16[2,4,64,128]{3,2,1,0:T(8,128)(2,1)S(1)}, bf16[2,4,64,128]{3,2,1,0:T(8,128)(2,1)S(1)}, u32[]{:S(2)}, u32[]{:S(2)}) collective-permute-start(bf16[2,4,64,128]{3,2,1,0:T(8,128)(2,1)S(1)} %get-tuple-element.282), channel_id=1, source_target_pairs={{0,14},{1,15},{2,12},{3,13},{4,10},{5,11},{6,8},{7,9},{8,6},{9,7},... | collective-permute-start | bytes 393224 | tf_op jit(solution)/shard_map/ppermute | solution.py:663
  53.7 3.0 %collective-permute-done.11.refs_3_ = bf16[2,4,64,128]{3,2,1,0:T(8,128)(2,1)S(1)} collective-permute-done((bf16[2,4,64,128]{3,2,1,0:T(8,128)(2,1)S(1)}, bf16[2,4,64,128]{3,2,1,0:T(8,128)(2,1)S(1)}, u32[]{:S(2)}, u32[]{:S(2)}) %collective-permute-start.11) | collective-permute-done | bytes 131104 | tf_op jit(solution)/shard_map/ppermute | solution.py:663
  58.1 16.7 %collective-permute-done.12.refs_4_ = bf16[2,4,64,128]{3,2,1,0:T(8,128)(2,1)S(1)} collective-permute-done((bf16[2,4,64,128]{3,2,1,0:T(8,128)(2,1)S(1)}, bf16[2,4,64,128]{3,2,1,0:T(8,128)(2,1)S(1)}, u32[]{:S(2)}, u32[]{:S(2)}) %collective-permute-start.12) | collective-permute-done | bytes 131104 | tf_op jit(solution)/shard_map/ppermute | solution.py:663
  76.0 2.5 collective-permute-done.13.refs_5_
  82.7 1.6 collective-permute-start.16
  84.4 1.3 reduce_max.18
  87.4 1.3 dynamic_slice.47.backdrop_ref
  90.2 5.1 %band_matrices.1 = (bf16[256,128]{1,0:T(8,128)(2,1)S(1)}, bf16[128,256]{1,0:T(8,128)(2,1)S(1)}, bf16[128,384]{1,0:T(8,128)(2,1)S(1)}, bf16[128,256]{1,0:T(8,128)...) custom-call(s32[2]{0:T(128)S(1)} %pad_add_fusion.place_ref, ...), custom_call_target="tpu_custom_call" | custom-call | tf_op jit(solution)/shard_map/band_matrices/pallas_call | solution.py:621
  103.0 4.6 %gather_planes.1 = (f32[67,128,128]{2,1,0:T(8,128)}, f32[12,128,128]{2,1,0:T(8,128)}) custom-call(s32[1]{0:T(128)} %bitcast.7.channel_ref.part_ref, s32[16]{0:T(128)S(1)} %sub.32.starts_ref, s32[16]{0:T(128)S(1)} %reshape.105.spill_starts_ref, bf16[2,16,4,64,128]{4,3,2,1,0:T(8,128)(2,1)S(1)} %bitcast.47, bf16[4,2,2,4,64,128]{5,4,3,2,1,0:T(8,128)(2,1)S(1)} %bitcast.49, ...), custom_call_target="tpu_custom_call" | custom-call | tf_op jit(solution)/shard_map/gather_planes/pallas_call | solution.py:162
  107.6 1.2 convert_element_type.46
  108.8 5.8 %collective-permute-start.17 = (f16[12,128,128]{2,1,0:T(8,128)(2,1)S(1)}, f16[12,128,128]{2,1,0:T(8,128)(2,1)S(1)}, u32[]{:S(2)}, u32[]{:S(2)}) collective-permute-start(f16[12,128,128]{2,1,0:T(8,128)(2,1)S(1)} %convert_element_type.46), channel_id=1, source_target_pairs={{0,1},{1,2},{2,3},{3,4},{4,5},{5,6},{6,7},{8,9},{9,10},{10,11},{11... | collective-permute-start | bytes 1179656 | tf_op jit(solution)/shard_map/ppermute | solution.py:746
  114.6 5.6 %deskew.1 = (f32[128,64,128]{2,1,0:T(8,128)S(1)}, bf16[128,64,128]{2,1,0:T(8,128)(2,1)S(1)}, bf16[128,16,128]{2,1,0:T(8,128)(2,1)S(1)}, bf16[128,16,128]{2,1,0:T(8,128)(2,1)S(1)}) custom-call(s32[1]{0:T(128)} %bitcast.8.odd_ref, f32[1]{0:T(128)} %dynamic_slice.47.backdrop_ref, s32[128]{0:T(128)S(1)} %get-tuple-element.276.band_ref, ...), custom_call_target="tpu_custom_call" | custom-call | flops 5000000000 | bytes 12000000 | tf_op jit(solution)/shard_map/deskew/pallas_call | solution.py:248
  120.3 2.4 deskew_more.1
  122.8 4.9 %collective-permute-start.20 = (bf16[128,16,128]{2,1,0:T(8,128)(2,1)S(1)}, bf16[128,16,128]{2,1,0:T(8,128)(2,1)S(1)}, u32[]{:S(2)}, u32[]{:S(2)}) collective-permute-start(bf16[128,16,128]{2,1,0:T(8,128)(2,1)S(1)} %get-tuple-element.297), channel_id=1, source_target_pairs={{1,2},{2,1},{3,4},{4,3},{5,6},{6,5},{9,10},{10,9},{11,12},{12,11},... | collective-permute-start | bytes 1572872 | tf_op jit(solution)/shard_map/ppermute | solution.py:514
  127.8 1.3 collective-permute-start.21
  129.2 4.8 %collective-permute-start.23 = (bf16[16,16,128]{2,1,0:T(8,128)(2,1)S(1)}, bf16[16,16,128]{2,1,0:T(8,128)(2,1)S(1)}, u32[]{:S(2)}, u32[]{:S(2)}) collective-permute-start(bf16[16,16,128]{2,1,0:T(8,128)(2,1)S(1)} %constant_dynamic-slice_fusion.9), channel_id=1, source_target_pairs={{1,18},{2,17},{3,20},{4,19},{5,22},{6,21},{9,26},{10,25},{11,28},{... | collective-permute-start | bytes 196616 | tf_op jit(solution)/shard_map/ppermute | solution.py:520
  134.0 4.0 %blur_inner.4.inner_ref = f32[9216,128]{1,0:T(8,128)S(1)} custom-call(bf16[128,64,128]{2,1,0:T(8,128)(2,1)S(1)} %get-tuple-element.292.own_ref, bf16[256,128]{1,0:T(8,128)(2,1)S(1)} %copy-done.19, bf16[128,256]{1,0:T(8,128)(2,1)S(1)} %copy-done.23, bf16[128,384]{1,0:T(8,128)(2,1)S(1)} %copy-done.11), custom_call_target="tpu_custom_call" | custom-call | flops 20000000000 | bytes 8000000 | tf_op jit(solution)/shard_map/blur_inner/pallas_call | solution.py:451
  138.0 1.6 constant_dynamic-slice_fusion.12
  139.7 5.2 %blur_quotient.2 = (bf16[128,64,128]{2,1,0:T(8,128)(2,1)S(1)}, bf16[128,16,128]{2,1,0:T(8,128)(2,1)S(1)}, bf16[128,16,128]{2,1,0:T(8,128)(2,1)S(1)}) custom-call(s32[1]{0:T(128)} %bitcast.8.odd_ref, s32[1]{0:T(128)} %constant.158.clone.1.turn_ref.swap_ref.part_ref, f32[1]{0:T(128)} %dynamic_slice.47.backdrop_ref, f32[9216,128]{1,0:T(8,128)S(1)} %blur_inner.4.inner_ref, ...), custom_call_target="tpu_custom_call" | custom-call | flops 10000000000 | bytes 16000000 | tf_op jit(solution)/shard_map/blur_quotient/pallas_call | solution.py:476
  145.0 2.4 collective-permute-start.25
  148.6 4.0 %collective-permute-start.28 = (bf16[16,16,128]{2,1,0:T(8,128)(2,1)S(1)}, bf16[16,16,128]{2,1,0:T(8,128)(2,1)S(1)}, u32[]{:S(2)}, u32[]{:S(2)}) collective-permute-start(bf16[16,16,128]{2,1,0:T(8,128)(2,1)S(1)} %constant_dynamic-slice_fusion.6), channel_id=1, source_target_pairs={{1,18},{2,17},{3,20},{4,19},{5,22},{6,21},{9,26},{10,25},{11,28},{... | collective-permute-start | bytes 196616 | tf_op jit(solution)/shard_map/ppermute | solution.py:520
  152.6 4.7 %blur_inner.5.inner_ref = f32[9216,128]{1,0:T(8,128)S(1)} custom-call(bf16[128,64,128]{2,1,0:T(8,128)(2,1)S(1)} %get-tuple-element.303.own_ref, bf16[256,128]{1,0:T(8,128)(2,1)S(1)} %copy-done.13, bf16[128,256]{1,0:T(8,128)(2,1)S(1)} %copy-done.17, bf16[128,384]{1,0:T(8,128)(2,1)S(1)} %get-tuple-element.306.my_ref), custom_call_target="tpu_custom_call" | custom-call | flops 20000000000 | bytes 8000000 | tf_op jit(solution)/shard_map/blur_inner/pallas_call | solution.py:451
  157.4 6.1 %blur_estimate.2 = (f32[128,64,128]{2,1,0:T(8,128)S(1)}, f32[64,128]{1,0:T(8,128)}, bf16[128,64,128]{2,1,0:T(8,128)(2,1)S(1)}, bf16[128,16,128]{2,1,0:T(8,128)(2,1)S(1)}, bf16[128,16,128]{2,1,0:T(8,128)(2,1)S(1)}) custom-call(s32[1]{0:T(128)} %bitcast.8.odd_ref, s32[1]{0:T(128)} %constant.158.clone.1.turn_ref.swap_ref.part_ref, ...), custom_call_target="tpu_custom_call" | custom-call | flops 10000000000 | bytes 16000000 | tf_op jit(solution)/shard_map/blur_estimate/pallas_call | solution.py:476
  163.7 3.5 %collective-permute-start.30 = (bf16[128,16,128]{2,1,0:T(8,128)(2,1)S(1)}, bf16[128,16,128]{2,1,0:T(8,128)(2,1)S(1)}, u32[]{:S(2)}, u32[]{:S(2)}) collective-permute-start(bf16[128,16,128]{2,1,0:T(8,128)(2,1)S(1)} %get-tuple-element.316), channel_id=1, source_target_pairs={{1,2},{2,1},{3,4},{4,3},{5,6},{6,5},{9,10},{10,9},{11,12},{12,11},... | collective-permute-start | bytes 1572872 | tf_op jit(solution)/shard_map/ppermute | solution.py:514
  167.3 1.3 collective-permute-start.31
  168.6 3.5 %collective-permute-start.33 = (bf16[16,16,128]{2,1,0:T(8,128)(2,1)S(1)}, bf16[16,16,128]{2,1,0:T(8,128)(2,1)S(1)}, u32[]{:S(2)}, u32[]{:S(2)}) collective-permute-start(bf16[16,16,128]{2,1,0:T(8,128)(2,1)S(1)} %constant_dynamic-slice_fusion.3), channel_id=1, source_target_pairs={{1,18},{2,17},{3,20},{4,19},{5,22},{6,21},{9,26},{10,25},{11,28},{... | collective-permute-start | bytes 196616 | tf_op jit(solution)/shard_map/ppermute | solution.py:520
  172.2 4.0 %blur_inner.6.inner_ref = f32[9216,128]{1,0:T(8,128)S(1)} custom-call(bf16[128,64,128]{2,1,0:T(8,128)(2,1)S(1)} %get-tuple-element.314.own_ref, bf16[256,128]{1,0:T(8,128)(2,1)S(1)} %copy-done.19, bf16[128,256]{1,0:T(8,128)(2,1)S(1)} %copy-done.23, bf16[128,384]{1,0:T(8,128)(2,1)S(1)} %copy-done.11), custom_call_target="tpu_custom_call" | custom-call | flops 20000000000 | bytes 8000000 | tf_op jit(solution)/shard_map/blur_inner/pallas_call | solution.py:451
  176.2 5.2 %blur_quotient.3 = (bf16[128,64,128]{2,1,0:T(8,128)(2,1)S(1)}, bf16[128,16,128]{2,1,0:T(8,128)(2,1)S(1)}, bf16[128,16,128]{2,1,0:T(8,128)(2,1)S(1)}) custom-call(s32[1]{0:T(128)} %bitcast.8.odd_ref, s32[1]{0:T(128)} %constant.158.clone.1.turn_ref.swap_ref.part_ref, f32[1]{0:T(128)} %dynamic_slice.47.backdrop_ref, f32[9216,128]{1,0:T(8,128)S(1)} %blur_inner.6.inner_ref, ...), custom_call_target="tpu_custom_call" | custom-call | flops 10000000000 | bytes 16000000 | tf_op jit(solution)/shard_map/blur_quotient/pallas_call | solution.py:476
  181.5 5.2 %collective-permute-start.35 = (bf16[128,16,128]{2,1,0:T(8,128)(2,1)S(1)}, bf16[128,16,128]{2,1,0:T(8,128)(2,1)S(1)}, u32[]{:S(2)}, u32[]{:S(2)}) collective-permute-start(bf16[128,16,128]{2,1,0:T(8,128)(2,1)S(1)} %get-tuple-element.319), channel_id=1, source_target_pairs={{1,2},{2,1},{3,4},{4,3},{5,6},{6,5},{9,10},{10,9},{11,12},{12,11},... | collective-permute-start | bytes 1572872 | tf_op jit(solution)/shard_map/ppermute | solution.py:514
  187.1 3.4 %collective-permute-start.38 = (bf16[16,16,128]{2,1,0:T(8,128)(2,1)S(1)}, bf16[16,16,128]{2,1,0:T(8,128)(2,1)S(1)}, u32[]{:S(2)}, u32[]{:S(2)}) collective-permute-start(bf16[16,16,128]{2,1,0:T(8,128)(2,1)S(1)} %constant_dynamic-slice_fusion), channel_id=1, source_target_pairs={{1,18},{2,17},{3,20},{4,19},{5,22},{6,21},{9,26},{10,25},{11,28},{... | collective-permute-start | bytes 196616 | tf_op jit(solution)/shard_map/ppermute | solution.py:520
  190.6 4.7 %blur_inner.7.inner_ref = f32[9216,128]{1,0:T(8,128)S(1)} custom-call(bf16[128,64,128]{2,1,0:T(8,128)(2,1)S(1)} %get-tuple-element.317.own_ref, bf16[256,128]{1,0:T(8,128)(2,1)S(1)} %copy-done.13, bf16[128,256]{1,0:T(8,128)(2,1)S(1)} %copy-done.17, bf16[128,384]{1,0:T(8,128)(2,1)S(1)} %get-tuple-element.306.my_ref), custom_call_target="tpu_custom_call" | custom-call | flops 20000000000 | bytes 8000000 | tf_op jit(solution)/shard_map/blur_inner/pallas_call | solution.py:451
  195.5 5.1 %blur_estimate.3 = (f32[64,64,128]{2,1,0:T(8,128)S(1)}, f32[64,64,128]{2,1,0:T(8,128)S(1)}, f32[64,128]{1,0:T(8,128)S(1)}) custom-call(s32[1]{0:T(128)} %bitcast.8.odd_ref, s32[1]{0:T(128)} %bitcast.21.swap_ref, f32[1]{0:T(128)} %dynamic_slice.47.backdrop_ref, f32[9216,128]{1,0:T(8,128)S(1)} %blur_inner.7.inner_ref, ...), custom_call_target="tpu_custom_call" | custom-call | flops 10000000000 | bytes 16000000 | tf_op jit(solution)/shard_map/blur_estimate/pallas_call | solution.py:476
  200.6 1.3 copy-done.3
  203.4 2.0 multiply_convert_fusion
  205.7 1.5 collective-permute-start.39
  207.2 1.3 place_own.2.partial_ref
  208.5 1.3 place_own.3.partial_ref
  209.9 33.4 %collective-permute-done.18.other_ref = f32[64,64,128]{2,1,0:T(8,128)} collective-permute-done((f32[64,64,128]{2,1,0:T(8,128)}, f32[64,64,128]{2,1,0:T(8,128)}, u32[]{:S(2)}, u32[]{:S(2)}) %collective-permute-start.18) | collective-permute-done | bytes 2097184 | tf_op jit(solution)/shard_map/ppermute | solution.py:634
  243.3 2.9 %place_other.2 = f32[2,64,64,128]{3,2,1,0:T(8,128)} custom-call(s32[1]{0:T(128)} %bitcast.7.channel_ref.part_ref, f32[64,64,128]{2,1,0:T(8,128)} %collective-permute-done.18.other_ref, f32[2,64,64,128]{3,2,1,0:T(8,128)} %place_own.2.partial_ref), custom_call_target="tpu_custom_call", output_to_operand_aliasing={{}: (2, {})} | custom-call | tf_op jit(solution)/shard_map/place_other/pallas_call | solution.py:53
  246.2 18.8 %collective-permute-done.39 = f16[65,64,128]{2,1,0:T(8,128)(2,1)S(1)} collective-permute-done((f16[65,64,128]{2,1,0:T(8,128)(2,1)S(1)}, f16[65,64,128]{2,1,0:T(8,128)(2,1)S(1)}, u32[]{:S(2)}, u32[]{:S(2)}) %collective-permute-start.39) | collective-permute-done | bytes 1064992 | tf_op jit(solution)/shard_map/ppermute | solution.py:634
  266.5 1.3 place_other.3
  (176 shorter events, 25.8 us)
Async XLA Ops:
  5.3 15.9 %copy-start.32 = (s32[128,1]{0,1:T(1,128)S(1)}, s32[128,1]{0,1:T(1,128)}, u32[]{:S(2)}) copy-start(s32[128,1]{0,1:T(1,128)} %param.12) | copy-start | bytes 1540
  5.3 16.6 %copy-start.39 = (s32[128]{0:T(128)S(1)}, s32[128]{0:T(128)}, u32[]{:S(2)}) copy-start(s32[128]{0:T(128)} %param.13) | copy-start | bytes 1540
  5.3 18.8 %copy-start.37 = (s32[64]{0:T(128)S(1)}, s32[64]{0:T(128)}, u32[]{:S(2)}) copy-start(s32[64]{0:T(128)} %param.14) | copy-start | bytes 772
  5.3 52.3 %copy-start.38 = (bf16[64,2]{0,1:T(2,128)(2,1)S(1)}, bf16[64,2]{0,1:T(2,128)(2,1)}, u32[]{:S(2)}) copy-start(bf16[64,2]{0,1:T(2,128)(2,1)} %param.15) | copy-start | bytes 772
  5.3 97.7 %all-to-all-start = ((bf16[16,2,4,64,128]{4,3,2,1,0:T(8,128)(2,1)}), bf16[16,2,4,64,128]{4,3,2,1,0:T(8,128)(2,1)S(1)}, u32[]{:S(2)}, u32[]{:S(2)}) async-start(bf16[16,2,4,64,128]{4,3,2,1,0:T(8,128)(2,1)} %bitcast.50), calls=%async_computation | async-start | bytes 4194304 | tf_op jit(solution)/shard_map/all_to_all | solution.py:682
  12.7 38.0 %collective-permute-start.10 = (bf16[2,4,64,128]{3,2,1,0:T(8,128)(2,1)S(1)}, bf16[2,4,64,128]{3,2,1,0:T(8,128)(2,1)S(1)}, u32[]{:S(2)}, u32[]{:S(2)}) collective-permute-start(bf16[2,4,64,128]{3,2,1,0:T(8,128)(2,1)S(1)} %get-tuple-element.281.refs_0_), channel_id=1, source_target_pairs={{0,2},{1,3},{2,0},{3,1},{4,6},{5,7},{6,4},{7,5},{8,10},{9,11},{10,... | collective-permute-start | bytes 393224 | tf_op jit(solution)/shard_map/ppermute | solution.py:663
  14.1 60.8 %collective-permute-start.12 = (bf16[2,4,64,128]{3,2,1,0:T(8,128)(2,1)S(1)}, bf16[2,4,64,128]{3,2,1,0:T(8,128)(2,1)S(1)}, u32[]{:S(2)}, u32[]{:S(2)}) collective-permute-start(bf16[2,4,64,128]{3,2,1,0:T(8,128)(2,1)S(1)} %get-tuple-element.281.refs_0_), channel_id=1, source_target_pairs={{0,4},{1,5},{2,6},{3,7},{4,0},{5,1},{6,2},{7,3},{8,12},{9,13},{10,... | collective-permute-start | bytes 393224 | tf_op jit(solution)/shard_map/ppermute | solution.py:663
  16.2 40.6 %collective-permute-start.11 = (bf16[2,4,64,128]{3,2,1,0:T(8,128)(2,1)S(1)}, bf16[2,4,64,128]{3,2,1,0:T(8,128)(2,1)S(1)}, u32[]{:S(2)}, u32[]{:S(2)}) collective-permute-start(bf16[2,4,64,128]{3,2,1,0:T(8,128)(2,1)S(1)} %get-tuple-element.282), channel_id=1, source_target_pairs={{0,10},{1,11},{2,8},{3,9},{4,14},{5,15},{6,12},{7,13},{8,2},{9,3},... | collective-permute-start | bytes 393224 | tf_op jit(solution)/shard_map/ppermute | solution.py:663
  17.4 61.2 %collective-permute-start.13 = (bf16[2,4,64,128]{3,2,1,0:T(8,128)(2,1)S(1)}, bf16[2,4,64,128]{3,2,1,0:T(8,128)(2,1)S(1)}, u32[]{:S(2)}, u32[]{:S(2)}) collective-permute-start(bf16[2,4,64,128]{3,2,1,0:T(8,128)(2,1)S(1)} %get-tuple-element.282), channel_id=1, source_target_pairs={{0,12},{1,13},{2,14},{3,15},{4,8},{5,9},{6,10},{7,11},{8,4},{9,5},... | collective-permute-start | bytes 393224 | tf_op jit(solution)/shard_map/ppermute | solution.py:663
  17.5 61.7 %collective-permute-start.14 = (bf16[2,4,64,128]{3,2,1,0:T(8,128)(2,1)S(1)}, bf16[2,4,64,128]{3,2,1,0:T(8,128)(2,1)S(1)}, u32[]{:S(2)}, u32[]{:S(2)}) collective-permute-start(bf16[2,4,64,128]{3,2,1,0:T(8,128)(2,1)S(1)} %get-tuple-element.281.refs_0_), channel_id=1, source_target_pairs={{0,6},{1,7},{2,4},{3,5},{4,2},{5,3},{6,0},{7,1},{8,14},{9,15},{10,... | collective-permute-start | bytes 393224 | tf_op jit(solution)/shard_map/ppermute | solution.py:663
  23.1 56.8 %copy-start.33 = (pred[8,16]{1,0:T(8,128)(4,1)}, pred[8,16]{1,0:T(8,128)(4,1)S(1)}, u32[]{:S(2)}) copy-start(pred[8,16]{1,0:T(8,128)(4,1)S(1)} %get-tuple-element.351) | copy-start | bytes 388
  24.1 55.8 %copy-start.36 = (f32[64,1]{0,1:T(1,128)}, f32[64,1]{0,1:T(1,128)S(1)}, u32[]{:S(2)}) copy-start(f32[64,1]{0,1:T(1,128)S(1)} %convert_bitcast_fusion.1) | copy-start | bytes 772
  50.7 29.1 %collective-permute-start.15 = (bf16[2,4,64,128]{3,2,1,0:T(8,128)(2,1)S(1)}, bf16[2,4,64,128]{3,2,1,0:T(8,128)(2,1)S(1)}, u32[]{:S(2)}, u32[]{:S(2)}) collective-permute-start(bf16[2,4,64,128]{3,2,1,0:T(8,128)(2,1)S(1)} %get-tuple-element.282), channel_id=1, source_target_pairs={{0,14},{1,15},{2,12},{3,13},{4,10},{5,11},{6,8},{7,9},{8,6},{9,7},... | collective-permute-start | bytes 393224 | tf_op jit(solution)/shard_map/ppermute | solution.py:663
  57.4 22.5 %collective-permute-start.9 = (bf16[2,4,64,128]{3,2,1,0:T(8,128)(2,1)S(1)}, bf16[2,4,64,128]{3,2,1,0:T(8,128)(2,1)S(1)}, u32[]{:S(2)}, u32[]{:S(2)}) collective-permute-start(bf16[2,4,64,128]{3,2,1,0:T(8,128)(2,1)S(1)} %get-tuple-element.282), channel_id=1, source_target_pairs={{0,8},{1,9},{2,10},{3,11},{4,12},{5,13},{6,14},{7,15},{8,0},{9,1},... | collective-permute-start | bytes 393224 | tf_op jit(solution)/shard_map/ppermute | solution.py:663
  57.6 22.3 %copy-start.35 = (f32[64,2]{0,1:T(2,128)}, f32[64,2]{0,1:T(2,128)S(1)}, u32[]{:S(2)}) copy-start(f32[64,2]{0,1:T(2,128)S(1)} %convert_element_type.41) | copy-start | bytes 1540
  74.8 27.3 %collective-permute-start.8 = (f32[64,3]{0,1:T(4,128)}, f32[64,3]{0,1:T(4,128)}, u32[]{:S(2)}, u32[]{:S(2)}) collective-permute-start(f32[64,3]{0,1:T(4,128)} %pad_maximum_fusion.1), channel_id=1, source_target_pairs={{0,8},{8,0},{16,24},{24,16},{1,9},{9,1},{17,25},{25,17},{2,10},{10... | collective-permute-start | bytes 2312 | tf_op jit(solution)/shard_map/ppermute | solution.py:634
  82.7 20.3 %collective-permute-start.16 = (bf16[4,2,2,4,64,128]{5,4,3,2,1,0:T(8,128)(2,1)S(1)}, bf16[4,2,2,4,64,128]{5,4,3,2,1,0:T(8,128)(2,1)}, u32[]{:S(2)}, u32[]{:S(2)}) collective-permute-start(bf16[4,2,2,4,64,128]{5,4,3,2,1,0:T(8,128)(2,1)S(1)} %bitcast.48), channel_id=1, source_target_pairs={{0,1},{1,0},{2,3},{3,2},{4,5},{5,4},{6,7},{7,6},{8,9},{9,8},{10,11... | collective-permute-start | bytes 3145736 | tf_op jit(solution)/shard_map/ppermute | solution.py:667
  108.8 11.4 %collective-permute-start.17 = (f16[12,128,128]{2,1,0:T(8,128)(2,1)S(1)}, f16[12,128,128]{2,1,0:T(8,128)(2,1)S(1)}, u32[]{:S(2)}, u32[]{:S(2)}) collective-permute-start(f16[12,128,128]{2,1,0:T(8,128)(2,1)S(1)} %convert_element_type.46), channel_id=1, source_target_pairs={{0,1},{1,2},{2,3},{3,4},{4,5},{5,6},{6,7},{8,9},{9,10},{10,11},{11... | collective-permute-start | bytes 1179656 | tf_op jit(solution)/shard_map/ppermute | solution.py:746
  120.3 13.7 %copy-start.11 = (bf16[128,384]{1,0:T(8,128)(2,1)S(1)}, bf16[128,384]{1,0:T(8,128)(2,1)}, u32[]{:S(2)}) copy-start(bf16[128,384]{1,0:T(8,128)(2,1)} %copy-done.10) | copy-start | bytes 294916
  120.3 13.7 %copy-start.19 = (bf16[256,128]{1,0:T(8,128)(2,1)S(1)}, bf16[256,128]{1,0:T(8,128)(2,1)}, u32[]{:S(2)}) copy-start(bf16[256,128]{1,0:T(8,128)(2,1)} %copy-done.18) | copy-start | bytes 196612
  120.3 13.7 %copy-start.23 = (bf16[128,256]{1,0:T(8,128)(2,1)S(1)}, bf16[128,256]{1,0:T(8,128)(2,1)}, u32[]{:S(2)}) copy-start(bf16[128,256]{1,0:T(8,128)(2,1)} %copy-done.22) | copy-start | bytes 196612
  122.7 53.5 %copy-start = (f32[128,64,128]{2,1,0:T(8,128)}, f32[128,64,128]{2,1,0:T(8,128)S(1)}, u32[]{:S(2)}) copy-start(f32[128,64,128]{2,1,0:T(8,128)S(1)} %get-tuple-element.291.both_ref.point_ref) | copy-start | bytes 12582916
  122.8 16.9 %collective-permute-start.19 = (bf16[128,16,128]{2,1,0:T(8,128)(2,1)S(1)}, bf16[128,16,128]{2,1,0:T(8,128)(2,1)S(1)}, u32[]{:S(2)}, u32[]{:S(2)}) collective-permute-start(bf16[128,16,128]{2,1,0:T(8,128)(2,1)S(1)} %get-tuple-element.296), channel_id=1, source_target_pairs={{0,1},{1,0},{2,3},{3,2},{4,5},{5,4},{6,7},{7,6},{8,9},{9,8},{10,11... | collective-permute-start | bytes 1572872 | tf_op jit(solution)/shard_map/ppermute | solution.py:514
  122.8 16.8 %collective-permute-start.20 = (bf16[128,16,128]{2,1,0:T(8,128)(2,1)S(1)}, bf16[128,16,128]{2,1,0:T(8,128)(2,1)S(1)}, u32[]{:S(2)}, u32[]{:S(2)}) collective-permute-start(bf16[128,16,128]{2,1,0:T(8,128)(2,1)S(1)} %get-tuple-element.297), channel_id=1, source_target_pairs={{1,2},{2,1},{3,4},{4,3},{5,6},{6,5},{9,10},{10,9},{11,12},{12,11},... | collective-permute-start | bytes 1572872 | tf_op jit(solution)/shard_map/ppermute | solution.py:514
  127.8 11.8 %collective-permute-start.21 = (bf16[16,64,128]{2,1,0:T(8,128)(2,1)S(1)}, bf16[16,64,128]{2,1,0:T(8,128)(2,1)S(1)}, u32[]{:S(2)}, u32[]{:S(2)}) collective-permute-start(bf16[16,64,128]{2,1,0:T(8,128)(2,1)S(1)} %constant_dynamic-slice_fusion.11), channel_id=1, source_target_pairs={{0,16},{8,24},{16,0},{24,8},{1,17},{9,25},{17,1},{25,9},{2,18},{10... | collective-permute-start | bytes 786440 | tf_op jit(solution)/shard_map/ppermute | solution.py:517
  129.2 10.5 %collective-permute-start.22 = (bf16[16,16,128]{2,1,0:T(8,128)(2,1)S(1)}, bf16[16,16,128]{2,1,0:T(8,128)(2,1)S(1)}, u32[]{:S(2)}, u32[]{:S(2)}) collective-permute-start(bf16[16,16,128]{2,1,0:T(8,128)(2,1)S(1)} %constant_dynamic-slice_fusion.10), channel_id=1, source_target_pairs={{0,17},{1,16},{2,19},{3,18},{4,21},{5,20},{6,23},{7,22},{8,25},{9,... | collective-permute-start | bytes 196616 | tf_op jit(solution)/shard_map/ppermute | solution.py:520
  129.2 10.5 %collective-permute-start.23 = (bf16[16,16,128]{2,1,0:T(8,128)(2,1)S(1)}, bf16[16,16,128]{2,1,0:T(8,128)(2,1)S(1)}, u32[]{:S(2)}, u32[]{:S(2)}) collective-permute-start(bf16[16,16,128]{2,1,0:T(8,128)(2,1)S(1)} %constant_dynamic-slice_fusion.9), channel_id=1, source_target_pairs={{1,18},{2,17},{3,20},{4,19},{5,22},{6,21},{9,26},{10,25},{11,28},{... | collective-permute-start | bytes 196616 | tf_op jit(solution)/shard_map/ppermute | solution.py:520
  139.6 13.0 %copy-start.13 = (bf16[256,128]{1,0:T(8,128)(2,1)S(1)}, bf16[256,128]{1,0:T(8,128)(2,1)}, u32[]{:S(2)}) copy-start(bf16[256,128]{1,0:T(8,128)(2,1)} %copy-done.12) | copy-start | bytes 196612
  139.6 13.0 %copy-start.17 = (bf16[128,256]{1,0:T(8,128)(2,1)S(1)}, bf16[128,256]{1,0:T(8,128)(2,1)}, u32[]{:S(2)}) copy-start(bf16[128,256]{1,0:T(8,128)(2,1)} %copy-done.16) | copy-start | bytes 196612
  144.9 12.5 %collective-permute-start.24 = (bf16[128,16,128]{2,1,0:T(8,128)(2,1)S(1)}, bf16[128,16,128]{2,1,0:T(8,128)(2,1)S(1)}, u32[]{:S(2)}, u32[]{:S(2)}) collective-permute-start(bf16[128,16,128]{2,1,0:T(8,128)(2,1)S(1)} %get-tuple-element.307), channel_id=1, source_target_pairs={{0,1},{1,0},{2,3},{3,2},{4,5},{5,4},{6,7},{7,6},{8,9},{9,8},{10,11... | collective-permute-start | bytes 1572872 | tf_op jit(solution)/shard_map/ppermute | solution.py:514
  145.0 12.4 %collective-permute-start.25 = (bf16[128,16,128]{2,1,0:T(8,128)(2,1)S(1)}, bf16[128,16,128]{2,1,0:T(8,128)(2,1)S(1)}, u32[]{:S(2)}, u32[]{:S(2)}) collective-permute-start(bf16[128,16,128]{2,1,0:T(8,128)(2,1)S(1)} %get-tuple-element.308), channel_id=1, source_target_pairs={{1,2},{2,1},{3,4},{4,3},{5,6},{6,5},{9,10},{10,9},{11,12},{12,11},... | collective-permute-start | bytes 1572872 | tf_op jit(solution)/shard_map/ppermute | solution.py:514
  147.4 10.0 %copy-start.15 = (bf16[128,256]{1,0:T(8,128)(2,1)S(1)}, bf16[128,256]{1,0:T(8,128)(2,1)}, u32[]{:S(2)}) copy-start(bf16[128,256]{1,0:T(8,128)(2,1)} %copy-done.14) | copy-start | bytes 196612
  147.4 10.0 %copy-start.25 = (bf16[64,192]{1,0:T(8,128)(2,1)S(1)}, bf16[64,192]{1,0:T(8,128)(2,1)}, u32[]{:S(2)}) copy-start(bf16[64,192]{1,0:T(8,128)(2,1)} %copy-done.24) | copy-start | bytes 73732
  147.4 9.9 %collective-permute-start.26 = (bf16[16,64,128]{2,1,0:T(8,128)(2,1)S(1)}, bf16[16,64,128]{2,1,0:T(8,128)(2,1)S(1)}, u32[]{:S(2)}, u32[]{:S(2)}) collective-permute-start(bf16[16,64,128]{2,1,0:T(8,128)(2,1)S(1)} %constant_dynamic-slice_fusion.8), channel_id=1, source_target_pairs={{0,16},{8,24},{16,0},{24,8},{1,17},{9,25},{17,1},{25,9},{2,18},{10... | collective-permute-start | bytes 786440 | tf_op jit(solution)/shard_map/ppermute | solution.py:517
  148.6 8.8 %collective-permute-start.27 = (bf16[16,16,128]{2,1,0:T(8,128)(2,1)S(1)}, bf16[16,16,128]{2,1,0:T(8,128)(2,1)S(1)}, u32[]{:S(2)}, u32[]{:S(2)}) collective-permute-start(bf16[16,16,128]{2,1,0:T(8,128)(2,1)S(1)} %constant_dynamic-slice_fusion.7), channel_id=1, source_target_pairs={{0,17},{1,16},{2,19},{3,18},{4,21},{5,20},{6,23},{7,22},{8,25},{9,... | collective-permute-start | bytes 196616 | tf_op jit(solution)/shard_map/ppermute | solution.py:520
  148.6 8.8 %collective-permute-start.28 = (bf16[16,16,128]{2,1,0:T(8,128)(2,1)S(1)}, bf16[16,16,128]{2,1,0:T(8,128)(2,1)S(1)}, u32[]{:S(2)}, u32[]{:S(2)}) collective-permute-start(bf16[16,16,128]{2,1,0:T(8,128)(2,1)S(1)} %constant_dynamic-slice_fusion.6), channel_id=1, source_target_pairs={{1,18},{2,17},{3,20},{4,19},{5,22},{6,21},{9,26},{10,25},{11,28},{... | collective-permute-start | bytes 196616 | tf_op jit(solution)/shard_map/ppermute | solution.py:520
  163.5 12.7 %collective-permute-start.29 = (bf16[128,16,128]{2,1,0:T(8,128)(2,1)S(1)}, bf16[128,16,128]{2,1,0:T(8,128)(2,1)S(1)}, u32[]{:S(2)}, u32[]{:S(2)}) collective-permute-start(bf16[128,16,128]{2,1,0:T(8,128)(2,1)S(1)} %get-tuple-element.315), channel_id=1, source_target_pairs={{0,1},{1,0},{2,3},{3,2},{4,5},{5,4},{6,7},{7,6},{8,9},{9,8},{10,11... | collective-permute-start | bytes 1572872 | tf_op jit(solution)/shard_map/ppermute | solution.py:514
  163.7 12.5 %collective-permute-start.30 = (bf16[128,16,128]{2,1,0:T(8,128)(2,1)S(1)}, bf16[128,16,128]{2,1,0:T(8,128)(2,1)S(1)}, u32[]{:S(2)}, u32[]{:S(2)}) collective-permute-start(bf16[128,16,128]{2,1,0:T(8,128)(2,1)S(1)} %get-tuple-element.316), channel_id=1, source_target_pairs={{1,2},{2,1},{3,4},{4,3},{5,6},{6,5},{9,10},{10,9},{11,12},{12,11},... | collective-permute-start | bytes 1572872 | tf_op jit(solution)/shard_map/ppermute | solution.py:514
  167.3 8.9 %collective-permute-start.31 = (bf16[16,64,128]{2,1,0:T(8,128)(2,1)S(1)}, bf16[16,64,128]{2,1,0:T(8,128)(2,1)S(1)}, u32[]{:S(2)}, u32[]{:S(2)}) collective-permute-start(bf16[16,64,128]{2,1,0:T(8,128)(2,1)S(1)} %constant_dynamic-slice_fusion.5), channel_id=1, source_target_pairs={{0,16},{8,24},{16,0},{24,8},{1,17},{9,25},{17,1},{25,9},{2,18},{10... | collective-permute-start | bytes 786440 | tf_op jit(solution)/shard_map/ppermute | solution.py:517
  168.6 7.6 %collective-permute-start.32 = (bf16[16,16,128]{2,1,0:T(8,128)(2,1)S(1)}, bf16[16,16,128]{2,1,0:T(8,128)(2,1)S(1)}, u32[]{:S(2)}, u32[]{:S(2)}) collective-permute-start(bf16[16,16,128]{2,1,0:T(8,128)(2,1)S(1)} %constant_dynamic-slice_fusion.4), channel_id=1, source_target_pairs={{0,17},{1,16},{2,19},{3,18},{4,21},{5,20},{6,23},{7,22},{8,25},{9,... | collective-permute-start | bytes 196616 | tf_op jit(solution)/shard_map/ppermute | solution.py:520
  168.6 7.6 %collective-permute-start.33 = (bf16[16,16,128]{2,1,0:T(8,128)(2,1)S(1)}, bf16[16,16,128]{2,1,0:T(8,128)(2,1)S(1)}, u32[]{:S(2)}, u32[]{:S(2)}) collective-permute-start(bf16[16,16,128]{2,1,0:T(8,128)(2,1)S(1)} %constant_dynamic-slice_fusion.3), channel_id=1, source_target_pairs={{1,18},{2,17},{3,20},{4,19},{5,22},{6,21},{9,26},{10,25},{11,28},{... | collective-permute-start | bytes 196616 | tf_op jit(solution)/shard_map/ppermute | solution.py:520
  181.4 14.0 %collective-permute-start.34 = (bf16[128,16,128]{2,1,0:T(8,128)(2,1)S(1)}, bf16[128,16,128]{2,1,0:T(8,128)(2,1)S(1)}, u32[]{:S(2)}, u32[]{:S(2)}) collective-permute-start(bf16[128,16,128]{2,1,0:T(8,128)(2,1)S(1)} %get-tuple-element.318), channel_id=1, source_target_pairs={{0,1},{1,0},{2,3},{3,2},{4,5},{5,4},{6,7},{7,6},{8,9},{9,8},{10,11... | collective-permute-start | bytes 1572872 | tf_op jit(solution)/shard_map/ppermute | solution.py:514
  181.5 13.9 %collective-permute-start.35 = (bf16[128,16,128]{2,1,0:T(8,128)(2,1)S(1)}, bf16[128,16,128]{2,1,0:T(8,128)(2,1)S(1)}, u32[]{:S(2)}, u32[]{:S(2)}) collective-permute-start(bf16[128,16,128]{2,1,0:T(8,128)(2,1)S(1)} %get-tuple-element.319), channel_id=1, source_target_pairs={{1,2},{2,1},{3,4},{4,3},{5,6},{6,5},{9,10},{10,9},{11,12},{12,11},... | collective-permute-start | bytes 1572872 | tf_op jit(solution)/shard_map/ppermute | solution.py:514
  186.8 8.6 %collective-permute-start.36 = (bf16[16,64,128]{2,1,0:T(8,128)(2,1)S(1)}, bf16[16,64,128]{2,1,0:T(8,128)(2,1)S(1)}, u32[]{:S(2)}, u32[]{:S(2)}) collective-permute-start(bf16[16,64,128]{2,1,0:T(8,128)(2,1)S(1)} %constant_dynamic-slice_fusion.2), channel_id=1, source_target_pairs={{0,16},{8,24},{16,0},{24,8},{1,17},{9,25},{17,1},{25,9},{2,18},{10... | collective-permute-start | bytes 786440 | tf_op jit(solution)/shard_map/ppermute | solution.py:517
  187.1 8.2 %collective-permute-start.37 = (bf16[16,16,128]{2,1,0:T(8,128)(2,1)S(1)}, bf16[16,16,128]{2,1,0:T(8,128)(2,1)S(1)}, u32[]{:S(2)}, u32[]{:S(2)}) collective-permute-start(bf16[16,16,128]{2,1,0:T(8,128)(2,1)S(1)} %constant_dynamic-slice_fusion.1), channel_id=1, source_target_pairs={{0,17},{1,16},{2,19},{3,18},{4,21},{5,20},{6,23},{7,22},{8,25},{9,... | collective-permute-start | bytes 196616 | tf_op jit(solution)/shard_map/ppermute | solution.py:520
  187.1 8.3 %collective-permute-start.38 = (bf16[16,16,128]{2,1,0:T(8,128)(2,1)S(1)}, bf16[16,16,128]{2,1,0:T(8,128)(2,1)S(1)}, u32[]{:S(2)}, u32[]{:S(2)}) collective-permute-start(bf16[16,16,128]{2,1,0:T(8,128)(2,1)S(1)} %constant_dynamic-slice_fusion), channel_id=1, source_target_pairs={{1,18},{2,17},{3,20},{4,19},{5,22},{6,21},{9,26},{10,25},{11,28},{... | collective-permute-start | bytes 196616 | tf_op jit(solution)/shard_map/ppermute | solution.py:520
  195.3 47.9 %collective-permute-start.18 = (f32[64,64,128]{2,1,0:T(8,128)}, f32[64,64,128]{2,1,0:T(8,128)}, u32[]{:S(2)}, u32[]{:S(2)}) collective-permute-start(f32[64,64,128]{2,1,0:T(8,128)} %constant_dynamic-slice_fusion.12), channel_id=1, source_target_pairs={{0,8},{8,0},{16,24},{24,16},{1,9},{9,1},{17,25},{25,17},{2,10},{10... | collective-permute-start | bytes 6291464 | tf_op jit(solution)/shard_map/ppermute | solution.py:634
  205.7 59.3 %collective-permute-start.39 = (f16[65,64,128]{2,1,0:T(8,128)(2,1)S(1)}, f16[65,64,128]{2,1,0:T(8,128)(2,1)S(1)}, u32[]{:S(2)}, u32[]{:S(2)}) collective-permute-start(f16[65,64,128]{2,1,0:T(8,128)(2,1)S(1)} %concatenate.11), channel_id=1, source_target_pairs={{0,8},{8,0},{16,24},{24,16},{1,9},{9,1},{17,25},{25,17},{2,10},{10... | collective-permute-start | bytes 3194888 | tf_op jit(solution)/shard_map/ppermute | solution.py:634
  (25 other events, 37.6 us)
